TPU v7x, 256 devices: a whole 4x4x8 slice. The times are simulated.
256 devices in a mesh: row: 16 (over x, y), col: 16 (over z, core).
Axes of the slice: x: 4, y: 4, z: 8, core: 2. Of those that a mesh axis runs over, the one named last changes fastest.
Arguments:
- tokens: bfloat16 [192, 192, 768], P('row', 'col'), may hold values from -6 to 6
- w_in: bfloat16 [768, 1536], replicated, may hold values from -0.21875 to 0.21875
- w_xproj: bfloat16 [768, 80], replicated, may hold values from -0.21875 to 0.21875
- w_dt: bfloat16 [48, 768], replicated, may hold values from -0.875 to 0.875
- dt_bias: float32 [768], replicated, may hold values from -7 to -2.3
- a_log: float32 [16, 768], replicated, may hold values from 0 to 2.77
- d_skip: float32 [768], replicated, may hold values from 0.5 to 1.5
- w_out: bfloat16 [768, 768], replicated, may hold values from -0.21875 to 0.21875
- out_grad: bfloat16 [192, 192, 768], P('row', 'col'), may hold values from -6 to 6
Outputs:
- layer_out: bfloat16 [192, 192, 768], P('row', 'col')
- token_grad: bfloat16 [192, 192, 768], P('row', 'col')
All inputs are finite; a program needn't handle non-finite values.
Results may differ from a plain program's by a relative error of at most 0.0064.
Values sent between devices are 32-bit elements; how exact they have to be, the bound alone decides.
No kernel may reach another device: no remote copies, remote signals or barrier semaphores. Data moves between devices by JAX's collectives and lax.ppermute only.
A program may use at most 192 MiB of HBM per device.

v0:
```python
import jax
import jax.numpy as jnp
from jax import lax
from jax.sharding import PartitionSpec as P


def prefix(part, axis, combine, identity, reverse):
    count = lax.axis_size(axis)
    place = lax.axis_index(axis)
    ahead = count - 1 - place if reverse else place
    gathered = jax.tree.map(lambda a: lax.all_gather(a, axis), part)
    state = jax.tree.map(lambda a, e: jnp.zeros_like(a) + jnp.asarray(e, a.dtype), part, identity)

    def one(hop, state):
        source = count - 1 - hop if reverse else hop
        return combine(
            state, jax.tree.map(lambda a: lax.dynamic_index_in_dim(a, source, 0, False), gathered)
        )

    return lax.fori_loop(0, ahead, one, state)


def compose(earlier, later):
    return (earlier[0] * later[0], later[0] * earlier[1] + later[1])


def silu_grad(values):
    sigmoid = jax.nn.sigmoid(values)
    return sigmoid * (1.0 + values * (1.0 - sigmoid))


def dot_transposed(left, right):
    return lax.dot_general(
        left, right, (((1,), (1,)), ((), ())), preferred_element_type=jnp.float32
    )


def combine_for():
    return compose


def carry_item(prod_edge, state_edge):
    return ((prod_edge, state_edge), (jnp.ones_like(prod_edge), jnp.zeros_like(state_edge)))


def forward_lines(rates, items, start, make_source, keep):

    def forward_advance(carry, item):
        product, state = carry
        decay = jnp.exp(item[0][:, None, :] * rates)
        state = decay * state + make_source(item)
        return ((product * decay, state), state if keep else None)

    return lax.scan(forward_advance, start, items)


def backward_lines(rates, items, start, make_source, keep):

    def backward_advance(carry, item):
        product, term = carry
        decay = jnp.exp(item[0][:, None, :] * rates)
        adjoint = make_source(item) + term
        return ((product * decay, decay * adjoint), adjoint if keep else None)

    return lax.scan(backward_advance, start, items, reverse=True)


def input_source(item):
    return item[0][:, None, :] * item[1][:, :, None] * item[2][:, None, :]


def passed_source(item):
    return item[1]


def grad_source(item):
    return item[1][:, :, None] * item[2][:, None, :]


def body(tokens, w_in, w_xproj, w_dt, dt_bias, a_log, d_skip, w_out, out_grad):
    tile_rows, tile_cols, model_width = tokens.shape
    cell_count = tile_rows * tile_cols
    low_rank, inner_width = w_dt.shape
    states = a_log.shape[0]
    flat_tokens = tokens.reshape(cell_count, model_width)
    projected = jnp.dot(flat_tokens, w_in, preferred_element_type=jnp.float32)
    x_pre = projected[:, :inner_width]
    z_pre = projected[:, inner_width:]
    x_act = jax.nn.silu(x_pre).astype(jnp.bfloat16)
    x_dbl = jnp.dot(x_act, w_xproj, preferred_element_type=jnp.float32)
    dt_low = x_dbl[:, :low_rank].astype(jnp.bfloat16)
    b_sel = x_dbl[:, low_rank : low_rank + states]
    c_sel = x_dbl[:, low_rank + states :]
    dt_pre = jnp.dot(dt_low, w_dt, preferred_element_type=jnp.float32) + dt_bias
    step_size = jax.nn.softplus(dt_pre)
    gated_grad = dot_transposed(out_grad.reshape(cell_count, model_width), w_out)
    z_silu = jax.nn.silu(z_pre)
    scan_grad = gated_grad * z_silu
    rates = -jnp.exp(a_log)
    combine = combine_for()
    step_grid = step_size.reshape(tile_rows, tile_cols, inner_width)
    x_grid = x_act.astype(jnp.float32).reshape(tile_rows, tile_cols, inner_width)
    grad_grid = scan_grad.reshape(tile_rows, tile_cols, inner_width)
    b_grid = b_sel.reshape(tile_rows, tile_cols, states)
    c_grid = c_sel.reshape(tile_rows, tile_cols, states)
    step_turned = jnp.swapaxes(step_grid, 0, 1)
    x_turned = jnp.swapaxes(x_grid, 0, 1)
    b_turned = jnp.swapaxes(b_grid, 0, 1)
    row_ones = jnp.ones((tile_rows, states, inner_width), jnp.float32)
    row_zeros = jnp.zeros((tile_rows, states, inner_width), jnp.float32)
    col_ones = jnp.ones((tile_cols, states, inner_width), jnp.float32)
    col_zeros = jnp.zeros((tile_cols, states, inner_width), jnp.float32)
    row_items = (step_turned, b_turned, x_turned)
    (row_total, row_end), unused = forward_lines(
        rates, row_items, (row_ones, row_zeros), input_source, False
    )
    row_item, row_empty = carry_item(row_total, row_end)
    row_in = prefix(row_item, "col", combine, row_empty, False)[1]
    unused, row_turned = forward_lines(rates, row_items, (row_ones, row_in), input_source, True)
    row_state = jnp.swapaxes(row_turned, 0, 1)
    (col_total, col_end), unused = forward_lines(
        rates, (step_grid, row_state), (col_ones, col_zeros), passed_source, False
    )
    col_item, col_empty = carry_item(col_total, col_end)
    col_in = prefix(col_item, "row", combine, col_empty, False)[1]
    unused, full_state = forward_lines(
        rates, (step_grid, row_state), (col_ones, col_in), passed_source, True
    )
    scan_out = jnp.sum(c_grid[:, :, :, None] * full_state, axis=2) + d_skip * x_grid
    csel_grad = jnp.sum(grad_grid[:, :, None, :] * full_state, axis=3)
    back_items = (step_grid, c_grid, grad_grid)
    (unused, col_term), unused = backward_lines(
        rates, back_items, (col_ones, col_zeros), grad_source, False
    )
    back_item, back_empty = carry_item(col_total, col_term)
    col_from = prefix(back_item, "row", combine, back_empty, True)[1]
    unused, col_adjoint = backward_lines(rates, back_items, (col_ones, col_from), grad_source, True)
    edge_items = (step_turned, jnp.swapaxes(col_adjoint, 0, 1))
    (unused, row_term), unused = backward_lines(
        rates, edge_items, (row_ones, row_zeros), passed_source, False
    )
    edge_item, edge_empty = carry_item(row_total, row_term)
    row_from = prefix(edge_item, "col", combine, edge_empty, True)[1]
    unused, adjoint_turned = backward_lines(
        rates, edge_items, (row_ones, row_from), passed_source, True
    )
    row_adjoint = jnp.swapaxes(adjoint_turned, 0, 1)
    decays = jnp.exp(step_grid[:, :, None, :] * rates)
    col_before = jnp.concatenate([col_in[None], full_state[:-1]], axis=0)
    row_before = jnp.concatenate([row_in[:, None], row_state[:, :-1]], axis=1)
    decay_grad = col_adjoint * col_before + row_adjoint * row_before
    step_grad = jnp.sum(
        decay_grad * decays * rates + row_adjoint * b_grid[:, :, :, None] * x_grid[:, :, None, :],
        axis=2,
    )
    bsel_grad = jnp.sum(row_adjoint * step_grid[:, :, None, :] * x_grid[:, :, None, :], axis=3)
    xscan_grad = (
        jnp.sum(row_adjoint * step_grid[:, :, None, :] * b_grid[:, :, :, None], axis=2)
        + grad_grid * d_skip
    )
    scan_flat = scan_out.reshape(cell_count, inner_width)
    gated_out = (scan_flat * z_silu).astype(jnp.bfloat16)
    layer_out = jnp.dot(gated_out, w_out, preferred_element_type=jnp.float32).astype(jnp.bfloat16)
    z_grad = gated_grad * scan_flat * silu_grad(z_pre)
    pre_grad = (step_grad.reshape(cell_count, inner_width) * jax.nn.sigmoid(dt_pre)).astype(
        jnp.bfloat16
    )
    low_grad = dot_transposed(pre_grad, w_dt)
    dbl_grad = jnp.concatenate(
        [low_grad, bsel_grad.reshape(cell_count, states), csel_grad.reshape(cell_count, states)],
        axis=1,
    ).astype(jnp.bfloat16)
    x_grad = xscan_grad.reshape(cell_count, inner_width) + dot_transposed(dbl_grad, w_xproj)
    proj_grad = jnp.concatenate([x_grad * silu_grad(x_pre), z_grad], axis=1).astype(jnp.bfloat16)
    token_grad = dot_transposed(proj_grad, w_in).astype(jnp.bfloat16)
    return (
        layer_out.reshape(tile_rows, tile_cols, model_width),
        token_grad.reshape(tile_rows, tile_cols, model_width),
    )


def solution(mesh):
    return jax.shard_map(
        body,
        mesh=mesh,
        in_specs=(P("row", "col", None), P(), P(), P(), P(), P(), P(), P(), P("row", "col", None)),
        out_specs=(P("row", "col", None), P("row", "col", None)),
        check_vma=False,
    )
```

profile of v0, /device:TPU:30, one launch (start us, length us, event | category | flops | bytes accessed | tf_op | source)
XLA Modules:
  0.0 648.6 jit_solution(18397907629401181457)
XLA Ops:
  10.9 2.8 fusion.16
  21.6 2.8 copy_bitcast_fusion.1
  24.4 36.0 %while.172 = (s32[]{:T(128)}, f32[12,16,768]{2,1,0:T(8,128)S(1)}, f32[12,16,768]{2,1,0:T(8,128)}, f32[12,12,768]{2,1,0:T(8,128)}, f32[16,768]{1,0:T(8,128)S(1)},...) while((s32[]{:T(128)}, f32[12,16,768]{2,1,0:T(8,128)S(1)}, ...), condition=%wide.region_1.2_spmd.clone, body=%wide.region_0.1_spmd.clone.sunk | while | flops 1179651 | bytes 2632055 | solution.py:54
  64.8 13.0 %while.174 = (s32[]{:T(128)}, f32[12,16,768]{2,1,0:T(8,128)S(1)}, f32[12,12,768]{2,1,0:T(8,128)}, f32[16,768]{1,0:T(8,128)S(1)}, f32[12,12,16]{2,1,0:T(8,128)S(1...) while((s32[]{:T(128)}, f32[12,16,768]{2,1,0:T(8,128)S(1)}, ...), condition=%wide.region_14.15_spmd.clone, body=%wide.region_13.14_spmd.clone.sunk | while | flops 737284 | bytes 1452419 | solution.py:65
  78.7 46.0 %all-gather.13.cloned.1.call-done = f32[192,16,768]{2,1,0:T(8,128)} async-done(((f32[12,16,768]{2,1,0:T(8,128)}), f32[192,16,768]{2,1,0:T(8,128)}) %all-gather.13.cloned.1.call-update) | async-done | bytes 9437200 | tf_op jit(solution)/shard_map/all_gather | solution.py:11
  124.8 61.2 %all-gather.15.cloned.1.call-done = f32[192,16,768]{2,1,0:T(8,128)} async-done(((f32[12,16,768]{2,1,0:T(8,128)}), f32[192,16,768]{2,1,0:T(8,128)}) %all-gather.15.cloned.1.call-update) | async-done | bytes 9437200 | tf_op jit(solution)/shard_map/all_gather | solution.py:11
  186.9 3.8 broadcast.28.clone2
  190.7 46.2 %while.165 = (s32[]{:T(128)}, f32[12,16,768]{2,1,0:T(8,128)}, f32[12,12,16,768]{3,2,0,1:T(8,128)}, f32[12,12,768]{2,1,0:T(8,128)}, f32[16,768]{1,0:T(8,128)S(1)}...) while((s32[]{:T(128)}, f32[12,16,768]{2,1,0:T(8,128)}, f32[12,12,16,768]{3,2,0,1:T(8,128)}, ...), condition=%wide.region_5.6_spmd, body=%wide.region_4.5_spmd.sunk | while | flops 737282 | bytes 2042217 | solution.py:54
  226.8 2.4 bitcast_dynamic-update-slice_fusion.8
  236.9 41.1 %while.173 = (s32[]{:T(128)}, f32[12,16,768]{2,1,0:T(8,128)}, f32[12,16,768]{2,1,0:T(8,128)}, f32[12,12,768]{2,1,0:T(8,128)}, f32[16,768]{1,0:T(8,128)S(1)}, /*i...) while((s32[]{:T(128)}, f32[12,16,768]{2,1,0:T(8,128)}, f32[12,16,768]{2,1,0:T(8,128)}, ...), condition=%wide.region_7.8_spmd.clone, body=%wide.region_6.7_spmd.clone.sunk | while | flops 884739 | bytes 3108975 | solution.py:54
  240.8 2.7 bitcast_add_fusion.18
  244.3 2.7 bitcast_add_fusion.18
  247.8 2.7 bitcast_add_fusion.18
  251.3 2.7 bitcast_add_fusion.18
  254.8 2.6 bitcast_add_fusion.18
  258.2 2.6 bitcast_add_fusion.18
  261.6 2.6 bitcast_add_fusion.18
  265.1 2.6 bitcast_add_fusion.18
  268.5 2.6 bitcast_add_fusion.18
  271.9 2.6 bitcast_add_fusion.18
  275.3 2.6 bitcast_add_fusion.18
  278.7 98.5 %all-gather.17.cloned.1.call-done = f32[192,16,768]{2,1,0:T(8,128)} async-done(((f32[12,16,768]{2,1,0:T(8,128)}), f32[192,16,768]{2,1,0:T(8,128)}) %all-gather.17.cloned.1.call-update) | async-done | bytes 9437200 | tf_op jit(solution)/shard_map/all_gather | solution.py:11
  377.2 3.8 broadcast.28.clone.3
  381.0 24.6 %while.169 = (s32[]{:T(128)}, f32[12,16,768]{2,1,0:T(8,128)S(1)}, f32[12,12,16,768]{3,2,1,0:T(8,128)}, f32[12,12,768]{2,1,0:T(8,128)}, f32[16,768]{1,0:T(8,128)S...) while((s32[]{:T(128)}, f32[12,16,768]{2,1,0:T(8,128)S(1)}, ...), condition=%wide.region_18.19_spmd, body=%wide.region_17.18_spmd.sunk | while | flops 884739 | bytes 2669693 | solution.py:65
  405.6 6.7 %copy.62 = f32[12,12,16,768]{3,2,0,1:T(8,128)} copy(f32[12,12,16,768]{3,2,1,0:T(8,128)} %get-tuple-element.896) | data formatting | bytes 14155776 | tf_op jit(solution)/shard_map/while | solution.py:65
  412.3 27.5 %while.175 = (s32[]{:T(128)}, f32[12,16,768]{2,1,0:T(8,128)S(1)}, f32[12,12,768]{2,1,0:T(8,128)}, f32[16,768]{1,0:T(8,128)S(1)}, f32[12,12,16,768]{3,2,1,0:T(8,128)}, /*index=5*/s32[]{:T(128)}, s32[]{:T(128)}, s32[]{:T(128)}) while((s32[]{:T(128)}, f32[12,16,768]{2,1,0:T(8,128)S(1)}, f32[12,12,768]{2,1,0:T(8,128)}, ...), condition=%wide.region_20.21_spmd.clone, body=%wide.region_19.20_spmd.clone.sunk | while | flops 589828 | bytes 1929339 | solution.py:65
  441.4 6.2 slice.34
  447.6 12.2 %all-gather.19.cloned.1.call-done = f32[192,16,768]{2,1,0:T(8,128)} async-done(((f32[12,16,768]{2,1,0:T(8,128)}), f32[192,16,768]{2,1,0:T(8,128)}) %all-gather.19.cloned.1.call-update) | async-done | bytes 9437200 | tf_op jit(solution)/shard_map/all_gather | solution.py:11
  459.9 23.8 %while.166 = (s32[]{:T(128)}, f32[12,16,768]{2,1,0:T(8,128)S(1)}, s32[]{:T(128)}, f32[16,12,16,768]{3,2,1,0:T(8,128)}, f32[16,12,16,768]{3,2,1,0:T(8,128)}, /*index=5*/s32[]{:T(128)}, s32[]{:T(128)}, s32[]{:T(128)}) while((s32[]{:T(128)}, f32[12,16,768]{2,1,0:T(8,128)S(1)}, s32[]{:T(128)}, f32[16,12,16,768]{3,2,1,0:T(8,128)}, ...), condition=%wide.region_9.10_spmd, body=%wide.region_8.9_spmd.sunk | while | flops 294917 | bytes 2359427 | solution.py:20
  484.5 3.8 broadcast.28.clone.2
  488.3 38.9 %while.167 = (s32[]{:T(128)}, f32[12,16,768]{2,1,0:T(8,128)}, f32[12,12,16,768]{3,2,1,0:T(8,128)}, f32[12,12,768]{2,1,0:T(8,128)}, f32[16,768]{1,0:T(8,128)S(1)}, /*index=5*/f32[12,12,16,768]{3,2,1,0:T(8,128)}, s32[]{:T(128)}) while((s32[]{:T(128)}, f32[12,16,768]{2,1,0:T(8,128)}, f32[12,12,16,768]{3,2,1,0:T(8,128)}, ...), condition=%wide.region_11.12_spmd, body=%wide.region_10.11_spmd.sunk | while | flops 442370 | bytes 2519133 | solution.py:54
  489.1 2.4 bitcast_dynamic-update-slice_fusion.9
  492.4 2.4 bitcast_dynamic-update-slice_fusion.9
  495.6 2.4 bitcast_dynamic-update-slice_fusion.9
  498.8 2.4 bitcast_dynamic-update-slice_fusion.9
  502.0 2.4 bitcast_dynamic-update-slice_fusion.9
  505.2 2.5 bitcast_dynamic-update-slice_fusion.9
  508.5 2.4 bitcast_dynamic-update-slice_fusion.9
  511.7 2.5 bitcast_dynamic-update-slice_fusion.9
  515.0 2.5 bitcast_dynamic-update-slice_fusion.9
  518.3 2.5 bitcast_dynamic-update-slice_fusion.9
  521.6 2.5 bitcast_dynamic-update-slice_fusion.9
  524.8 2.4 bitcast_dynamic-update-slice_fusion.9
  527.3 6.4 slice.27
  542.1 23.8 %while.170 = (s32[]{:T(128)}, f32[12,16,768]{2,1,0:T(8,128)S(1)}, s32[]{:T(128)}, f32[16,12,16,768]{3,2,1,0:T(8,128)}, f32[16,12,16,768]{3,2,1,0:T(8,128)}, /*index=5*/s32[]{:T(128)}, s32[]{:T(128)}, s32[]{:T(128)}, s32[]{:T(128)}) while((s32[]{:T(128)}, f32[12,16,768]{2,1,0:T(8,128)S(1)}, s32[]{:T(128)}, f32[16,12,16,768]{3,2,1,0:T(8,128)}, ...), condition=%wide.region_22.23_spmd, body=%wide.region_21.22_spmd.sunk | while | flops 294918 | bytes 2359447 | solution.py:20
  565.9 3.8 broadcast.28.clone
  569.7 50.3 %while.171 = (s32[]{:T(128)}, f32[12,16,768]{2,1,0:T(8,128)S(1)}, f32[12,12,16,768]{3,2,0,1:T(8,128)}, f32[12,12,768]{2,1,0:T(8,128)}, f32[16,768]{1,0:T(8,128)S...) while((s32[]{:T(128)}, f32[12,16,768]{2,1,0:T(8,128)S(1)}, f32[12,12,16,768]{3,2,0,1:T(8,128)}, ...), condition=%wide.region_24.25_spmd, body=%wide.region_23.24_spmd.sunk | while | flops 589827 | bytes 3698805 | solution.py:65
  620.0 12.6 %fusion.7 = (f32[12,12,768]{2,1,0:T(8,128)S(1)}, bf16[12,12,16]{2,1,0:T(8,128)(2,1)}, f32[12,12,768]{2,1,0:T(8,128)}) fusion(f32[12,12,16,768]{3,2,1,0:T(8,128)} %get-tuple-element.896, f32[11,12,16,768]{3,2,1,0:T(8,128)} %slice.27, f32[1,12,16,768]{3,2,1,0:T(8,128)} %bitcast.185, f32[12,11,16,768]{3,2,1,0:T(8,128)} %slice.34, ...), kind=kLoop, calls=%fused_computation.51 | loop fusion | flops 29857536 | bytes 30144000 | tf_op jit(solution)/shard_map/reduce_sum | solution.py:152
  (363 shorter events, 300.8 us)
Async XLA Ops:
  7.2 2.3 copy-start
  7.2 9.2 %copy-start.14 = (f32[768]{0:T(1024)S(1)}, f32[768]{0:T(1024)}, u32[]{:S(2)}) copy-start(f32[768]{0:T(1024)} %param.37) | copy-start | bytes 9220
  7.2 117.6 %all-gather.13.cloned.1.call-start = ((), (), s32[]{:S(2)}) async-start(), calls=%async_computation | async-start | bytes 10027008 | tf_op jit(solution)/shard_map/all_gather | solution.py:11
  10.0 0.9 copy-start.8
  60.4 0.8 copy-start.6
  60.4 3.6 copy-start.11
  61.2 124.8 %all-gather.15.cloned.1.call-start = ((), (), s32[]{:S(2)}) async-start(), calls=%async_computation.1 | async-start | bytes 10027008 | tf_op jit(solution)/shard_map/all_gather | solution.py:11
  62.0 216.7 %all-gather.21.cloned.1.call-start = ((), (), s32[]{:S(2)}) async-start(), calls=%async_computation.4 | async-start | bytes 10027008 | tf_op jit(solution)/shard_map/all_gather | solution.py:11
  77.8 0.9 copy-start.5
  78.7 298.5 %all-gather.17.cloned.1.call-start = ((), (), s32[]{:S(2)}) async-start(), calls=%async_computation.2 | async-start | bytes 10027008 | tf_op jit(solution)/shard_map/all_gather | solution.py:11
  186.0 4.7 copy-start.1
  278.0 181.8 %all-gather.19.cloned.1.call-start = ((), (), s32[]{:S(2)}) async-start(), calls=%async_computation.3 | async-start | bytes 10027008 | tf_op jit(solution)/shard_map/all_gather | solution.py:11
  278.6 263.5 %all-gather.23.cloned.1.call-start = ((), (), s32[]{:S(2)}) async-start(), calls=%async_computation.5 | async-start | bytes 10027008 | tf_op jit(solution)/shard_map/all_gather | solution.py:11
  405.6 6.7 %copy-start.3 = (f32[12,16,768]{2,1,0:T(8,128)S(1)}, f32[12,16,768]{2,1,0:T(8,128)}, u32[]{:S(2)}) copy-start(f32[12,16,768]{2,1,0:T(8,128)} %custom-call.5) | copy-start | bytes 1769476
  439.8 0.8 copy-start.4
  483.6 4.7 copy-start.2
  527.3 6.4 slice-start
  527.3 6.4 copy-start.7
  527.3 6.7 %slice-start.1 = ((s8[7077888]{0:T(1024)(128)(4,1)}), s8[2883584]{0:T(1024)(128)(4,1)S(1)}, s32[]{:S(2)}) async-start(s8[7077888]{0:T(1024)(128)(4,1)} %bitcast.181), calls=%async_computation.7 | async-start | bytes 5767168
  533.9 3.2 copy-start.12
  569.7 50.3 %copy-start.10 = (f32[12,12,16]{2,1,0:T(8,128)S(1)}, f32[12,12,16]{2,1,0:T(8,128)}, u32[]{:S(2)}) copy-start(f32[12,12,16]{2,1,0:T(8,128)} %copy.44) | copy-start | bytes 27652
  620.0 17.6 %copy-start.9 = (f32[144,768]{1,0:T(8,128)S(1)}, f32[144,768]{1,0:T(8,128)}, u32[]{:S(2)}) copy-start(f32[144,768]{1,0:T(8,128)} %get-tuple-element.1199) | copy-start | bytes 1327108
  620.0 17.6 %copy-start.13 = (f32[768]{0:T(1024)S(1)}, f32[768]{0:T(1024)}, u32[]{:S(2)}) copy-start(f32[768]{0:T(1024)} %param.39) | copy-start | bytes 9220
Sparse Core Ops, SparseCore 0:
  61.3 63.3 all-gather.12
  126.6 59.3 all-gather.14
  188.5 77.2 all-gather.20
  278.1 98.9 all-gather.16
  379.5 80.2 all-gather.18
  461.5 62.4 all-gather.22
where the time goes:
time: 659 us; the launch traced here: 649 us
  other arithmetic  254 us (39%)
  waiting for transfers between devices  219 us (33%)
  local copies, waits for them, and re-layouts  145 us (22%)
  between operations  14.5 us (2%)
  matrix products  13.2 us (2%)
    all_gather x6, waiting for transfers between devices, prefix(): gathered = jax.tree.map(lambda a: lax.all_gather(a, axis), part)  218 us
    dynamic_update_slice x48, other arithmetic, forward_lines(): return lax.scan(forward_advance, start, items)  92.2 us
    add x24, other arithmetic, forward_advance(): state = decay * state + make_source(item)  57.3 us
    add x30, other arithmetic, compose(): return (earlier[0] * later[0], later[0] * earlier[1] + later[1])  46.8 us
    mul x48, other arithmetic, backward_advance(): return ((product * decay, decay * adjoint), adjoint if keep else None)  39.7 us
    mul x48, local copies, waits for them, and re-layouts, input_source(): return item[0][:, None, :] * item[1][:, :, None] * item[2][:, None, :]  28.3 us
    mul x48, local copies, waits for them, and re-layouts, grad_source(): return item[1][:, :, None] * item[2][:, None, :]  20.1 us
    mul x24, local copies, waits for them, and re-layouts, backward_advance(): decay = jnp.exp(item[0][:, None, :] * rates)  19.3 us
  transfers between devices with their start and end apart: 6, of which 4 were waited for; matrix products, arithmetic and copies ran while one was open for 40% of the time, Pallas kernels for 0%

commit v1 on v0

v1 whole, which is shorter than its diff:
```python
import jax
import jax.numpy as jnp
from jax import lax
from jax.experimental import pallas as pl
from jax.experimental.pallas import tpu as pltpu
from jax.sharding import PartitionSpec as P

LOG2E = 1.4426950408889634
T = 12
PAD = 16
CELLS = T * PAD
N = 16
C = 768
HALF = 384
LANES = [slice(128 * k, 128 * k + 128) for k in range(C // 128)]
F32, BF16 = jnp.float32, jnp.bfloat16
VMEM_LIMIT = 60 * 1024 * 1024


def nt(left, right):
    return lax.dot_general(left, right, (((1,), (1,)), ((), ())), preferred_element_type=F32)


def blocks():
    for i in range(T):
        for h in range(2):
            q = 2 * i + h
            for half in range(2):
                yield i, h, half, 2 * (q // 3) + half, 8 * (q % 3)


def pack(out_ref, base, edge_ref):
    for i, h, half, chunk, row in blocks():
        out_ref[chunk, base + row : base + row + 8, :] = edge_ref[
            i, 8 * h : 8 * h + 8, HALF * half : HALF * half + HALF
        ]


def unpack(edge_ref, in_ref, base):
    for i, h, half, chunk, row in blocks():
        edge_ref[i, 8 * h : 8 * h + 8, HALF * half : HALF * half + HALF] = in_ref[
            chunk, base + row : base + row + 8, :
        ]


def pack_sums(out_ref, base, sum_rows):
    for chunk in range(16):
        group, half = chunk // 2, chunk % 2
        rows = [
            sum_rows[(3 * group + t) // 2][:, HALF * half : HALF * half + HALF] for t in range(3)
        ]
        out_ref[chunk, base : base + 8, :] = jnp.concatenate(
            rows + [jnp.zeros((5, HALF), F32)], axis=0
        )


def first_kernel(
    tokens_ref, w_in_ref, w_xproj_ref, w_dt_ref, dt_bias_ref, a_log_ref, w_out_ref, out_grad_ref,
    x_pre_ref, z_pre_ref, dt_pre_ref, gated_ref, step_ref, u_ref, x_ref, grad_ref, b_ref, c_ref,
    term_ref, sent_ref,
    tok_s, og_s, rates_s, end_s,
):
    tok_s[...] = jnp.zeros_like(tok_s)
    og_s[...] = jnp.zeros_like(og_s)
    for i in range(T):
        tok_s[i, 0:T, :] = tokens_ref[i]
        og_s[i, 0:T, :] = out_grad_ref[i]
    tok = tok_s[...].reshape(CELLS, C)
    x_pre = jnp.dot(tok, w_in_ref[:, 0:C], preferred_element_type=F32)
    z_pre = jnp.dot(tok, w_in_ref[:, C : 2 * C], preferred_element_type=F32)
    x_pre_ref[...] = x_pre
    z_pre_ref[...] = z_pre
    x_act = (x_pre * jax.nn.sigmoid(x_pre)).astype(BF16)
    x_dbl = jnp.dot(x_act, w_xproj_ref[...], preferred_element_type=F32)
    dt_low = x_dbl[:, 0:48].astype(BF16)
    x_dbl_t = lax.dot_general(
        w_xproj_ref[...], x_act, (((0,), (1,)), ((), ())), preferred_element_type=F32
    )
    for i in range(T):
        for j in range(T):
            cell = PAD * i + j
            b_ref[cell] = jnp.broadcast_to(x_dbl_t[48:64, cell : cell + 1], (N, 128))
            c_ref[cell] = jnp.broadcast_to(x_dbl_t[64:80, cell : cell + 1], (N, 128))
    dt_pre = jnp.dot(dt_low, w_dt_ref[...], preferred_element_type=F32) + dt_bias_ref[...]
    dt_pre_ref[...] = dt_pre
    step = jnp.maximum(dt_pre, 0.0) + jnp.log1p(jnp.exp(-jnp.abs(dt_pre)))
    step_ref[...] = step.reshape(T, PAD, C)
    x_full = x_act.astype(F32)
    x_ref[...] = x_full
    u_ref[...] = (step * x_full).reshape(T, PAD, C)
    gated = nt(og_s[...].reshape(CELLS, C), w_out_ref[...])
    gated_ref[...] = gated
    grad_ref[...] = (gated * (z_pre * jax.nn.sigmoid(z_pre))).reshape(T, PAD, C)
    rates_s[...] = -jnp.exp(a_log_ref[...]) * LOG2E
    term_ref[...] = jnp.zeros_like(term_ref)

    def one_row(back, carry):
        i = T - 1 - back
        row = [jnp.zeros((N, 128), F32) for _ in LANES]
        for j in range(T):
            b = b_ref[PAD * i + j]
            c = c_ref[PAD * i + j]
            for k, lanes in enumerate(LANES):
                decay = jnp.exp2(rates_s[:, lanes] * step_ref[i, j : j + 1, lanes])
                row[k] = decay * row[k] + b * u_ref[i, j : j + 1, lanes]
                term_ref[j, :, lanes] = decay * (
                    c * grad_ref[i, j : j + 1, lanes] + term_ref[j, :, lanes]
                )
        for k, lanes in enumerate(LANES):
            end_s[i, :, lanes] = row[k]
        return carry

    lax.fori_loop(0, T, one_row, 0)
    pack(sent_ref, 0, end_s)
    pack_sums(
        sent_ref, 24, [jnp.sum(step_ref[i, 0:T, :], axis=0, keepdims=True) for i in range(T)]
    )


def prefix_kernel(axis, spans, sum_base, got_ref, sums_ref, a_log_ref, out_ref):
    me = lax.axis_index(axis)
    group, half = me // 2, me % 2
    for t in range(3):
        state_rows = pl.multiple_of(8 * ((3 * group + t) % 2), 8)
        lanes = pl.multiple_of(HALF * half, 128)
        rate = -jnp.exp(a_log_ref[pl.ds(state_rows, 8), pl.ds(lanes, HALF)]) * LOG2E
        for base, reverse in spans:
            state = jnp.zeros((8, HALF), F32)
            rows = slice(base + 8 * t, base + 8 * t + 8)
            for hop in range(16):
                tile = 15 - hop if reverse else hop
                out_ref[tile, rows, :] = state
                decay = jnp.exp2(rate * sums_ref[tile, sum_base + t : sum_base + t + 1, :])
                state = decay * state + got_ref[tile, rows, :]


def forward_kernel(
    row_in_ref, a_log_ref, step_ref, u_ref, b_ref, term_ref, sent_ref, rates_s, row_s, col_s
):
    rates_s[...] = -jnp.exp(a_log_ref[...]) * LOG2E
    unpack(row_s, row_in_ref, 0)
    col_s[...] = jnp.zeros_like(col_s)

    def one_row(i, carry):
        row = [row_s[i, :, lanes] for lanes in LANES]
        for j in range(T):
            b = b_ref[PAD * i + j]
            for k, lanes in enumerate(LANES):
                decay = jnp.exp2(rates_s[:, lanes] * step_ref[i, j : j + 1, lanes])
                row[k] = decay * row[k] + b * u_ref[i, j : j + 1, lanes]
                col_s[j, :, lanes] = decay * col_s[j, :, lanes] + row[k]
        return carry

    lax.fori_loop(0, T, one_row, 0)
    pack(sent_ref, 0, col_s)
    pack(sent_ref, 24, term_ref)
    total = step_ref[0]
    for i in range(1, T):
        total = total + step_ref[i]
    pack_sums(sent_ref, 48, [total[j : j + 1, :] for j in range(T)])


def backward_kernel(
    col_got_ref, a_log_ref, step_ref, grad_ref, c_ref, sent_ref, rates_s, term_s, end_s
):
    rates_s[...] = -jnp.exp(a_log_ref[...]) * LOG2E
    unpack(term_s, col_got_ref, 24)

    def one_row(back, carry):
        i = T - 1 - back
        row = [jnp.zeros((N, 128), F32) for _ in LANES]
        for j in reversed(range(T)):
            c = c_ref[PAD * i + j]
            for k, lanes in enumerate(LANES):
                decay = jnp.exp2(rates_s[:, lanes] * step_ref[i, j : j + 1, lanes])
                adjoint = c * grad_ref[i, j : j + 1, lanes] + term_s[j, :, lanes]
                term_s[j, :, lanes] = decay * adjoint
                row[k] = decay * (adjoint + row[k])
        for k, lanes in enumerate(LANES):
            end_s[i, :, lanes] = row[k]
        return carry

    lax.fori_loop(0, T, one_row, 0)
    pack(sent_ref, 0, end_s)


def last_kernel(
    row_in_ref, col_got_ref, row_from_ref, x_pre_ref, z_pre_ref, dt_pre_ref, gated_ref, step_ref,
    u_ref, x_ref, grad_ref, b_ref, c_ref, a_log_ref, d_skip_ref, w_in_ref, w_xproj_ref, w_dt_ref,
    w_out_ref,
    layer_ref, token_ref,
    rates_s, row_s, col_s, full_keep, row_keep, scan_s, step_sum_s, x_sum_s, b_part, c_part, w_dt_s,
):
    neg_rates = -jnp.exp(a_log_ref[...])
    rates_s[...] = neg_rates * LOG2E
    unpack(row_s, row_in_ref, 0)
    unpack(col_s, col_got_ref, 0)
    for ref in (scan_s, step_sum_s, x_sum_s, b_part, c_part):
        ref[...] = jnp.zeros_like(ref)

    def down_row(i, carry):
        row = [row_s[i, :, lanes] for lanes in LANES]
        for j in range(T):
            cell = PAD * i + j
            b = b_ref[cell]
            c = c_ref[cell]
            part = jnp.zeros((N, 128), F32)
            for k, lanes in enumerate(LANES):
                decay = jnp.exp2(rates_s[:, lanes] * step_ref[i, j : j + 1, lanes])
                row_old = decay * row[k]
                row[k] = row_old + b * u_ref[i, j : j + 1, lanes]
                full_old = decay * col_s[j, :, lanes]
                full = full_old + row[k]
                col_s[j, :, lanes] = full
                row_keep[cell, :, lanes] = row_old
                full_keep[cell, :, lanes] = full_old
                scan_s[i, j : j + 1, lanes] = jnp.sum(c * full, axis=0, keepdims=True)
                part = part + full * grad_ref[i, j : j + 1, lanes]
            c_part[cell] = part
        return carry

    lax.fori_loop(0, T, down_row, 0)
    unpack(col_s, col_got_ref, 24)
    unpack(row_s, row_from_ref, 0)

    def up_row(back, carry):
        i = T - 1 - back
        row = [row_s[i, :, lanes] for lanes in LANES]
        for j in reversed(range(T)):
            cell = PAD * i + j
            b = b_ref[cell]
            c = c_ref[cell]
            part = jnp.zeros((N, 128), F32)
            for k, lanes in enumerate(LANES):
                decay = jnp.exp2(rates_s[:, lanes] * step_ref[i, j : j + 1, lanes])
                col_adjoint = c * grad_ref[i, j : j + 1, lanes] + col_s[j, :, lanes]
                col_s[j, :, lanes] = decay * col_adjoint
                row_adjoint = col_adjoint + row[k]
                row[k] = decay * row_adjoint
                decay_grad = (
                    col_adjoint * full_keep[cell, :, lanes] + row_adjoint * row_keep[cell, :, lanes]
                )
                step_sum_s[i, j : j + 1, lanes] = jnp.sum(
                    decay_grad * rates_s[:, lanes], axis=0, keepdims=True
                )
                x_sum_s[i, j : j + 1, lanes] = jnp.sum(row_adjoint * b, axis=0, keepdims=True)
                part = part + row_adjoint * u_ref[i, j : j + 1, lanes]
            b_part[cell] = part
        return carry

    lax.fori_loop(0, T, up_row, 0)

    x = x_ref[...]
    z_pre = z_pre_ref[...]
    x_pre = x_pre_ref[...]
    skip = d_skip_ref[...]
    step = step_ref[...].reshape(CELLS, C)
    grad = grad_ref[...].reshape(CELLS, C)
    scan_out = scan_s[...].reshape(CELLS, C) + skip * x
    z_sig = jax.nn.sigmoid(z_pre)
    gated_out = (scan_out * (z_pre * z_sig)).astype(BF16)
    layer = jnp.dot(gated_out, w_out_ref[...], preferred_element_type=F32).astype(BF16)
    for i in range(T):
        layer_ref[i] = layer[PAD * i : PAD * i + T, :]
    z_grad = (gated_ref[...] * scan_out * (z_sig * (1.0 + z_pre * (1.0 - z_sig)))).astype(BF16)
    x_sum = x_sum_s[...].reshape(CELLS, C)
    step_grad = step_sum_s[...].reshape(CELLS, C) * (1.0 / LOG2E) + x_sum * x
    pre_grad = (step_grad * jax.nn.sigmoid(dt_pre_ref[...])).astype(BF16)
    w_dt_s[...] = jnp.zeros_like(w_dt_s)
    w_dt_s[0:48, :] = w_dt_ref[...]
    low = nt(pre_grad, w_dt_s[...])
    rows = lax.broadcasted_iota(jnp.int32, (CELLS * N, 80), 0)
    cols = lax.broadcasted_iota(jnp.int32, (CELLS * N, 80), 1)
    state = rows % N
    b_sum = jnp.sum(b_part[...].reshape(CELLS * N, 128), axis=1, keepdims=True)
    c_sum = jnp.sum(c_part[...].reshape(CELLS * N, 128), axis=1, keepdims=True)
    placed = jnp.where(cols == state + 48, b_sum, jnp.where(cols == state + 64, c_sum, 0.0))
    owner = lax.broadcasted_iota(jnp.int32, (CELLS, CELLS * N), 1) // N
    cell = lax.broadcasted_iota(jnp.int32, (CELLS, CELLS * N), 0)
    choose = (owner == cell).astype(F32).astype(BF16)
    dbl = (low + jnp.dot(choose, placed.astype(BF16), preferred_element_type=F32)).astype(BF16)
    x_grad = x_sum * step + grad * skip + nt(dbl, w_xproj_ref[...])
    x_sig = jax.nn.sigmoid(x_pre)
    x_part = (x_grad * (x_sig * (1.0 + x_pre * (1.0 - x_sig)))).astype(BF16)
    token = (nt(x_part, w_in_ref[:, 0:C]) + nt(z_grad, w_in_ref[:, C : 2 * C])).astype(BF16)
    for i in range(T):
        token_ref[i] = token[PAD * i : PAD * i + T, :]


def call(kernel, out_shape, scratch, name):
    return pl.pallas_call(
        kernel,
        out_shape=out_shape,
        scratch_shapes=scratch,
        name=name,
        compiler_params=pltpu.CompilerParams(vmem_limit_bytes=VMEM_LIMIT),
    )


def f32(*shape):
    return jax.ShapeDtypeStruct(shape, F32)


def vmem(*shape):
    return pltpu.VMEM(shape, F32)


def prefix(axis, spans, sum_base, rows, got, sums, a_log):
    def kernel(got_ref, sums_ref, a_log_ref, out_ref):
        prefix_kernel(axis, spans, sum_base, got_ref, sums_ref, a_log_ref, out_ref)

    return call(kernel, f32(16, rows, HALF), (), "prefix_" + axis)(got, sums, a_log)


def swap(sent, axis):
    return lax.all_to_all(sent, axis, 0, 0, tiled=True)


def body(tokens, w_in, w_xproj, w_dt, dt_bias, a_log, d_skip, w_out, out_grad):
    edge = vmem(T, N, C)
    (x_pre, z_pre, dt_pre, gated, step, u, x, grad, b, c, term, row_sent) = call(
        first_kernel,
        (
            f32(CELLS, C), f32(CELLS, C), f32(CELLS, C), f32(CELLS, C),
            f32(T, PAD, C), f32(T, PAD, C), f32(CELLS, C), f32(T, PAD, C),
            f32(CELLS, N, 128), f32(CELLS, N, 128), f32(T, N, C), f32(16, 32, HALF),
        ),
        (pltpu.VMEM((T, PAD, C), BF16), pltpu.VMEM((T, PAD, C), BF16), vmem(N, C), edge),
        "first",
    )(tokens, w_in, w_xproj, w_dt, dt_bias.reshape(1, C), a_log, w_out, out_grad)
    row_got = swap(row_sent, "col")
    row_in = swap(prefix("col", ((0, False),), 24, 24, row_got, row_got, a_log), "col")
    col_sent = call(
        forward_kernel, f32(16, 56, HALF), (vmem(N, C), edge, edge), "forward"
    )(row_in, a_log, step, u, b, term)
    col_all = swap(col_sent, "row")
    col_got = swap(
        prefix("row", ((0, False), (24, True)), 48, 48, col_all, col_all, a_log), "row"
    )
    back_sent = call(
        backward_kernel, f32(16, 24, HALF), (vmem(N, C), edge, edge), "backward"
    )(col_got, a_log, step, grad, c)
    back_all = swap(back_sent, "col")
    row_from = swap(prefix("col", ((0, True),), 24, 24, back_all, row_got, a_log), "col")
    out = jax.ShapeDtypeStruct((T, T, C), BF16)
    wide = vmem(T, PAD, C)
    return call(
        last_kernel,
        (out, out),
        (
            vmem(N, C), edge, edge, vmem(CELLS, N, C), vmem(CELLS, N, C), wide, wide, wide,
            vmem(CELLS, N, 128), vmem(CELLS, N, 128), pltpu.VMEM((80, C), BF16),
        ),
        "last",
    )(
        row_in, col_got, row_from, x_pre, z_pre, dt_pre, gated, step, u, x, grad, b, c, a_log,
        d_skip.reshape(1, C), w_in, w_xproj, w_dt, w_out,
    )


def solution(mesh):
    return jax.shard_map(
        body,
        mesh=mesh,
        in_specs=(P("row", "col", None), P(), P(), P(), P(), P(), P(), P(), P("row", "col", None)),
        out_specs=(P("row", "col", None), P("row", "col", None)),
        check_vma=False,
    )
```

time: 659 us -> 200 us (0.30)
  the two profiles are of different devices: /device:TPU:30 before, /device:TPU:1 now
where the time goes in v1:
time: 200 us; the launch traced here: 199 us
  blocking collectives  129 us (64%)
  Pallas kernels  43.8 us (22%)
  waiting for transfers between devices  18.1 us (9%)
  local copies, waits for them, and re-layouts  4.4 us (2%)
  starting transfers between devices  3.49 us (2%)
    all_to_all x5, blocking collectives, swap(): return lax.all_to_all(sent, axis, 0, 0, tiled=True)  129 us
    all_to_all x1, waiting for transfers between devices, swap(): return lax.all_to_all(sent, axis, 0, 0, tiled=True)  18.1 us
    pallas_call x1, Pallas kernels, body(): call(last_kernel, (out, out), (vmem(N, C), edge, edge, vmem(CELLS, N, C),...  16.5 us
    pallas_call x1, Pallas kernels, body(): call(first_kernel, (f32(CELLS, C), f32(CELLS, C), f32(CELLS, C), f32(CELL...  9.92 us
    pallas_call x3, Pallas kernels, prefix(): call(kernel, f32(16, rows, HALF), (), 'prefix_' + axis)(got, sums, a_log)  7.55 us
    pallas_call x1, Pallas kernels, body(): call(forward_kernel, f32(16, 56, HALF), (vmem(N, C), edge, edge), 'forward')  5.1 us
    pallas_call x1, Pallas kernels, body(): call(backward_kernel, f32(16, 24, HALF), (vmem(N, C), edge, edge), 'backw...  4.67 us
  transfers between devices with their start and end apart: 1, of which 1 were waited for; matrix products, arithmetic and copies ran while one was open for 0% of the time, Pallas kernels for 0%

profile of v1, /device:TPU:1, one launch (start us, length us, event | category | flops | bytes accessed | tf_op | source)
XLA Modules:
  0.0 199.0 jit_solution(12117221293468419958)
XLA Ops:
  0.6 1.7 copy.11.w_xproj_ref
  2.3 1.3 reshape.10.dt_bias_ref
  3.6 9.9 %first.1 = (f32[192,768]{1,0:T(8,128)}, f32[192,768]{1,0:T(8,128)}, f32[192,768]{1,0:T(8,128)}, f32[192,768]{1,0:T(8,128)}, f32[12,16,768]{2,1,0:T(8,128)}, /*in...) custom-call(bf16[12,12,768]{2,1,0:T(8,128)(2,1)} %tokens_ref.1, ...), custom_call_target="tpu_custom_call" | custom-call | tf_op jit(solution)/shard_map/first/pallas_call | solution.py:321
  13.5 32.9 %all_to_all.30.got_ref.sums_ref = f32[16,32,384]{2,1,0:T(8,128)} all-to-all(f32[16,32,384]{2,1,0:T(8,128)} %get-tuple-element.14), channel_id=1, replica_groups=mesh['row'=16,'col'=16] {'col'}, dimensions={0} | all-to-all | bytes 1572864 | tf_op jit(solution)/shard_map/all_to_all | solution.py:316
  46.4 2.3 %prefix_col.2 = f32[16,24,384]{2,1,0:T(8,128)} custom-call(f32[16,32,384]{2,1,0:T(8,128)} %all_to_all.30.got_ref.sums_ref, f32[16,32,384]{2,1,0:T(8,128)} %all_to_all.30.got_ref.sums_ref, f32[16,768]{1,0:T(8,128)} %a_log_ref.13), custom_call_target="tpu_custom_call" | custom-call | tf_op jit(solution)/shard_map/prefix_col/pallas_call | solution.py:312
  48.8 22.6 %all_to_all.31.row_in_ref = f32[16,24,384]{2,1,0:T(8,128)} all-to-all(f32[16,24,384]{2,1,0:T(8,128)} %prefix_col.2), channel_id=1, replica_groups=mesh['row'=16,'col'=16] {'col'}, dimensions={0} | all-to-all | bytes 1179648 | tf_op jit(solution)/shard_map/all_to_all | solution.py:316
  71.4 5.1 %forward.1 = f32[16,56,384]{2,1,0:T(8,128)} custom-call(f32[16,24,384]{2,1,0:T(8,128)} %all_to_all.31.row_in_ref, f32[16,768]{1,0:T(8,128)} %a_log_ref.13, f32[12,16,768]{2,1,0:T(8,128)} %get-tuple-element.15.step_ref, f32[12,16,768]{2,1,0:T(8,128)} %get-tuple-element.16.u_ref, f32[192,16,128]{2,1,0:T(8,128)} %get-tuple-element.17.b_ref, ...), custom_call_target="tpu_custom_call" | custom-call | tf_op jit(solution)/shard_map/forward/pallas_call | solution.py:333
  76.5 26.2 %all_to_all.32.got_ref.sums_ref = f32[16,56,384]{2,1,0:T(8,128)} all-to-all(f32[16,56,384]{2,1,0:T(8,128)} %forward.1), channel_id=1, replica_groups=mesh['row'=16,'col'=16] {'row'}, dimensions={0} | all-to-all | bytes 2752512 | tf_op jit(solution)/shard_map/all_to_all | solution.py:316
  102.7 3.0 %prefix_row.1 = f32[16,48,384]{2,1,0:T(8,128)} custom-call(f32[16,56,384]{2,1,0:T(8,128)} %all_to_all.32.got_ref.sums_ref, f32[16,56,384]{2,1,0:T(8,128)} %all_to_all.32.got_ref.sums_ref, f32[16,768]{1,0:T(8,128)} %a_log_ref.13), custom_call_target="tpu_custom_call" | custom-call | tf_op jit(solution)/shard_map/prefix_row/pallas_call | solution.py:312
  105.7 20.5 %all_to_all.33.col_got_ref = f32[16,48,384]{2,1,0:T(8,128)} all-to-all(f32[16,48,384]{2,1,0:T(8,128)} %prefix_row.1), channel_id=1, replica_groups=mesh['row'=16,'col'=16] {'row'}, dimensions={0} | all-to-all | bytes 2359296 | tf_op jit(solution)/shard_map/all_to_all | solution.py:316
  126.2 4.7 %backward.1 = f32[16,24,384]{2,1,0:T(8,128)} custom-call(f32[16,48,384]{2,1,0:T(8,128)} %all_to_all.33.col_got_ref, f32[16,768]{1,0:T(8,128)} %a_log_ref.13, f32[12,16,768]{2,1,0:T(8,128)} %get-tuple-element.15.step_ref, f32[12,16,768]{2,1,0:T(8,128)} %get-tuple-element.19.grad_ref, f32[192,16,128]{2,1,0:T(8,128)} %get-tuple-element.20.c_ref), custom_call_target="tpu_custom_call" | custom-call | tf_op jit(solution)/shard_map/backward/pallas_call | solution.py:340
  130.9 26.3 %all_to_all.34.got_ref = f32[16,24,384]{2,1,0:T(8,128)} all-to-all(f32[16,24,384]{2,1,0:T(8,128)} %backward.1), channel_id=1, replica_groups=mesh['row'=16,'col'=16] {'col'}, dimensions={0} | all-to-all | bytes 1179648 | tf_op jit(solution)/shard_map/all_to_all | solution.py:316
  157.2 0.0 copy-start.1
  157.2 2.2 %prefix_col.3 = f32[16,24,384]{2,1,0:T(8,128)} custom-call(f32[16,24,384]{2,1,0:T(8,128)} %all_to_all.34.got_ref, f32[16,32,384]{2,1,0:T(8,128)} %all_to_all.30.got_ref.sums_ref, f32[16,768]{1,0:T(8,128)} %a_log_ref.13), custom_call_target="tpu_custom_call" | custom-call | tf_op jit(solution)/shard_map/prefix_col/pallas_call | solution.py:312
  159.4 3.5 %all-to-all-start.5 = ((f32[16,24,384]{2,1,0:T(8,128)}), f32[16,24,384]{2,1,0:T(8,128)S(1)}, u32[]{:S(2)}, u32[]{:S(2)}) async-start(f32[16,24,384]{2,1,0:T(8,128)} %prefix_col.3), calls=%async_computation.5 | async-start | bytes 1179648 | tf_op jit(solution)/shard_map/all_to_all | solution.py:316
  162.9 0.0 copy-done.1
  162.9 0.6 reshape.11.d_skip_ref
  163.5 18.1 %all-to-all-done.5.row_from_ref = f32[16,24,384]{2,1,0:T(8,128)S(1)} async-done(((f32[16,24,384]{2,1,0:T(8,128)}), f32[16,24,384]{2,1,0:T(8,128)S(1)}, u32[]{:S(2)}, u32[]{:S(2)}) %all-to-all-start.5) | async-done | bytes 589856 | tf_op jit(solution)/shard_map/all_to_all | solution.py:316
  181.6 0.0 copy-start
  181.6 0.8 copy-done
  182.5 16.5 %last.1 = (bf16[12,12,768]{2,1,0:T(8,128)(2,1)}, bf16[12,12,768]{2,1,0:T(8,128)(2,1)}) custom-call(f32[16,24,384]{2,1,0:T(8,128)} %all_to_all.31.row_in_ref, f32[16,48,384]{2,1,0:T(8,128)} %all_to_all.33.col_got_ref, f32[16,24,384]{2,1,0:T(8,128)} %copy-done, f32[192,768]{1,0:T(8,128)} %get-tuple-element.21.x_pre_ref, ...), custom_call_target="tpu_custom_call" | custom-call | tf_op jit(solution)/shard_map/last/pallas_call | solution.py:347
Async XLA Ops:
  157.2 5.7 %copy-start.1 = (f32[768]{0:T(1024)S(1)}, f32[768]{0:T(1024)}, u32[]{:S(2)}) copy-start(f32[768]{0:T(1024)} %param.15) | copy-start | bytes 9220
  159.4 22.2 %all-to-all-start.5 = ((f32[16,24,384]{2,1,0:T(8,128)}), f32[16,24,384]{2,1,0:T(8,128)S(1)}, u32[]{:S(2)}, u32[]{:S(2)}) async-start(f32[16,24,384]{2,1,0:T(8,128)} %prefix_col.3), calls=%async_computation.5 | async-start | bytes 1179648 | tf_op jit(solution)/shard_map/all_to_all | solution.py:316
  181.6 0.8 copy-start

commit v2 on v1

--- a/solution.py
+++ b/solution.py
@@ -14,7 +14,6 @@
 HALF = 384
 LANES = [slice(128 * k, 128 * k + 128) for k in range(C // 128)]
 F32, BF16 = jnp.float32, jnp.bfloat16
-VMEM_LIMIT = 60 * 1024 * 1024
 
 
 def nt(left, right):
@@ -54,33 +53,52 @@
         )
 
 
+def fetch(pairs, sems):
+    copies = [pltpu.make_async_copy(src, dst, sems.at[k]) for k, (src, dst) in enumerate(pairs)]
+    for copy in copies:
+        copy.start()
+    return copies
+
+
 def first_kernel(
-    tokens_ref, w_in_ref, w_xproj_ref, w_dt_ref, dt_bias_ref, a_log_ref, w_out_ref, out_grad_ref,
+    tokens_hbm, w_in_hbm, w_xproj_hbm, w_dt_hbm, a_log_hbm, w_out_hbm, out_grad_hbm, dt_bias_ref,
     x_pre_ref, z_pre_ref, dt_pre_ref, gated_ref, step_ref, u_ref, x_ref, grad_ref, b_ref, c_ref,
-    term_ref, sent_ref,
-    tok_s, og_s, rates_s, end_s,
+    term_ref, rates_ref, sent_ref,
+    tokens_ref, w_x_ref, w_z_ref, w_xproj_ref, w_dt_ref, a_log_ref, w_out_ref, out_grad_ref,
+    tok_s, og_s, end_s, sems,
 ):
+    copies = fetch(
+        (
+            (tokens_hbm, tokens_ref),
+            (w_in_hbm.at[:, 0:C], w_x_ref),
+            (w_xproj_hbm, w_xproj_ref),
+            (w_dt_hbm, w_dt_ref),
+            (a_log_hbm, a_log_ref),
+            (w_in_hbm.at[:, C : 2 * C], w_z_ref),
+            (out_grad_hbm, out_grad_ref),
+            (w_out_hbm, w_out_ref),
+        ),
+        sems,
+    )
     tok_s[...] = jnp.zeros_like(tok_s)
     og_s[...] = jnp.zeros_like(og_s)
+    copies[0].wait()
     for i in range(T):
         tok_s[i, 0:T, :] = tokens_ref[i]
-        og_s[i, 0:T, :] = out_grad_ref[i]
     tok = tok_s[...].reshape(CELLS, C)
-    x_pre = jnp.dot(tok, w_in_ref[:, 0:C], preferred_element_type=F32)
-    z_pre = jnp.dot(tok, w_in_ref[:, C : 2 * C], preferred_element_type=F32)
+    copies[1].wait()
+    x_pre = jnp.dot(tok, w_x_ref[...], preferred_element_type=F32)
     x_pre_ref[...] = x_pre
-    z_pre_ref[...] = z_pre
     x_act = (x_pre * jax.nn.sigmoid(x_pre)).astype(BF16)
-    x_dbl = jnp.dot(x_act, w_xproj_ref[...], preferred_element_type=F32)
-    dt_low = x_dbl[:, 0:48].astype(BF16)
-    x_dbl_t = lax.dot_general(
-        w_xproj_ref[...], x_act, (((0,), (1,)), ((), ())), preferred_element_type=F32
-    )
+    copies[2].wait()
+    dt_low = nt(x_act, w_xproj_ref[...])[:, 0:48].astype(BF16)
+    x_dbl_t = nt(w_xproj_ref[...], x_act)
     for i in range(T):
         for j in range(T):
             cell = PAD * i + j
             b_ref[cell] = jnp.broadcast_to(x_dbl_t[48:64, cell : cell + 1], (N, 128))
             c_ref[cell] = jnp.broadcast_to(x_dbl_t[64:80, cell : cell + 1], (N, 128))
+    copies[3].wait()
     dt_pre = jnp.dot(dt_low, w_dt_ref[...], preferred_element_type=F32) + dt_bias_ref[...]
     dt_pre_ref[...] = dt_pre
     step = jnp.maximum(dt_pre, 0.0) + jnp.log1p(jnp.exp(-jnp.abs(dt_pre)))
@@ -88,10 +106,18 @@
     x_full = x_act.astype(F32)
     x_ref[...] = x_full
     u_ref[...] = (step * x_full).reshape(T, PAD, C)
+    copies[4].wait()
+    rates_ref[...] = -jnp.exp(a_log_ref[...]) * LOG2E
+    copies[5].wait()
+    z_pre = jnp.dot(tok, w_z_ref[...], preferred_element_type=F32)
+    z_pre_ref[...] = z_pre
+    copies[6].wait()
+    for i in range(T):
+        og_s[i, 0:T, :] = out_grad_ref[i]
+    copies[7].wait()
     gated = nt(og_s[...].reshape(CELLS, C), w_out_ref[...])
     gated_ref[...] = gated
     grad_ref[...] = (gated * (z_pre * jax.nn.sigmoid(z_pre))).reshape(T, PAD, C)
-    rates_s[...] = -jnp.exp(a_log_ref[...]) * LOG2E
     term_ref[...] = jnp.zeros_like(term_ref)
 
     def one_row(back, carry):
@@ -101,7 +127,7 @@
             b = b_ref[PAD * i + j]
             c = c_ref[PAD * i + j]
             for k, lanes in enumerate(LANES):
-                decay = jnp.exp2(rates_s[:, lanes] * step_ref[i, j : j + 1, lanes])
+                decay = jnp.exp2(rates_ref[:, lanes] * step_ref[i, j : j + 1, lanes])
                 row[k] = decay * row[k] + b * u_ref[i, j : j + 1, lanes]
                 term_ref[j, :, lanes] = decay * (
                     c * grad_ref[i, j : j + 1, lanes] + term_ref[j, :, lanes]
@@ -117,13 +143,13 @@
     )
 
 
-def prefix_kernel(axis, spans, sum_base, got_ref, sums_ref, a_log_ref, out_ref):
+def prefix_kernel(axis, spans, sum_base, got_ref, sums_ref, rates_ref, out_ref):
     me = lax.axis_index(axis)
     group, half = me // 2, me % 2
     for t in range(3):
         state_rows = pl.multiple_of(8 * ((3 * group + t) % 2), 8)
         lanes = pl.multiple_of(HALF * half, 128)
-        rate = -jnp.exp(a_log_ref[pl.ds(state_rows, 8), pl.ds(lanes, HALF)]) * LOG2E
+        rate = rates_ref[pl.ds(state_rows, 8), pl.ds(lanes, HALF)]
         for base, reverse in spans:
             state = jnp.zeros((8, HALF), F32)
             rows = slice(base + 8 * t, base + 8 * t + 8)
@@ -135,9 +161,8 @@
 
 
 def forward_kernel(
-    row_in_ref, a_log_ref, step_ref, u_ref, b_ref, term_ref, sent_ref, rates_s, row_s, col_s
+    row_in_ref, rates_s, step_ref, u_ref, b_ref, term_ref, sent_ref, row_s, col_s
 ):
-    rates_s[...] = -jnp.exp(a_log_ref[...]) * LOG2E
     unpack(row_s, row_in_ref, 0)
     col_s[...] = jnp.zeros_like(col_s)
 
@@ -161,9 +186,8 @@
 
 
 def backward_kernel(
-    col_got_ref, a_log_ref, step_ref, grad_ref, c_ref, sent_ref, rates_s, term_s, end_s
+    col_got_ref, rates_s, step_ref, grad_ref, c_ref, sent_ref, term_s, end_s
 ):
-    rates_s[...] = -jnp.exp(a_log_ref[...]) * LOG2E
     unpack(term_s, col_got_ref, 24)
 
     def one_row(back, carry):
@@ -186,13 +210,21 @@
 
 def last_kernel(
     row_in_ref, col_got_ref, row_from_ref, x_pre_ref, z_pre_ref, dt_pre_ref, gated_ref, step_ref,
-    u_ref, x_ref, grad_ref, b_ref, c_ref, a_log_ref, d_skip_ref, w_in_ref, w_xproj_ref, w_dt_ref,
-    w_out_ref,
-    layer_ref, token_ref,
-    rates_s, row_s, col_s, full_keep, row_keep, scan_s, step_sum_s, x_sum_s, b_part, c_part, w_dt_s,
+    u_ref, x_ref, grad_ref, b_ref, c_ref, rates_s, d_skip_ref, w_in_hbm, w_xproj_hbm, w_dt_hbm,
+    w_out_hbm,
+    layer_hbm, token_hbm,
+    w_in_ref, w_xproj_ref, w_dt_ref, w_out_ref, layer_ref, token_ref,
+    row_s, col_s, full_keep, row_keep, scan_s, step_sum_s, x_sum_s, b_part, c_part, w_dt_s, sems,
 ):
-    neg_rates = -jnp.exp(a_log_ref[...])
-    rates_s[...] = neg_rates * LOG2E
+    copies = fetch(
+        (
+            (w_out_hbm, w_out_ref),
+            (w_dt_hbm, w_dt_ref),
+            (w_xproj_hbm, w_xproj_ref),
+            (w_in_hbm, w_in_ref),
+        ),
+        sems,
+    )
     unpack(row_s, row_in_ref, 0)
     unpack(col_s, col_got_ref, 0)
     for ref in (scan_s, step_sum_s, x_sum_s, b_part, c_part):
@@ -212,14 +244,29 @@
                 full_old = decay * col_s[j, :, lanes]
                 full = full_old + row[k]
                 col_s[j, :, lanes] = full
-                row_keep[cell, :, lanes] = row_old
-                full_keep[cell, :, lanes] = full_old
+                row_keep[T * i + j, :, lanes] = row_old
+                full_keep[T * i + j, :, lanes] = full_old
                 scan_s[i, j : j + 1, lanes] = jnp.sum(c * full, axis=0, keepdims=True)
                 part = part + full * grad_ref[i, j : j + 1, lanes]
             c_part[cell] = part
         return carry
 
     lax.fori_loop(0, T, down_row, 0)
+    x = x_ref[...]
+    z_pre = z_pre_ref[...]
+    skip = d_skip_ref[...]
+    scan_out = scan_s[...].reshape(CELLS, C) + skip * x
+    z_sig = jax.nn.sigmoid(z_pre)
+    gated_out = (scan_out * (z_pre * z_sig)).astype(BF16)
+    copies[0].wait()
+    layer = jnp.dot(gated_out, w_out_ref[...], preferred_element_type=F32).astype(BF16)
+    for i in range(T):
+        layer_ref[i] = layer[PAD * i : PAD * i + T, :]
+    layer_copy = pltpu.make_async_copy(layer_ref, layer_hbm, sems.at[4])
+    layer_copy.start()
+    scan_s[...] = (gated_ref[...] * scan_out * (z_sig * (1.0 + z_pre * (1.0 - z_sig)))).reshape(
+        T, PAD, C
+    )
     unpack(col_s, col_got_ref, 24)
     unpack(row_s, row_from_ref, 0)
 
@@ -238,7 +285,7 @@
                 row_adjoint = col_adjoint + row[k]
                 row[k] = decay * row_adjoint
                 decay_grad = (
-                    col_adjoint * full_keep[cell, :, lanes] + row_adjoint * row_keep[cell, :, lanes]
+                    col_adjoint * full_keep[T * i + j, :, lanes] + row_adjoint * row_keep[T * i + j, :, lanes]
                 )
                 step_sum_s[i, j : j + 1, lanes] = jnp.sum(
                     decay_grad * rates_s[:, lanes], axis=0, keepdims=True
@@ -251,21 +298,13 @@
     lax.fori_loop(0, T, up_row, 0)
 
     x = x_ref[...]
-    z_pre = z_pre_ref[...]
     x_pre = x_pre_ref[...]
-    skip = d_skip_ref[...]
     step = step_ref[...].reshape(CELLS, C)
     grad = grad_ref[...].reshape(CELLS, C)
-    scan_out = scan_s[...].reshape(CELLS, C) + skip * x
-    z_sig = jax.nn.sigmoid(z_pre)
-    gated_out = (scan_out * (z_pre * z_sig)).astype(BF16)
-    layer = jnp.dot(gated_out, w_out_ref[...], preferred_element_type=F32).astype(BF16)
-    for i in range(T):
-        layer_ref[i] = layer[PAD * i : PAD * i + T, :]
-    z_grad = (gated_ref[...] * scan_out * (z_sig * (1.0 + z_pre * (1.0 - z_sig)))).astype(BF16)
     x_sum = x_sum_s[...].reshape(CELLS, C)
     step_grad = step_sum_s[...].reshape(CELLS, C) * (1.0 / LOG2E) + x_sum * x
     pre_grad = (step_grad * jax.nn.sigmoid(dt_pre_ref[...])).astype(BF16)
+    copies[1].wait()
     w_dt_s[...] = jnp.zeros_like(w_dt_s)
     w_dt_s[0:48, :] = w_dt_ref[...]
     low = nt(pre_grad, w_dt_s[...])
@@ -279,22 +318,40 @@
     cell = lax.broadcasted_iota(jnp.int32, (CELLS, CELLS * N), 0)
     choose = (owner == cell).astype(F32).astype(BF16)
     dbl = (low + jnp.dot(choose, placed.astype(BF16), preferred_element_type=F32)).astype(BF16)
-    x_grad = x_sum * step + grad * skip + nt(dbl, w_xproj_ref[...])
+    copies[2].wait()
+    x_grad = (
+        x_sum * step
+        + grad * d_skip_ref[...]
+        + jnp.dot(dbl, w_xproj_ref[...], preferred_element_type=F32)
+    )
     x_sig = jax.nn.sigmoid(x_pre)
     x_part = (x_grad * (x_sig * (1.0 + x_pre * (1.0 - x_sig)))).astype(BF16)
-    token = (nt(x_part, w_in_ref[:, 0:C]) + nt(z_grad, w_in_ref[:, C : 2 * C])).astype(BF16)
+    z_part = scan_s[...].reshape(CELLS, C).astype(BF16)
+    copies[3].wait()
+    token = (nt(x_part, w_in_ref[:, 0:C]) + nt(z_part, w_in_ref[:, C : 2 * C])).astype(BF16)
     for i in range(T):
         token_ref[i] = token[PAD * i : PAD * i + T, :]
-
-
-def call(kernel, out_shape, scratch, name):
+    token_copy = pltpu.make_async_copy(token_ref, token_hbm, sems.at[5])
+    token_copy.start()
+    layer_copy.wait()
+    token_copy.wait()
+
+
+IN_VMEM = pl.BlockSpec(memory_space=pltpu.VMEM)
+IN_HBM = pl.BlockSpec(memory_space=pltpu.HBM)
+
+
+def call(kernel, out_shape, scratch, name, limit, *args, fetched=(), out_spec=IN_VMEM):
+    many = isinstance(out_shape, tuple)
     return pl.pallas_call(
         kernel,
         out_shape=out_shape,
+        in_specs=[IN_HBM if k in fetched else IN_VMEM for k in range(len(args))],
+        out_specs=tuple(out_spec for _ in out_shape) if many else out_spec,
         scratch_shapes=scratch,
         name=name,
-        compiler_params=pltpu.CompilerParams(vmem_limit_bytes=VMEM_LIMIT),
-    )
+        compiler_params=pltpu.CompilerParams(vmem_limit_bytes=limit * 1024 * 1024),
+    )(*args)
 
 
 def f32(*shape):
@@ -305,11 +362,11 @@
     return pltpu.VMEM(shape, F32)
 
 
-def prefix(axis, spans, sum_base, rows, got, sums, a_log):
-    def kernel(got_ref, sums_ref, a_log_ref, out_ref):
-        prefix_kernel(axis, spans, sum_base, got_ref, sums_ref, a_log_ref, out_ref)
-
-    return call(kernel, f32(16, rows, HALF), (), "prefix_" + axis)(got, sums, a_log)
+def prefix(axis, spans, sum_base, rows, got, sums, rates):
+    def kernel(got_ref, sums_ref, rates_ref, out_ref):
+        prefix_kernel(axis, spans, sum_base, got_ref, sums_ref, rates_ref, out_ref)
+
+    return call(kernel, f32(16, rows, HALF), (), "prefix_" + axis, 4, got, sums, rates)
 
 
 def swap(sent, axis):
@@ -317,44 +374,56 @@
 
 
 def body(tokens, w_in, w_xproj, w_dt, dt_bias, a_log, d_skip, w_out, out_grad):
-    edge = vmem(T, N, C)
-    (x_pre, z_pre, dt_pre, gated, step, u, x, grad, b, c, term, row_sent) = call(
+    edge, wide = vmem(T, N, C), vmem(T, PAD, C)
+    flat, grid, spread = f32(CELLS, C), f32(T, PAD, C), f32(CELLS, N, 128)
+    kept = vmem(T * T, N, C)
+    padded, cells = pltpu.VMEM((T, PAD, C), BF16), pltpu.VMEM((T, T, C), BF16)
+    square, narrow = pltpu.VMEM((C, C), BF16), pltpu.VMEM((80, C), BF16)
+    low_rank = pltpu.VMEM((48, C), BF16)
+    w_xproj = w_xproj.T
+    x_pre, z_pre, dt_pre, gated, step, u, x, grad, b, c, term, rates, row_sent = call(
         first_kernel,
         (
-            f32(CELLS, C), f32(CELLS, C), f32(CELLS, C), f32(CELLS, C),
-            f32(T, PAD, C), f32(T, PAD, C), f32(CELLS, C), f32(T, PAD, C),
-            f32(CELLS, N, 128), f32(CELLS, N, 128), f32(T, N, C), f32(16, 32, HALF),
+            flat, flat, flat, flat, grid, grid, flat, grid, spread, spread, f32(T, N, C),
+            f32(N, C), f32(16, 32, HALF),
         ),
-        (pltpu.VMEM((T, PAD, C), BF16), pltpu.VMEM((T, PAD, C), BF16), vmem(N, C), edge),
-        "first",
-    )(tokens, w_in, w_xproj, w_dt, dt_bias.reshape(1, C), a_log, w_out, out_grad)
+        (
+            cells, square, square, narrow, low_rank, vmem(N, C), square, cells,
+            padded, padded, edge, pltpu.SemaphoreType.DMA((8,)),
+        ),
+        "first", 54,
+        tokens, w_in, w_xproj, w_dt, a_log, w_out, out_grad, dt_bias,
+        fetched=range(7),
+    )
     row_got = swap(row_sent, "col")
-    row_in = swap(prefix("col", ((0, False),), 24, 24, row_got, row_got, a_log), "col")
+    row_in = swap(prefix("col", ((0, False),), 24, 24, row_got, row_got, rates), "col")
     col_sent = call(
-        forward_kernel, f32(16, 56, HALF), (vmem(N, C), edge, edge), "forward"
-    )(row_in, a_log, step, u, b, term)
+        forward_kernel, f32(16, 56, HALF), (edge, edge), "forward", 6,
+        row_in, rates, step, u, b, term,
+    )
     col_all = swap(col_sent, "row")
     col_got = swap(
-        prefix("row", ((0, False), (24, True)), 48, 48, col_all, col_all, a_log), "row"
+        prefix("row", ((0, False), (24, True)), 48, 48, col_all, col_all, rates), "row"
     )
     back_sent = call(
-        backward_kernel, f32(16, 24, HALF), (vmem(N, C), edge, edge), "backward"
-    )(col_got, a_log, step, grad, c)
+        backward_kernel, f32(16, 24, HALF), (edge, edge), "backward", 6,
+        col_got, rates, step, grad, c,
+    )
     back_all = swap(back_sent, "col")
-    row_from = swap(prefix("col", ((0, True),), 24, 24, back_all, row_got, a_log), "col")
+    row_from = swap(prefix("col", ((0, True),), 24, 24, back_all, row_got, rates), "col")
     out = jax.ShapeDtypeStruct((T, T, C), BF16)
-    wide = vmem(T, PAD, C)
     return call(
         last_kernel,
         (out, out),
         (
-            vmem(N, C), edge, edge, vmem(CELLS, N, C), vmem(CELLS, N, C), wide, wide, wide,
-            vmem(CELLS, N, 128), vmem(CELLS, N, 128), pltpu.VMEM((80, C), BF16),
+            pltpu.VMEM((C, 2 * C), BF16), narrow, low_rank, square, cells, cells,
+            edge, edge, kept, kept, wide, wide, wide,
+            vmem(CELLS, N, 128), vmem(CELLS, N, 128), narrow, pltpu.SemaphoreType.DMA((6,)),
         ),
-        "last",
-    )(
-        row_in, col_got, row_from, x_pre, z_pre, dt_pre, gated, step, u, x, grad, b, c, a_log,
-        d_skip.reshape(1, C), w_in, w_xproj, w_dt, w_out,
+        "last", 42,
+        row_in, col_got, row_from, x_pre, z_pre, dt_pre, gated, step, u, x, grad, b, c, rates,
+        d_skip, w_in, w_xproj, w_dt, w_out,
+        fetched=range(15, 19), out_spec=IN_HBM,
     )
 
 

time: 200 us -> 178 us (0.89)
  blocking collectives: 129 us -> 148 us
  waiting for transfers between devices: 18.1 us -> 0 us
  Pallas kernels: 43.8 us -> 28.9 us
  local copies, waits for them, and re-layouts: 4.4 us -> 0.07 us
  starting transfers between devices: 3.49 us -> 0 us
    all_to_all x5 -> x6, blocking collectives: 129 us -> 148 us  [swap(): return lax.all_to_all(sent, axis, 0, 0, tiled=True)]
    all_to_all x1 -> x0, waiting for transfers between devices: 18.1 us -> none  [swap(): return lax.all_to_all(sent, axis, 0, 0, tiled=True)]
    pallas_call x7, Pallas kernels: 43.8 us -> 28.9 us  [call(): pl.pallas_call(kernel, out_shape=out_shape, in_specs=[IN_HBM if k in fetc...]
    all_to_all x1 -> x0, starting transfers between devices: 3.49 us -> none  [swap(): return lax.all_to_all(sent, axis, 0, 0, tiled=True)]
    unnamed x5 -> x32, local copies, waits for them, and re-layouts: 2.54 us -> 0.07 us
  transfers between devices with their start and end apart: 1 -> 0, of which waited for: 1 -> 0; matrix products, arithmetic and copies ran while one was open for 0% -> 0% of each run, Pallas kernels for 0% -> 0%
where the time goes in v2:
time: 178 us; the launch traced here: 177 us
  blocking collectives  148 us (83%)
  Pallas kernels  28.9 us (16%)
    all_to_all x6, blocking collectives, swap(): return lax.all_to_all(sent, axis, 0, 0, tiled=True)  148 us
    pallas_call x7, Pallas kernels, call(): pl.pallas_call(kernel, out_shape=out_shape, in_specs=[IN_HBM if k in fetc...  28.9 us

profile of v2, /device:TPU:1, one launch (start us, length us, event | category | flops | bytes accessed | tf_op | source)
XLA Modules:
  0.0 177.4 jit_solution(10467985941376612016)
XLA Ops:
  0.6 11.1 %first.1 = (f32[192,768]{1,0:T(8,128)}, f32[192,768]{1,0:T(8,128)}, f32[192,768]{1,0:T(8,128)}, f32[192,768]{1,0:T(8,128)}, f32[12,16,768]{2,1,0:T(8,128)}, /*in...) custom-call(bf16[12,12,768]{2,1,0:T(8,128)(2,1)} %tokens_hbm.1, ...), custom_call_target="tpu_custom_call" | custom-call | tf_op jit(solution)/shard_map/first/pallas_call | solution.py:346
  11.8 0.0 copy-start.6
  11.8 32.9 %all_to_all.30.got_ref.sums_ref = f32[16,32,384]{2,1,0:T(8,128)S(1)} all-to-all(f32[16,32,384]{2,1,0:T(8,128)} %get-tuple-element.15), channel_id=1, replica_groups=mesh['row'=16,'col'=16] {'col'}, dimensions={0} | all-to-all | bytes 1572864 | tf_op jit(solution)/shard_map/all_to_all | solution.py:373
  44.7 0.0 copy-done.6
  44.7 0.0 copy-start
  44.7 0.0 copy-start.2
  44.7 0.0 copy-start.5
  44.7 0.0 copy-start.12
  44.7 0.1 prefix_col.2
  44.8 22.0 %all_to_all.31.row_in_ref = f32[16,24,384]{2,1,0:T(8,128)S(1)} all-to-all(f32[16,24,384]{2,1,0:T(8,128)S(1)} %prefix_col.2), channel_id=1, replica_groups=mesh['row'=16,'col'=16] {'col'}, dimensions={0} | all-to-all | bytes 1179648 | tf_op jit(solution)/shard_map/all_to_all | solution.py:373
  66.8 0.0 copy-done
  66.8 0.0 copy-done.2
  66.8 0.0 copy-done.5
  66.8 0.0 copy-done.12
  66.8 1.9 %forward.1 = f32[16,56,384]{2,1,0:T(8,128)S(1)} custom-call(f32[16,24,384]{2,1,0:T(8,128)S(1)} %all_to_all.31.row_in_ref, f32[16,768]{1,0:T(8,128)S(1)} %copy-done.6, f32[12,16,768]{2,1,0:T(8,128)S(1)} %copy-done.2, f32[12,16,768]{2,1,0:T(8,128)S(1)} %copy-done.5, f32[192,16,128]{2,1,0:T(8,128)S(1)} %copy-done, f32[12,16,768]{2,1,0:T(8,128)S(1)} %copy-done.12), custom_call_target="tpu_custom_call" | custom-call | tf_op jit(solution)/shard_map/forward/pallas_call | solution.py:346
  68.8 26.0 %all_to_all.32.got_ref.sums_ref = f32[16,56,384]{2,1,0:T(8,128)S(1)} all-to-all(f32[16,56,384]{2,1,0:T(8,128)S(1)} %forward.1), channel_id=1, replica_groups=mesh['row'=16,'col'=16] {'row'}, dimensions={0} | all-to-all | bytes 2752512 | tf_op jit(solution)/shard_map/all_to_all | solution.py:373
  94.8 0.2 prefix_row.1
  94.9 0.0 copy-start.1
  94.9 0.0 copy-start.4
  95.0 20.7 %all_to_all.33.col_got_ref = f32[16,48,384]{2,1,0:T(8,128)S(1)} all-to-all(f32[16,48,384]{2,1,0:T(8,128)S(1)} %prefix_row.1), channel_id=1, replica_groups=mesh['row'=16,'col'=16] {'row'}, dimensions={0} | all-to-all | bytes 2359296 | tf_op jit(solution)/shard_map/all_to_all | solution.py:373
  115.6 0.0 copy-done.1
  115.6 0.0 copy-done.4
  115.7 1.7 backward.1
  117.4 0.0 copy-start.10
  117.4 0.0 copy-start.11
  117.4 24.2 %all_to_all.34.got_ref = f32[16,24,384]{2,1,0:T(8,128)S(1)} all-to-all(f32[16,24,384]{2,1,0:T(8,128)S(1)} %backward.1), channel_id=1, replica_groups=mesh['row'=16,'col'=16] {'col'}, dimensions={0} | all-to-all | bytes 1179648 | tf_op jit(solution)/shard_map/all_to_all | solution.py:373
  141.6 0.0 copy-start.3
  141.6 0.0 copy-start.7
  141.6 0.0 copy-start.8
  141.6 0.0 copy-start.9
  141.6 0.0 copy-start.13
  141.6 0.0 copy-start.14
  141.6 0.0 copy-start.15
  141.6 0.1 prefix_col.3
  141.8 21.8 %all_to_all.35.row_from_ref = f32[16,24,384]{2,1,0:T(8,128)S(1)} all-to-all(f32[16,24,384]{2,1,0:T(8,128)S(1)} %prefix_col.3), channel_id=1, replica_groups=mesh['row'=16,'col'=16] {'col'}, dimensions={0} | all-to-all | bytes 1179648 | tf_op jit(solution)/shard_map/all_to_all | solution.py:373
  163.6 0.0 copy-done.10
  163.6 0.0 copy-done.11
  163.6 0.0 copy-done.3
  163.6 0.0 copy-done.7
  163.6 0.0 copy-done.8
  163.6 0.0 copy-done.9
  163.6 0.0 copy-done.13
  163.7 0.0 copy-done.14
  163.7 0.0 copy-done.15
  163.7 13.7 %last.1 = (bf16[12,12,768]{2,1,0:T(8,128)(2,1)}, bf16[12,12,768]{2,1,0:T(8,128)(2,1)}) custom-call(f32[16,24,384]{2,1,0:T(8,128)S(1)} %all_to_all.31.row_in_ref, f32[16,48,384]{2,1,0:T(8,128)S(1)} %all_to_all.33.col_got_ref, f32[16,24,384]{2,1,0:T(8,128)S(1)} %all_to_all.35.row_from_ref, f32[192,768]{1,0:T(8,128)S(1)} %copy-done.7, ...), custom_call_target="tpu_custom_call" | custom-call | tf_op jit(solution)/shard_map/last/pallas_call | solution.py:346
Async XLA Ops:
  11.8 32.9 %copy-start.6 = (f32[16,768]{1,0:T(8,128)S(1)}, f32[16,768]{1,0:T(8,128)}, u32[]{:S(2)}) copy-start(f32[16,768]{1,0:T(8,128)} %get-tuple-element.16.rates_ref.rates_s) | copy-start | bytes 147460
  44.7 22.1 %copy-start = (f32[192,16,128]{2,1,0:T(8,128)S(1)}, f32[192,16,128]{2,1,0:T(8,128)}, u32[]{:S(2)}) copy-start(f32[192,16,128]{2,1,0:T(8,128)} %get-tuple-element.19.b_ref) | copy-start | bytes 4718596
  44.7 22.1 %copy-start.2 = (f32[12,16,768]{2,1,0:T(8,128)S(1)}, f32[12,16,768]{2,1,0:T(8,128)}, u32[]{:S(2)}) copy-start(f32[12,16,768]{2,1,0:T(8,128)} %get-tuple-element.17.step_ref) | copy-start | bytes 1769476
  44.7 22.1 %copy-start.5 = (f32[12,16,768]{2,1,0:T(8,128)S(1)}, f32[12,16,768]{2,1,0:T(8,128)}, u32[]{:S(2)}) copy-start(f32[12,16,768]{2,1,0:T(8,128)} %get-tuple-element.18.u_ref) | copy-start | bytes 1769476
  44.7 22.1 %copy-start.12 = (f32[12,16,768]{2,1,0:T(8,128)S(1)}, f32[12,16,768]{2,1,0:T(8,128)}, u32[]{:S(2)}) copy-start(f32[12,16,768]{2,1,0:T(8,128)} %get-tuple-element.20.term_ref) | copy-start | bytes 1769476
  94.9 20.7 %copy-start.1 = (f32[192,16,128]{2,1,0:T(8,128)S(1)}, f32[192,16,128]{2,1,0:T(8,128)}, u32[]{:S(2)}) copy-start(f32[192,16,128]{2,1,0:T(8,128)} %get-tuple-element.22.c_ref) | copy-start | bytes 4718596
  94.9 20.7 %copy-start.4 = (f32[12,16,768]{2,1,0:T(8,128)S(1)}, f32[12,16,768]{2,1,0:T(8,128)}, u32[]{:S(2)}) copy-start(f32[12,16,768]{2,1,0:T(8,128)} %get-tuple-element.21.grad_ref) | copy-start | bytes 1769476
  117.4 46.2 %copy-start.10 = (f32[192,768]{1,0:T(8,128)S(1)}, f32[192,768]{1,0:T(8,128)}, u32[]{:S(2)}) copy-start(f32[192,768]{1,0:T(8,128)} %get-tuple-element.26.gated_ref) | copy-start | bytes 1769476
  117.4 46.2 %copy-start.11 = (f32[192,768]{1,0:T(8,128)S(1)}, f32[192,768]{1,0:T(8,128)}, u32[]{:S(2)}) copy-start(f32[192,768]{1,0:T(8,128)} %get-tuple-element.27.x_ref) | copy-start | bytes 1769476
  141.6 22.0 %copy-start.3 = (bf16[768,768]{1,0:T(8,128)(2,1)S(1)}, bf16[768,768]{1,0:T(8,128)(2,1)}, u32[]{:S(2)}) copy-start(bf16[768,768]{1,0:T(8,128)(2,1)} %w_out_hbm.3) | copy-start | bytes 3538948
  141.6 22.0 %copy-start.7 = (f32[192,768]{1,0:T(8,128)S(1)}, f32[192,768]{1,0:T(8,128)}, u32[]{:S(2)}) copy-start(f32[192,768]{1,0:T(8,128)} %get-tuple-element.23.x_pre_ref) | copy-start | bytes 1769476
  141.6 22.0 %copy-start.8 = (f32[192,768]{1,0:T(8,128)S(1)}, f32[192,768]{1,0:T(8,128)}, u32[]{:S(2)}) copy-start(f32[192,768]{1,0:T(8,128)} %get-tuple-element.24.z_pre_ref) | copy-start | bytes 1769476
  141.6 22.0 %copy-start.9 = (f32[192,768]{1,0:T(8,128)S(1)}, f32[192,768]{1,0:T(8,128)}, u32[]{:S(2)}) copy-start(f32[192,768]{1,0:T(8,128)} %get-tuple-element.25.dt_pre_ref) | copy-start | bytes 1769476
  141.6 22.0 %copy-start.13 = (bf16[768,80]{0,1:T(8,128)(2,1)S(1)}, bf16[768,80]{0,1:T(8,128)(2,1)}, u32[]{:S(2)}) copy-start(bf16[768,80]{0,1:T(8,128)(2,1)} %param.11) | copy-start | bytes 368644
  141.6 22.0 %copy-start.14 = (bf16[48,768]{1,0:T(8,128)(2,1)S(1)}, bf16[48,768]{1,0:T(8,128)(2,1)}, u32[]{:S(2)}) copy-start(bf16[48,768]{1,0:T(8,128)(2,1)} %w_dt_hbm.3) | copy-start | bytes 221188
  141.6 22.0 %copy-start.15 = (f32[768]{0:T(1024)S(1)}, f32[768]{0:T(1024)}, u32[]{:S(2)}) copy-start(f32[768]{0:T(1024)} %d_skip_ref.1) | copy-start | bytes 9220

commit v3 on v2

--- a/solution.py
+++ b/solution.py
@@ -20,37 +20,48 @@
     return lax.dot_general(left, right, (((1,), (1,)), ((), ())), preferred_element_type=F32)
 
 
-def blocks():
+def pieces():
     for i in range(T):
         for h in range(2):
             q = 2 * i + h
-            for half in range(2):
-                yield i, h, half, 2 * (q // 3) + half, 8 * (q % 3)
-
-
-def pack(out_ref, base, edge_ref):
-    for i, h, half, chunk, row in blocks():
-        out_ref[chunk, base + row : base + row + 8, :] = edge_ref[
-            i, 8 * h : 8 * h + 8, HALF * half : HALF * half + HALF
+            for k in range(3):
+                yield i, slice(8 * h, 8 * h + 8), k, q // 3, 8 * (3 * (q % 3) + k)
+
+
+def half_lanes(half, k):
+    if isinstance(half, int):
+        return slice(HALF * half + 128 * k, HALF * half + 128 * k + 128)
+    return pl.ds(pl.multiple_of(HALF * half + 128 * k, 128), 128)
+
+
+def pack_half(chunk_of, base, edge_ref, half):
+    for i, states, k, group, row in pieces():
+        chunk_of(group)[base + row : base + row + 8, :] = edge_ref[i, states, half_lanes(half, k)]
+
+
+def unpack_half(edge_ref, chunk_of, base, half):
+    for i, states, k, group, row in pieces():
+        edge_ref[i, states, half_lanes(half, k)] = chunk_of(group)[base + row : base + row + 8, :]
+
+
+def pack_sums(chunk_of, base, sum_ref, half):
+    for group in range(8):
+        rows = [
+            sum_ref[pl.ds(3 * group // 2 + u, 1), half_lanes(half, k)]
+            for u in range(2)
+            for k in range(3)
         ]
-
-
-def unpack(edge_ref, in_ref, base):
-    for i, h, half, chunk, row in blocks():
-        edge_ref[i, 8 * h : 8 * h + 8, HALF * half : HALF * half + HALF] = in_ref[
-            chunk, base + row : base + row + 8, :
-        ]
-
-
-def pack_sums(out_ref, base, sum_rows):
-    for chunk in range(16):
-        group, half = chunk // 2, chunk % 2
-        rows = [
-            sum_rows[(3 * group + t) // 2][:, HALF * half : HALF * half + HALF] for t in range(3)
-        ]
-        out_ref[chunk, base : base + 8, :] = jnp.concatenate(
-            rows + [jnp.zeros((5, HALF), F32)], axis=0
+        chunk_of(group)[base : base + 8, :] = jnp.concatenate(
+            rows + [jnp.zeros((2, 128), F32)], axis=0
         )
+
+
+def both_halves(ref):
+    return [(lambda group, half=half: ref.at[2 * group + half]) for half in range(2)]
+
+
+def one_half(ref):
+    return lambda group: ref.at[group]
 
 
 def fetch(pairs, sems):
@@ -63,9 +74,9 @@
 def first_kernel(
     tokens_hbm, w_in_hbm, w_xproj_hbm, w_dt_hbm, a_log_hbm, w_out_hbm, out_grad_hbm, dt_bias_ref,
     x_pre_ref, z_pre_ref, dt_pre_ref, gated_ref, step_ref, u_ref, x_ref, grad_ref, b_ref, c_ref,
-    term_ref, rates_ref, sent_ref,
+    term_ref, rates_ref, own_ref, other_ref,
     tokens_ref, w_x_ref, w_z_ref, w_xproj_ref, w_dt_ref, a_log_ref, w_out_ref, out_grad_ref,
-    tok_s, og_s, end_s, sems,
+    tok_s, og_s, end_s, sum_s, sems,
 ):
     copies = fetch(
         (
@@ -137,33 +148,86 @@
         return carry
 
     lax.fori_loop(0, T, one_row, 0)
-    pack(sent_ref, 0, end_s)
-    pack_sums(
-        sent_ref, 24, [jnp.sum(step_ref[i, 0:T, :], axis=0, keepdims=True) for i in range(T)]
-    )
+    for i in range(T):
+        sum_s[i : i + 1, :] = jnp.sum(step_ref[i, 0:T, :], axis=0, keepdims=True)
+    core = lax.axis_index("col") % 2
+    for ref, half in ((own_ref, core), (other_ref, 1 - core)):
+        pack_half(one_half(ref), 0, end_s, half)
+        pack_sums(one_half(ref), 72, sum_s, half)
+
+
+def chip_decay(core, rates_ref, part, group, t, k):
+    states = 8 * ((3 * group + t) % 2)
+    u = (3 * group + t) // 2 - 3 * group // 2
+    rate = rates_ref[states : states + 8, half_lanes(core, k)]
+    return jnp.exp2(rate * part[72 + 3 * u + k : 73 + 3 * u + k, :])
+
+
+def combine_kernel(reverse, own_ref, got_ref, own_sums_ref, got_sums_ref, rates_ref, out_ref):
+    core = lax.axis_index("col") % 2
+    own_first = core == (1 if reverse else 0)
+    for group in range(8):
+        own, got = own_ref[group], got_ref[group]
+        own_sums, got_sums = own_sums_ref[group], got_sums_ref[group]
+        early, late = jnp.where(own_first, own, got), jnp.where(own_first, got, own)
+        late_sums = jnp.where(own_first, got_sums, own_sums)
+        for t in range(3):
+            for k in range(3):
+                rows = slice(8 * (3 * t + k), 8 * (3 * t + k) + 8)
+                decay = chip_decay(core, rates_ref, late_sums, group, t, k)
+                out_ref[group, rows, :] = decay * early[rows] + late[rows]
+        if not reverse:
+            out_ref[group, 72:80, :] = own[72:80] + got[72:80]
+
+
+def split_kernel(
+    reverse, state_ref, own_ref, got_ref, own_sums_ref, got_sums_ref, rates_ref, keep_ref, send_ref
+):
+    core = lax.axis_index("col") % 2
+    own_first = core == (1 if reverse else 0)
+    for group in range(8):
+        early = jnp.where(own_first, own_ref[group], got_ref[group])
+        early_sums = jnp.where(own_first, own_sums_ref[group], got_sums_ref[group])
+        for t in range(3):
+            for k in range(3):
+                rows = slice(8 * (3 * t + k), 8 * (3 * t + k) + 8)
+                state = state_ref[group, rows, :]
+                through = (
+                    chip_decay(core, rates_ref, early_sums, group, t, k) * state + early[rows]
+                )
+                keep_ref[group, rows, :] = jnp.where(own_first, state, through)
+                send_ref[group, rows, :] = jnp.where(own_first, through, state)
 
 
 def prefix_kernel(axis, spans, sum_base, got_ref, sums_ref, rates_ref, out_ref):
     me = lax.axis_index(axis)
     group, half = me // 2, me % 2
+    tiles = got_ref.shape[0]
     for t in range(3):
-        state_rows = pl.multiple_of(8 * ((3 * group + t) % 2), 8)
-        lanes = pl.multiple_of(HALF * half, 128)
-        rate = rates_ref[pl.ds(state_rows, 8), pl.ds(lanes, HALF)]
-        for base, reverse in spans:
-            state = jnp.zeros((8, HALF), F32)
-            rows = slice(base + 8 * t, base + 8 * t + 8)
-            for hop in range(16):
-                tile = 15 - hop if reverse else hop
-                out_ref[tile, rows, :] = state
-                decay = jnp.exp2(rate * sums_ref[tile, sum_base + t : sum_base + t + 1, :])
-                state = decay * state + got_ref[tile, rows, :]
+        states = pl.multiple_of(8 * ((3 * group + t) % 2), 8)
+        later = (3 * group + t) // 2 > (3 * group) // 2
+        for k in range(3):
+            rate = rates_ref[pl.ds(states, 8), half_lanes(half, k)]
+            for base, reverse in spans:
+                state = jnp.zeros((8, 128), F32)
+                rows = slice(base + 8 * (3 * t + k), base + 8 * (3 * t + k) + 8)
+                for hop in range(tiles):
+                    tile = tiles - 1 - hop if reverse else hop
+                    out_ref[tile, rows, :] = state
+                    total = jnp.where(
+                        later,
+                        sums_ref[tile, sum_base + 3 + k : sum_base + 4 + k, :],
+                        sums_ref[tile, sum_base + k : sum_base + k + 1, :],
+                    )
+                    state = jnp.exp2(rate * total) * state + got_ref[tile, rows, :]
 
 
 def forward_kernel(
-    row_in_ref, rates_s, step_ref, u_ref, b_ref, term_ref, sent_ref, row_s, col_s
+    keep_ref, came_ref, rates_s, step_ref, u_ref, b_ref, term_ref, sent_ref, row_s, col_s, sum_s
 ):
-    unpack(row_s, row_in_ref, 0)
+    core = lax.axis_index("col") % 2
+    unpack_half(row_s, one_half(keep_ref), 0, core)
+    unpack_half(row_s, one_half(came_ref), 0, 1 - core)
     col_s[...] = jnp.zeros_like(col_s)
 
     def one_row(i, carry):
@@ -177,18 +241,21 @@
         return carry
 
     lax.fori_loop(0, T, one_row, 0)
-    pack(sent_ref, 0, col_s)
-    pack(sent_ref, 24, term_ref)
     total = step_ref[0]
     for i in range(1, T):
         total = total + step_ref[i]
-    pack_sums(sent_ref, 48, [total[j : j + 1, :] for j in range(T)])
+    sum_s[...] = total
+    for half, chunk_of in enumerate(both_halves(sent_ref)):
+        pack_half(chunk_of, 0, col_s, half)
+        pack_half(chunk_of, 72, term_ref, half)
+        pack_sums(chunk_of, 144, sum_s, half)
 
 
 def backward_kernel(
-    col_got_ref, rates_s, step_ref, grad_ref, c_ref, sent_ref, term_s, end_s
+    col_got_ref, rates_s, step_ref, grad_ref, c_ref, own_ref, other_ref, term_s, end_s
 ):
-    unpack(term_s, col_got_ref, 24)
+    for half, chunk_of in enumerate(both_halves(col_got_ref)):
+        unpack_half(term_s, chunk_of, 72, half)
 
     def one_row(back, carry):
         i = T - 1 - back
@@ -205,11 +272,13 @@
         return carry
 
     lax.fori_loop(0, T, one_row, 0)
-    pack(sent_ref, 0, end_s)
+    core = lax.axis_index("col") % 2
+    pack_half(one_half(own_ref), 0, end_s, core)
+    pack_half(one_half(other_ref), 0, end_s, 1 - core)
 
 
 def last_kernel(
-    row_in_ref, col_got_ref, row_from_ref, x_pre_ref, z_pre_ref, dt_pre_ref, gated_ref, step_ref,
+    keep_ref, came_ref, col_got_ref, back_keep_ref, back_came_ref, x_pre_ref, z_pre_ref, dt_pre_ref, gated_ref, step_ref,
     u_ref, x_ref, grad_ref, b_ref, c_ref, rates_s, d_skip_ref, w_in_hbm, w_xproj_hbm, w_dt_hbm,
     w_out_hbm,
     layer_hbm, token_hbm,
@@ -225,8 +294,11 @@
         ),
         sems,
     )
-    unpack(row_s, row_in_ref, 0)
-    unpack(col_s, col_got_ref, 0)
+    core = lax.axis_index("col") % 2
+    unpack_half(row_s, one_half(keep_ref), 0, core)
+    unpack_half(row_s, one_half(came_ref), 0, 1 - core)
+    for half, chunk_of in enumerate(both_halves(col_got_ref)):
+        unpack_half(col_s, chunk_of, 0, half)
     for ref in (scan_s, step_sum_s, x_sum_s, b_part, c_part):
         ref[...] = jnp.zeros_like(ref)
 
@@ -267,8 +339,10 @@
     scan_s[...] = (gated_ref[...] * scan_out * (z_sig * (1.0 + z_pre * (1.0 - z_sig)))).reshape(
         T, PAD, C
     )
-    unpack(col_s, col_got_ref, 24)
-    unpack(row_s, row_from_ref, 0)
+    for half, chunk_of in enumerate(both_halves(col_got_ref)):
+        unpack_half(col_s, chunk_of, 72, half)
+    unpack_half(row_s, one_half(back_keep_ref), 0, core)
+    unpack_half(row_s, one_half(back_came_ref), 0, 1 - core)
 
     def up_row(back, carry):
         i = T - 1 - back
@@ -366,51 +440,77 @@
     def kernel(got_ref, sums_ref, rates_ref, out_ref):
         prefix_kernel(axis, spans, sum_base, got_ref, sums_ref, rates_ref, out_ref)
 
-    return call(kernel, f32(16, rows, HALF), (), "prefix_" + axis, 4, got, sums, rates)
-
-
-def swap(sent, axis):
-    return lax.all_to_all(sent, axis, 0, 0, tiled=True)
+    out = f32(got.shape[0], rows, 128)
+    return call(kernel, out, (), "prefix_" + axis, 4, got, sums, rates)
+
+
+def swap(sent, axis, groups=None):
+    return lax.all_to_all(sent, axis, 0, 0, tiled=True, axis_index_groups=groups)
+
+
+def row_scan(own, other, sums, rates, reverse):
+    partner = [(place, place ^ 1) for place in range(16)]
+    same_core = [[2 * chip + core for chip in range(8)] for core in range(2)]
+    got = lax.ppermute(other, "col", partner)
+    if sums is None:
+        sums = (own, got)
+
+    def combine(*refs):
+        combine_kernel(reverse, *refs)
+
+    def split(*refs):
+        split_kernel(reverse, *refs)
+
+    chip = call(
+        combine, f32(8, own.shape[1], 128), (), "combine", 6, own, got, *sums[:2], rates
+    )
+    chips = swap(chip, "col", same_core)
+    chip_sums = chips if len(sums) == 2 else sums[2]
+    state = swap(
+        prefix("col", ((0, reverse),), 72, 72, chips, chip_sums, rates), "col", same_core
+    )
+    half = f32(8, 72, 128)
+    keep, send = call(split, (half, half), (), "split", 6, state, own, got, *sums[:2], rates)
+    return keep, lax.ppermute(send, "col", partner), (*sums[:2], chip_sums)
 
 
 def body(tokens, w_in, w_xproj, w_dt, dt_bias, a_log, d_skip, w_out, out_grad):
     edge, wide = vmem(T, N, C), vmem(T, PAD, C)
     flat, grid, spread = f32(CELLS, C), f32(T, PAD, C), f32(CELLS, N, 128)
-    kept = vmem(T * T, N, C)
+    kept, sums = vmem(T * T, N, C), vmem(PAD, C)
     padded, cells = pltpu.VMEM((T, PAD, C), BF16), pltpu.VMEM((T, T, C), BF16)
     square, narrow = pltpu.VMEM((C, C), BF16), pltpu.VMEM((80, C), BF16)
     low_rank = pltpu.VMEM((48, C), BF16)
     w_xproj = w_xproj.T
-    x_pre, z_pre, dt_pre, gated, step, u, x, grad, b, c, term, rates, row_sent = call(
+    x_pre, z_pre, dt_pre, gated, step, u, x, grad, b, c, term, rates, own, other = call(
         first_kernel,
         (
             flat, flat, flat, flat, grid, grid, flat, grid, spread, spread, f32(T, N, C),
-            f32(N, C), f32(16, 32, HALF),
+            f32(N, C), f32(8, 80, 128), f32(8, 80, 128),
         ),
         (
             cells, square, square, narrow, low_rank, vmem(N, C), square, cells,
-            padded, padded, edge, pltpu.SemaphoreType.DMA((8,)),
+            padded, padded, edge, sums, pltpu.SemaphoreType.DMA((8,)),
         ),
         "first", 54,
         tokens, w_in, w_xproj, w_dt, a_log, w_out, out_grad, dt_bias,
         fetched=range(7),
     )
-    row_got = swap(row_sent, "col")
-    row_in = swap(prefix("col", ((0, False),), 24, 24, row_got, row_got, rates), "col")
+    keep, came, chip_sums = row_scan(own, other, None, rates, False)
     col_sent = call(
-        forward_kernel, f32(16, 56, HALF), (edge, edge), "forward", 6,
-        row_in, rates, step, u, b, term,
+        forward_kernel, f32(16, 152, 128), (edge, edge, sums), "forward", 6,
+        keep, came, rates, step, u, b, term,
     )
     col_all = swap(col_sent, "row")
     col_got = swap(
-        prefix("row", ((0, False), (24, True)), 48, 48, col_all, col_all, rates), "row"
-    )
-    back_sent = call(
-        backward_kernel, f32(16, 24, HALF), (edge, edge), "backward", 6,
+        prefix("row", ((0, False), (72, True)), 144, 144, col_all, col_all, rates), "row"
+    )
+    back_half = f32(8, 72, 128)
+    back_own, back_other = call(
+        backward_kernel, (back_half, back_half), (edge, edge), "backward", 6,
         col_got, rates, step, grad, c,
     )
-    back_all = swap(back_sent, "col")
-    row_from = swap(prefix("col", ((0, True),), 24, 24, back_all, row_got, rates), "col")
+    back_keep, back_came, chip_sums = row_scan(back_own, back_other, chip_sums, rates, True)
     out = jax.ShapeDtypeStruct((T, T, C), BF16)
     return call(
         last_kernel,
@@ -421,9 +521,9 @@
             vmem(CELLS, N, 128), vmem(CELLS, N, 128), narrow, pltpu.SemaphoreType.DMA((6,)),
         ),
         "last", 42,
-        row_in, col_got, row_from, x_pre, z_pre, dt_pre, gated, step, u, x, grad, b, c, rates,
+        keep, came, col_got, back_keep, back_came, x_pre, z_pre, dt_pre, gated, step, u, x, grad, b, c, rates,
         d_skip, w_in, w_xproj, w_dt, w_out,
-        fetched=range(15, 19), out_spec=IN_HBM,
+        fetched=range(17, 21), out_spec=IN_HBM,
     )
 
 

time: 178 us -> 156 us (0.88)
  blocking collectives: 148 us -> 106 us
  starting transfers between devices: 0 us -> 12.1 us
  waiting for transfers between devices: 0 us -> 5.09 us
  local copies, waits for them, and re-layouts: 0.07 us -> 1.85 us
    all_to_all x6, blocking collectives: 148 us -> 106 us  [swap(): lax.all_to_all(sent, axis, 0, 0, tiled=True, axis_index_groups=groups)]
    ppermute x0 -> x4, starting transfers between devices: none -> 12.1 us  [the longest x2 6.34 us: row_scan(): got = lax.ppermute(other, 'col', partner)]
    ppermute x0 -> x4, waiting for transfers between devices: none -> 5.09 us  [the longest x2 2.68 us: row_scan(): got = lax.ppermute(other, 'col', partner)]
    pallas_call x7 -> x11, Pallas kernels: 28.9 us -> 29.2 us  [call(): pl.pallas_call(kernel, out_shape=out_shape, in_specs=[IN_HBM if k in fetc...]
  transfers between devices with their start and end apart: 0 -> 4, of which waited for: 0 -> 4; matrix products, arithmetic and copies ran while one was open for 0% -> 0% of each run, Pallas kernels for 0% -> 0%
where the time goes in v3:
time: 156 us; the launch traced here: 155 us
  blocking collectives  106 us (68%)
  Pallas kernels  29.2 us (19%)
  starting transfers between devices  12.1 us (8%)
  waiting for transfers between devices  5.09 us (3%)
  local copies, waits for them, and re-layouts  1.85 us (1%)
    all_to_all x6, blocking collectives, swap(): lax.all_to_all(sent, axis, 0, 0, tiled=True, axis_index_groups=groups)  106 us
    pallas_call x11, Pallas kernels, call(): pl.pallas_call(kernel, out_shape=out_shape, in_specs=[IN_HBM if k in fetc...  29.2 us
    ppermute x2, starting transfers between devices, row_scan(): got = lax.ppermute(other, 'col', partner)  6.34 us
    ppermute x2, starting transfers between devices, row_scan(): return (keep, lax.ppermute(send, 'col', partner), (*sums[:2], chip_sums))  5.77 us
  transfers between devices with their start and end apart: 4, of which 4 were waited for; matrix products, arithmetic and copies ran while one was open for 0% of the time, Pallas kernels for 0%

profile of v3, /device:TPU:1, one launch (start us, length us, event | category | flops | bytes accessed | tf_op | source)
XLA Modules:
  0.0 155.2 jit_solution(3380855546141470712)
XLA Ops:
  0.6 11.1 %first.1 = (f32[192,768]{1,0:T(8,128)}, f32[192,768]{1,0:T(8,128)}, f32[192,768]{1,0:T(8,128)}, f32[192,768]{1,0:T(8,128)}, f32[12,16,768]{2,1,0:T(8,128)}, /*in...) custom-call(bf16[12,12,768]{2,1,0:T(8,128)(2,1)} %tokens_hbm.1, ...), custom_call_target="tpu_custom_call" | custom-call | tf_op jit(solution)/shard_map/first/pallas_call | solution.py:420
  11.7 3.3 %collective-permute-start = (f32[8,80,128]{2,1,0:T(8,128)}, f32[8,80,128]{2,1,0:T(8,128)S(1)}, u32[]{:S(2)}, u32[]{:S(2)}) collective-permute-start(f32[8,80,128]{2,1,0:T(8,128)} %get-tuple-element.23), channel_id=1, source_target_pairs={{0,1},{1,0},{2,3},{3,2},{4,5},{5,4},{6,7},{7,6},{8,9},{9,8},{10,11... | collective-permute-start | bytes 983048 | tf_op jit(solution)/shard_map/ppermute | solution.py:454
  15.0 1.5 collective-permute-done.refs_1_.refs_3_.refs_2_.refs_4_
  16.5 1.0 copy-done
  17.4 0.8 copy-done.5
  18.2 0.1 combine.2
  18.3 0.0 copy-start.15
  18.3 19.2 %all_to_all.30.got_ref.sums_ref = f32[8,80,128]{2,1,0:T(8,128)S(1)} all-to-all(f32[8,80,128]{2,1,0:T(8,128)S(1)} %combine.2), channel_id=1, replica_groups={{0,2,4,6,8,10,12,14},{1,3,5,7,9,11,13,15},{16,18,20,22,24,26,28,30},{17..., dimensions={0} | all-to-all | bytes 655360 | tf_op jit(solution)/shard_map/all_to_all | solution.py:448
  37.5 0.1 prefix_col.2
  37.6 0.0 copy-start.2
  37.6 0.0 copy-start.4
  37.6 13.0 %all_to_all.31.refs_0_ = f32[8,72,128]{2,1,0:T(8,128)S(1)} all-to-all(f32[8,72,128]{2,1,0:T(8,128)S(1)} %prefix_col.2), channel_id=1, replica_groups={{0,2,4,6,8,10,12,14},{1,3,5,7,9,11,13,15},{16,18,20,22,24,26,28,30},{17..., dimensions={0} | all-to-all | bytes 589824 | tf_op jit(solution)/shard_map/all_to_all | solution.py:448
  50.7 0.1 split.2
  50.8 3.1 %collective-permute-start.1 = (f32[8,72,128]{2,1,0:T(8,128)S(1)}, f32[8,72,128]{2,1,0:T(8,128)S(1)}, u32[]{:S(2)}, u32[]{:S(2)}) collective-permute-start(f32[8,72,128]{2,1,0:T(8,128)S(1)} %get-tuple-element.26), channel_id=1, source_target_pairs={{0,1},{1,0},{2,3},{3,2},{4,5},{5,4},{6,7},{7,6},{8,9},{9,8},{10,11... | collective-permute-start | bytes 884744 | tf_op jit(solution)/shard_map/ppermute | solution.py:474
  53.8 1.2 collective-permute-done.1.came_ref
  55.1 0.0 copy-done.15
  55.1 0.0 copy-done.8
  55.1 0.0 copy-done.2
  55.1 0.0 copy-done.4
  55.1 2.0 %forward.1 = f32[16,152,128]{2,1,0:T(8,128)S(1)} custom-call(f32[8,72,128]{2,1,0:T(8,128)S(1)} %get-tuple-element.25.keep_ref, f32[8,72,128]{2,1,0:T(8,128)S(1)} %collective-permute-done.1.came_ref, f32[16,768]{1,0:T(8,128)S(1)} %copy-done.5, f32[12,16,768]{2,1,0:T(8,128)S(1)} %copy-done.4, f32[12,16,768]{2,1,0:T(8,128)S(1)} %copy-done.8, ...), custom_call_target="tpu_custom_call" | custom-call | tf_op jit(solution)/shard_map/forward/pallas_call | solution.py:420
  57.0 0.0 copy-start.6
  57.1 24.8 %all_to_all.32.got_ref.sums_ref = f32[16,152,128]{2,1,0:T(8,128)S(1)} all-to-all(f32[16,152,128]{2,1,0:T(8,128)S(1)} %forward.1), channel_id=1, replica_groups=mesh['row'=16,'col'=16] {'row'}, dimensions={0} | all-to-all | bytes 2490368 | tf_op jit(solution)/shard_map/all_to_all | solution.py:448
  81.9 0.0 copy-done.6
  81.9 0.2 prefix_row.1
  82.1 20.0 %all_to_all.33.col_got_ref = f32[16,144,128]{2,1,0:T(8,128)S(1)} all-to-all(f32[16,144,128]{2,1,0:T(8,128)S(1)} %prefix_row.1), channel_id=1, replica_groups=mesh['row'=16,'col'=16] {'row'}, dimensions={0} | all-to-all | bytes 2359296 | tf_op jit(solution)/shard_map/all_to_all | solution.py:448
  102.1 0.0 copy-done.3
  102.1 1.7 %backward.1 = (f32[8,72,128]{2,1,0:T(8,128)S(1)}, f32[8,72,128]{2,1,0:T(8,128)S(1)}) custom-call(f32[16,144,128]{2,1,0:T(8,128)S(1)} %all_to_all.33.col_got_ref, f32[16,768]{1,0:T(8,128)S(1)} %copy-done.6, f32[12,16,768]{2,1,0:T(8,128)S(1)} %copy-done.4, f32[12,16,768]{2,1,0:T(8,128)S(1)} %copy-done.9, f32[192,16,128]{2,1,0:T(8,128)S(1)} %copy-done.3), custom_call_target="tpu_custom_call" | custom-call | tf_op jit(solution)/shard_map/backward/pallas_call | solution.py:420
  103.8 3.1 %collective-permute-start.2 = (f32[8,72,128]{2,1,0:T(8,128)S(1)}, f32[8,72,128]{2,1,0:T(8,128)S(1)}, u32[]{:S(2)}, u32[]{:S(2)}) collective-permute-start(f32[8,72,128]{2,1,0:T(8,128)S(1)} %get-tuple-element.34), channel_id=1, source_target_pairs={{0,1},{1,0},{2,3},{3,2},{4,5},{5,4},{6,7},{7,6},{8,9},{9,8},{10,11... | collective-permute-start | bytes 884744 | tf_op jit(solution)/shard_map/ppermute | solution.py:454
  106.8 1.2 collective-permute-done.2.refs_1_.refs_2_
  108.0 0.1 combine.3
  108.1 0.0 copy-start.13
  108.1 15.1 %all_to_all.34.got_ref = f32[8,72,128]{2,1,0:T(8,128)S(1)} all-to-all(f32[8,72,128]{2,1,0:T(8,128)S(1)} %combine.3), channel_id=1, replica_groups={{0,2,4,6,8,10,12,14},{1,3,5,7,9,11,13,15},{16,18,20,22,24,26,28,30},{17..., dimensions={0} | all-to-all | bytes 589824 | tf_op jit(solution)/shard_map/all_to_all | solution.py:448
  123.3 0.1 prefix_col.3
  123.4 0.0 copy-start.7
  123.4 0.0 copy-start.16
  123.4 0.0 copy-start.17
  123.4 0.0 copy-start.18
  123.4 13.7 %all_to_all.35.refs_0_ = f32[8,72,128]{2,1,0:T(8,128)S(1)} all-to-all(f32[8,72,128]{2,1,0:T(8,128)S(1)} %prefix_col.3), channel_id=1, replica_groups={{0,2,4,6,8,10,12,14},{1,3,5,7,9,11,13,15},{16,18,20,22,24,26,28,30},{17..., dimensions={0} | all-to-all | bytes 589824 | tf_op jit(solution)/shard_map/all_to_all | solution.py:448
  137.2 0.1 split.3
  137.3 2.7 %collective-permute-start.3 = (f32[8,72,128]{2,1,0:T(8,128)S(1)}, f32[8,72,128]{2,1,0:T(8,128)S(1)}, u32[]{:S(2)}, u32[]{:S(2)}) collective-permute-start(f32[8,72,128]{2,1,0:T(8,128)S(1)} %get-tuple-element.36), channel_id=1, source_target_pairs={{0,1},{1,0},{2,3},{3,2},{4,5},{5,4},{6,7},{7,6},{8,9},{9,8},{10,11... | collective-permute-start | bytes 884744 | tf_op jit(solution)/shard_map/ppermute | solution.py:474
  140.0 1.2 collective-permute-done.3.back_came_ref
  141.2 0.0 copy-done.12
  141.2 0.0 copy-done.7
  141.2 0.0 copy-done.10
  141.2 0.0 copy-done.16
  141.2 0.0 copy-done.17
  141.2 0.0 copy-done.18
  141.2 13.8 %last.1 = (bf16[12,12,768]{2,1,0:T(8,128)(2,1)}, bf16[12,12,768]{2,1,0:T(8,128)(2,1)}) custom-call(f32[8,72,128]{2,1,0:T(8,128)S(1)} %get-tuple-element.25.keep_ref, f32[8,72,128]{2,1,0:T(8,128)S(1)} %collective-permute-done.1.came_ref, f32[16,144,128]{2,1,0:T(8,128)S(1)} %all_to_all.33.col_got_ref, f32[8,72,128]{2,1,0:T(8,128)S(1)} %get-tuple-element.35.back_keep_ref, ...), custom_call_target="tpu_custom_call" | custom-call | tf_op jit(solution)/shard_map/last/pallas_call | solution.py:420
  (15 shorter events, 0.0 us)
Async XLA Ops:
  11.7 4.8 %collective-permute-start = (f32[8,80,128]{2,1,0:T(8,128)}, f32[8,80,128]{2,1,0:T(8,128)S(1)}, u32[]{:S(2)}, u32[]{:S(2)}) collective-permute-start(f32[8,80,128]{2,1,0:T(8,128)} %get-tuple-element.23), channel_id=1, source_target_pairs={{0,1},{1,0},{2,3},{3,2},{4,5},{5,4},{6,7},{7,6},{8,9},{9,8},{10,11... | collective-permute-start | bytes 983048 | tf_op jit(solution)/shard_map/ppermute | solution.py:454
  16.5 1.0 copy-start
  17.4 0.8 copy-start.5
  18.3 36.7 %copy-start.15 = (f32[12,16,768]{2,1,0:T(8,128)S(1)}, f32[12,16,768]{2,1,0:T(8,128)}, u32[]{:S(2)}) copy-start(f32[12,16,768]{2,1,0:T(8,128)} %get-tuple-element.30.term_ref) | copy-start | bytes 1769476
  37.5 17.5 %copy-start.8 = (f32[12,16,768]{2,1,0:T(8,128)S(1)}, f32[12,16,768]{2,1,0:T(8,128)}, u32[]{:S(2)}) copy-start(f32[12,16,768]{2,1,0:T(8,128)} %get-tuple-element.28.u_ref) | copy-start | bytes 1769476
  37.6 17.5 %copy-start.2 = (f32[192,16,128]{2,1,0:T(8,128)S(1)}, f32[192,16,128]{2,1,0:T(8,128)}, u32[]{:S(2)}) copy-start(f32[192,16,128]{2,1,0:T(8,128)} %get-tuple-element.29.b_ref) | copy-start | bytes 4718596
  37.6 17.4 %copy-start.4 = (f32[12,16,768]{2,1,0:T(8,128)S(1)}, f32[12,16,768]{2,1,0:T(8,128)}, u32[]{:S(2)}) copy-start(f32[12,16,768]{2,1,0:T(8,128)} %get-tuple-element.27.step_ref) | copy-start | bytes 1769476
  50.8 4.3 %collective-permute-start.1 = (f32[8,72,128]{2,1,0:T(8,128)S(1)}, f32[8,72,128]{2,1,0:T(8,128)S(1)}, u32[]{:S(2)}, u32[]{:S(2)}) collective-permute-start(f32[8,72,128]{2,1,0:T(8,128)S(1)} %get-tuple-element.26), channel_id=1, source_target_pairs={{0,1},{1,0},{2,3},{3,2},{4,5},{5,4},{6,7},{7,6},{8,9},{9,8},{10,11... | collective-permute-start | bytes 884744 | tf_op jit(solution)/shard_map/ppermute | solution.py:474
  57.0 24.8 %copy-start.6 = (f32[16,768]{1,0:T(8,128)S(1)}, f32[16,768]{1,0:T(8,128)}, u32[]{:S(2)}) copy-start(f32[16,768]{1,0:T(8,128)} %get-tuple-element.24.refs_4_.rates_ref.refs_5_.rates_s) | copy-start | bytes 147460
  82.1 20.0 %copy-start.3 = (f32[192,16,128]{2,1,0:T(8,128)S(1)}, f32[192,16,128]{2,1,0:T(8,128)}, u32[]{:S(2)}) copy-start(f32[192,16,128]{2,1,0:T(8,128)} %get-tuple-element.32.c_ref) | copy-start | bytes 4718596
  82.1 20.0 %copy-start.9 = (f32[12,16,768]{2,1,0:T(8,128)S(1)}, f32[12,16,768]{2,1,0:T(8,128)}, u32[]{:S(2)}) copy-start(f32[12,16,768]{2,1,0:T(8,128)} %get-tuple-element.31.grad_ref) | copy-start | bytes 1769476
  102.1 6.0 %copy-start.1 = (f32[8,80,128]{2,1,0:T(8,128)S(1)}, f32[8,80,128]{2,1,0:T(8,128)}, u32[]{:S(2)}) copy-start(f32[8,80,128]{2,1,0:T(8,128)} %get-tuple-element.22.refs_0_.refs_2_.refs_1_.refs_3_) | copy-start | bytes 983044
  103.8 4.3 %collective-permute-start.2 = (f32[8,72,128]{2,1,0:T(8,128)S(1)}, f32[8,72,128]{2,1,0:T(8,128)S(1)}, u32[]{:S(2)}, u32[]{:S(2)}) collective-permute-start(f32[8,72,128]{2,1,0:T(8,128)S(1)} %get-tuple-element.34), channel_id=1, source_target_pairs={{0,1},{1,0},{2,3},{3,2},{4,5},{5,4},{6,7},{7,6},{8,9},{9,8},{10,11... | collective-permute-start | bytes 884744 | tf_op jit(solution)/shard_map/ppermute | solution.py:454
  108.0 33.1 %copy-start.14 = (f32[192,768]{1,0:T(8,128)S(1)}, f32[192,768]{1,0:T(8,128)}, u32[]{:S(2)}) copy-start(f32[192,768]{1,0:T(8,128)} %get-tuple-element.41.x_ref) | copy-start | bytes 1769476
  108.1 33.0 %copy-start.13 = (f32[192,768]{1,0:T(8,128)S(1)}, f32[192,768]{1,0:T(8,128)}, u32[]{:S(2)}) copy-start(f32[192,768]{1,0:T(8,128)} %get-tuple-element.40.gated_ref) | copy-start | bytes 1769476
  123.3 17.9 %copy-start.11 = (f32[192,768]{1,0:T(8,128)S(1)}, f32[192,768]{1,0:T(8,128)}, u32[]{:S(2)}) copy-start(f32[192,768]{1,0:T(8,128)} %get-tuple-element.38.z_pre_ref) | copy-start | bytes 1769476
  123.3 17.9 %copy-start.12 = (f32[192,768]{1,0:T(8,128)S(1)}, f32[192,768]{1,0:T(8,128)}, u32[]{:S(2)}) copy-start(f32[192,768]{1,0:T(8,128)} %get-tuple-element.39.dt_pre_ref) | copy-start | bytes 1769476
  123.4 17.8 %copy-start.7 = (bf16[768,768]{1,0:T(8,128)(2,1)S(1)}, bf16[768,768]{1,0:T(8,128)(2,1)}, u32[]{:S(2)}) copy-start(bf16[768,768]{1,0:T(8,128)(2,1)} %w_out_hbm.3) | copy-start | bytes 3538948
  123.4 17.8 %copy-start.10 = (f32[192,768]{1,0:T(8,128)S(1)}, f32[192,768]{1,0:T(8,128)}, u32[]{:S(2)}) copy-start(f32[192,768]{1,0:T(8,128)} %get-tuple-element.37.x_pre_ref) | copy-start | bytes 1769476
  123.4 17.8 %copy-start.16 = (bf16[768,80]{0,1:T(8,128)(2,1)S(1)}, bf16[768,80]{0,1:T(8,128)(2,1)}, u32[]{:S(2)}) copy-start(bf16[768,80]{0,1:T(8,128)(2,1)} %param.11) | copy-start | bytes 368644
  123.4 17.8 %copy-start.17 = (bf16[48,768]{1,0:T(8,128)(2,1)S(1)}, bf16[48,768]{1,0:T(8,128)(2,1)}, u32[]{:S(2)}) copy-start(bf16[48,768]{1,0:T(8,128)(2,1)} %w_dt_hbm.3) | copy-start | bytes 221188
  123.4 17.8 %copy-start.18 = (f32[768]{0:T(1024)S(1)}, f32[768]{0:T(1024)}, u32[]{:S(2)}) copy-start(f32[768]{0:T(1024)} %d_skip_ref.1) | copy-start | bytes 9220
  137.3 3.9 %collective-permute-start.3 = (f32[8,72,128]{2,1,0:T(8,128)S(1)}, f32[8,72,128]{2,1,0:T(8,128)S(1)}, u32[]{:S(2)}, u32[]{:S(2)}) collective-permute-start(f32[8,72,128]{2,1,0:T(8,128)S(1)} %get-tuple-element.36), channel_id=1, source_target_pairs={{0,1},{1,0},{2,3},{3,2},{4,5},{5,4},{6,7},{7,6},{8,9},{9,8},{10,11... | collective-permute-start | bytes 884744 | tf_op jit(solution)/shard_map/ppermute | solution.py:474

commit v4 on v3

--- a/solution.py
+++ b/solution.py
@@ -64,20 +64,28 @@
     return lambda group: ref.at[group]
 
 
-def fetch(pairs, sems):
+def fetch(pairs, sems, now=None):
     copies = [pltpu.make_async_copy(src, dst, sems.at[k]) for k, (src, dst) in enumerate(pairs)]
-    for copy in copies:
+    for copy in copies[:now]:
         copy.start()
     return copies
 
 
 def first_kernel(
     tokens_hbm, w_in_hbm, w_xproj_hbm, w_dt_hbm, a_log_hbm, w_out_hbm, out_grad_hbm, dt_bias_ref,
+    x_pre_hbm, z_pre_hbm, dt_pre_hbm, gated_hbm, step_hbm, u_hbm, x_hbm, grad_hbm, b_hbm, c_hbm,
+    term_ref, rates_ref, own_ref, other_ref,
     x_pre_ref, z_pre_ref, dt_pre_ref, gated_ref, step_ref, u_ref, x_ref, grad_ref, b_ref, c_ref,
-    term_ref, rates_ref, own_ref, other_ref,
     tokens_ref, w_x_ref, w_z_ref, w_xproj_ref, w_dt_ref, a_log_ref, w_out_ref, out_grad_ref,
-    tok_s, og_s, end_s, sum_s, sems,
+    tok_s, og_s, end_s, sum_s, sems, out_sems,
 ):
+    leaving = []
+
+    def leave(src, dst):
+        copy = pltpu.make_async_copy(src, dst, out_sems.at[len(leaving)])
+        copy.start()
+        leaving.append(copy)
+
     copies = fetch(
         (
             (tokens_hbm, tokens_ref),
@@ -90,6 +98,7 @@
             (w_out_hbm, w_out_ref),
         ),
         sems,
+        5,
     )
     tok_s[...] = jnp.zeros_like(tok_s)
     og_s[...] = jnp.zeros_like(og_s)
@@ -98,10 +107,13 @@
         tok_s[i, 0:T, :] = tokens_ref[i]
     tok = tok_s[...].reshape(CELLS, C)
     copies[1].wait()
+    for copy in copies[5:]:
+        copy.start()
     x_pre = jnp.dot(tok, w_x_ref[...], preferred_element_type=F32)
     x_pre_ref[...] = x_pre
     x_act = (x_pre * jax.nn.sigmoid(x_pre)).astype(BF16)
     copies[2].wait()
+    leave(x_pre_ref, x_pre_hbm)
     dt_low = nt(x_act, w_xproj_ref[...])[:, 0:48].astype(BF16)
     x_dbl_t = nt(w_xproj_ref[...], x_act)
     for i in range(T):
@@ -109,6 +121,8 @@
             cell = PAD * i + j
             b_ref[cell] = jnp.broadcast_to(x_dbl_t[48:64, cell : cell + 1], (N, 128))
             c_ref[cell] = jnp.broadcast_to(x_dbl_t[64:80, cell : cell + 1], (N, 128))
+    leave(b_ref, b_hbm)
+    leave(c_ref, c_hbm)
     copies[3].wait()
     dt_pre = jnp.dot(dt_low, w_dt_ref[...], preferred_element_type=F32) + dt_bias_ref[...]
     dt_pre_ref[...] = dt_pre
@@ -117,11 +131,16 @@
     x_full = x_act.astype(F32)
     x_ref[...] = x_full
     u_ref[...] = (step * x_full).reshape(T, PAD, C)
+    leave(dt_pre_ref, dt_pre_hbm)
+    leave(step_ref, step_hbm)
+    leave(x_ref, x_hbm)
+    leave(u_ref, u_hbm)
     copies[4].wait()
     rates_ref[...] = -jnp.exp(a_log_ref[...]) * LOG2E
     copies[5].wait()
     z_pre = jnp.dot(tok, w_z_ref[...], preferred_element_type=F32)
     z_pre_ref[...] = z_pre
+    leave(z_pre_ref, z_pre_hbm)
     copies[6].wait()
     for i in range(T):
         og_s[i, 0:T, :] = out_grad_ref[i]
@@ -129,6 +148,8 @@
     gated = nt(og_s[...].reshape(CELLS, C), w_out_ref[...])
     gated_ref[...] = gated
     grad_ref[...] = (gated * (z_pre * jax.nn.sigmoid(z_pre))).reshape(T, PAD, C)
+    leave(gated_ref, gated_hbm)
+    leave(grad_ref, grad_hbm)
     term_ref[...] = jnp.zeros_like(term_ref)
 
     def one_row(back, carry):
@@ -154,6 +175,8 @@
     for ref, half in ((own_ref, core), (other_ref, 1 - core)):
         pack_half(one_half(ref), 0, end_s, half)
         pack_sums(one_half(ref), 72, sum_s, half)
+    for copy in leaving:
+        copy.wait()
 
 
 def chip_decay(core, rates_ref, part, group, t, k):
@@ -277,13 +300,29 @@
     pack_half(one_half(other_ref), 0, end_s, 1 - core)
 
 
+def put_part(part_ref, i, j, k, values):
+    rows = pl.ds(pl.multiple_of(8 * (PAD * i + j), 8), 8)
+    part_ref[k, rows, :] = values[0:8] + values[8:16]
+
+
+def add_parts(sum_ref, part_ref, i, turns=range(T)):
+    for turn in turns:
+        j, k = 8 * (turn // 6), turn % 6
+        base = 8 * (PAD * i + j)
+        total = part_ref[k, pl.ds(base, 8, stride=8), :]
+        for r in range(1, 8):
+            total = total + part_ref[k, pl.ds(base + r, 8, stride=8), :]
+        sum_ref[i, j : j + 8, LANES[k]] = total
+
+
 def last_kernel(
     keep_ref, came_ref, col_got_ref, back_keep_ref, back_came_ref, x_pre_ref, z_pre_ref, dt_pre_ref, gated_ref, step_ref,
     u_ref, x_ref, grad_ref, b_ref, c_ref, rates_s, d_skip_ref, w_in_hbm, w_xproj_hbm, w_dt_hbm,
     w_out_hbm,
     layer_hbm, token_hbm,
     w_in_ref, w_xproj_ref, w_dt_ref, w_out_ref, layer_ref, token_ref,
-    row_s, col_s, full_keep, row_keep, scan_s, step_sum_s, x_sum_s, b_part, c_part, w_dt_s, sems,
+    row_s, col_s, full_keep, row_keep, scan_s, step_sum_s, x_sum_s, b_part, c_part, part_a, part_b, w_dt_s, act_s,
+    z_part_s, dbl_s, sems,
 ):
     copies = fetch(
         (
@@ -299,10 +338,11 @@
     unpack_half(row_s, one_half(came_ref), 0, 1 - core)
     for half, chunk_of in enumerate(both_halves(col_got_ref)):
         unpack_half(col_s, chunk_of, 0, half)
-    for ref in (scan_s, step_sum_s, x_sum_s, b_part, c_part):
+    for ref in (b_part, c_part):
         ref[...] = jnp.zeros_like(ref)
 
     def down_row(i, carry):
+        before = jnp.maximum(i - 1, 0)
         row = [row_s[i, :, lanes] for lanes in LANES]
         for j in range(T):
             cell = PAD * i + j
@@ -318,27 +358,30 @@
                 col_s[j, :, lanes] = full
                 row_keep[T * i + j, :, lanes] = row_old
                 full_keep[T * i + j, :, lanes] = full_old
-                scan_s[i, j : j + 1, lanes] = jnp.sum(c * full, axis=0, keepdims=True)
+                put_part(part_a, i, j, k, c * full)
                 part = part + full * grad_ref[i, j : j + 1, lanes]
             c_part[cell] = part
+            add_parts(scan_s, part_a, before, (j,))
         return carry
 
     lax.fori_loop(0, T, down_row, 0)
-    x = x_ref[...]
-    z_pre = z_pre_ref[...]
+    add_parts(scan_s, part_a, T - 1)
     skip = d_skip_ref[...]
-    scan_out = scan_s[...].reshape(CELLS, C) + skip * x
-    z_sig = jax.nn.sigmoid(z_pre)
-    gated_out = (scan_out * (z_pre * z_sig)).astype(BF16)
+    for i in range(T):
+        rows = slice(PAD * i, PAD * i + PAD)
+        z_pre = z_pre_ref[rows, :]
+        scan_out = scan_s[i] + skip * x_ref[rows, :]
+        z_sig = jax.nn.sigmoid(z_pre)
+        act_s[rows, :] = (scan_out * (z_pre * z_sig)).astype(BF16)
+        z_part_s[rows, :] = (
+            gated_ref[rows, :] * scan_out * (z_sig * (1.0 + z_pre * (1.0 - z_sig)))
+        ).astype(BF16)
     copies[0].wait()
-    layer = jnp.dot(gated_out, w_out_ref[...], preferred_element_type=F32).astype(BF16)
+    layer = jnp.dot(act_s[...], w_out_ref[...], preferred_element_type=F32).astype(BF16)
     for i in range(T):
         layer_ref[i] = layer[PAD * i : PAD * i + T, :]
     layer_copy = pltpu.make_async_copy(layer_ref, layer_hbm, sems.at[4])
     layer_copy.start()
-    scan_s[...] = (gated_ref[...] * scan_out * (z_sig * (1.0 + z_pre * (1.0 - z_sig)))).reshape(
-        T, PAD, C
-    )
     for half, chunk_of in enumerate(both_halves(col_got_ref)):
         unpack_half(col_s, chunk_of, 72, half)
     unpack_half(row_s, one_half(back_keep_ref), 0, core)
@@ -346,6 +389,7 @@
 
     def up_row(back, carry):
         i = T - 1 - back
+        before = jnp.minimum(i + 1, T - 1)
         row = [row_s[i, :, lanes] for lanes in LANES]
         for j in reversed(range(T)):
             cell = PAD * i + j
@@ -361,48 +405,48 @@
                 decay_grad = (
                     col_adjoint * full_keep[T * i + j, :, lanes] + row_adjoint * row_keep[T * i + j, :, lanes]
                 )
-                step_sum_s[i, j : j + 1, lanes] = jnp.sum(
-                    decay_grad * rates_s[:, lanes], axis=0, keepdims=True
-                )
-                x_sum_s[i, j : j + 1, lanes] = jnp.sum(row_adjoint * b, axis=0, keepdims=True)
+                put_part(part_a, i, j, k, decay_grad * rates_s[:, lanes])
+                put_part(part_b, i, j, k, row_adjoint * b)
                 part = part + row_adjoint * u_ref[i, j : j + 1, lanes]
             b_part[cell] = part
+            add_parts(step_sum_s, part_a, before, (j,))
+            add_parts(x_sum_s, part_b, before, (j,))
         return carry
 
     lax.fori_loop(0, T, up_row, 0)
-
-    x = x_ref[...]
-    x_pre = x_pre_ref[...]
-    step = step_ref[...].reshape(CELLS, C)
-    grad = grad_ref[...].reshape(CELLS, C)
-    x_sum = x_sum_s[...].reshape(CELLS, C)
-    step_grad = step_sum_s[...].reshape(CELLS, C) * (1.0 / LOG2E) + x_sum * x
-    pre_grad = (step_grad * jax.nn.sigmoid(dt_pre_ref[...])).astype(BF16)
+    add_parts(step_sum_s, part_a, 0)
+    add_parts(x_sum_s, part_b, 0)
+
+    state = lax.broadcasted_iota(jnp.int32, (PAD * N, 80), 0) % N
+    col = lax.broadcasted_iota(jnp.int32, (PAD * N, 80), 1)
+    at_b, at_c = col == state + 48, col == state + 64
+    cell = lax.broadcasted_iota(jnp.int32, (PAD, PAD * N), 0)
+    choose = lax.broadcasted_iota(jnp.int32, (PAD, PAD * N), 1) // N == cell
+    choose = choose.astype(F32).astype(BF16)
+    for i in range(T):
+        rows = slice(PAD * i, PAD * i + PAD)
+        step_grad = step_sum_s[i] * (1.0 / LOG2E) + x_sum_s[i] * x_ref[rows, :]
+        act_s[rows, :] = (step_grad * jax.nn.sigmoid(dt_pre_ref[rows, :])).astype(BF16)
+        b_sum = jnp.sum(b_part[rows].reshape(PAD * N, 128), axis=1, keepdims=True)
+        c_sum = jnp.sum(c_part[rows].reshape(PAD * N, 128), axis=1, keepdims=True)
+        placed = jnp.where(at_b, b_sum, jnp.where(at_c, c_sum, 0.0)).astype(BF16)
+        dbl_s[rows, :] = jnp.dot(choose, placed, preferred_element_type=F32)
     copies[1].wait()
     w_dt_s[...] = jnp.zeros_like(w_dt_s)
     w_dt_s[0:48, :] = w_dt_ref[...]
-    low = nt(pre_grad, w_dt_s[...])
-    rows = lax.broadcasted_iota(jnp.int32, (CELLS * N, 80), 0)
-    cols = lax.broadcasted_iota(jnp.int32, (CELLS * N, 80), 1)
-    state = rows % N
-    b_sum = jnp.sum(b_part[...].reshape(CELLS * N, 128), axis=1, keepdims=True)
-    c_sum = jnp.sum(c_part[...].reshape(CELLS * N, 128), axis=1, keepdims=True)
-    placed = jnp.where(cols == state + 48, b_sum, jnp.where(cols == state + 64, c_sum, 0.0))
-    owner = lax.broadcasted_iota(jnp.int32, (CELLS, CELLS * N), 1) // N
-    cell = lax.broadcasted_iota(jnp.int32, (CELLS, CELLS * N), 0)
-    choose = (owner == cell).astype(F32).astype(BF16)
-    dbl = (low + jnp.dot(choose, placed.astype(BF16), preferred_element_type=F32)).astype(BF16)
+    dbl = (nt(act_s[...], w_dt_s[...]) + dbl_s[...]).astype(BF16)
     copies[2].wait()
-    x_grad = (
-        x_sum * step
-        + grad * d_skip_ref[...]
-        + jnp.dot(dbl, w_xproj_ref[...], preferred_element_type=F32)
-    )
-    x_sig = jax.nn.sigmoid(x_pre)
-    x_part = (x_grad * (x_sig * (1.0 + x_pre * (1.0 - x_sig)))).astype(BF16)
-    z_part = scan_s[...].reshape(CELLS, C).astype(BF16)
+    step_sum_s[...] = jnp.dot(dbl, w_xproj_ref[...], preferred_element_type=F32).reshape(T, PAD, C)
+    for i in range(T):
+        rows = slice(PAD * i, PAD * i + PAD)
+        x_pre = x_pre_ref[rows, :]
+        x_grad = x_sum_s[i] * step_ref[i] + grad_ref[i] * skip + step_sum_s[i]
+        x_sig = jax.nn.sigmoid(x_pre)
+        act_s[rows, :] = (x_grad * (x_sig * (1.0 + x_pre * (1.0 - x_sig)))).astype(BF16)
     copies[3].wait()
-    token = (nt(x_part, w_in_ref[:, 0:C]) + nt(z_part, w_in_ref[:, C : 2 * C])).astype(BF16)
+    token = (nt(act_s[...], w_in_ref[:, 0:C]) + nt(z_part_s[...], w_in_ref[:, C : 2 * C])).astype(
+        BF16
+    )
     for i in range(T):
         token_ref[i] = token[PAD * i : PAD * i + T, :]
     token_copy = pltpu.make_async_copy(token_ref, token_hbm, sems.at[5])
@@ -415,13 +459,15 @@
 IN_HBM = pl.BlockSpec(memory_space=pltpu.HBM)
 
 
-def call(kernel, out_shape, scratch, name, limit, *args, fetched=(), out_spec=IN_VMEM):
+def call(kernel, out_shape, scratch, name, limit, *args, fetched=(), sent=()):
     many = isinstance(out_shape, tuple)
     return pl.pallas_call(
         kernel,
         out_shape=out_shape,
         in_specs=[IN_HBM if k in fetched else IN_VMEM for k in range(len(args))],
-        out_specs=tuple(out_spec for _ in out_shape) if many else out_spec,
+        out_specs=tuple(IN_HBM if k in sent else IN_VMEM for k in range(len(out_shape)))
+        if many
+        else IN_VMEM,
         scratch_shapes=scratch,
         name=name,
         compiler_params=pltpu.CompilerParams(vmem_limit_bytes=limit * 1024 * 1024),
@@ -475,12 +521,12 @@
 
 
 def body(tokens, w_in, w_xproj, w_dt, dt_bias, a_log, d_skip, w_out, out_grad):
-    edge, wide = vmem(T, N, C), vmem(T, PAD, C)
+    edge, wide, dense = vmem(T, N, C), vmem(T, PAD, C), vmem(CELLS, C)
     flat, grid, spread = f32(CELLS, C), f32(T, PAD, C), f32(CELLS, N, 128)
-    kept, sums = vmem(T * T, N, C), vmem(PAD, C)
+    kept, sums, parts = vmem(T * T, N, C), vmem(PAD, C), vmem(C // 128, 8 * CELLS, 128)
     padded, cells = pltpu.VMEM((T, PAD, C), BF16), pltpu.VMEM((T, T, C), BF16)
     square, narrow = pltpu.VMEM((C, C), BF16), pltpu.VMEM((80, C), BF16)
-    low_rank = pltpu.VMEM((48, C), BF16)
+    low_rank, half_width = pltpu.VMEM((48, C), BF16), pltpu.VMEM((CELLS, C), BF16)
     w_xproj = w_xproj.T
     x_pre, z_pre, dt_pre, gated, step, u, x, grad, b, c, term, rates, own, other = call(
         first_kernel,
@@ -489,12 +535,14 @@
             f32(N, C), f32(8, 80, 128), f32(8, 80, 128),
         ),
         (
-            cells, square, square, narrow, low_rank, vmem(N, C), square, cells,
+            dense, dense, dense, dense, wide, wide, dense, wide, vmem(CELLS, N, 128),
+            vmem(CELLS, N, 128), cells, square, square, narrow, low_rank, vmem(N, C), square, cells,
             padded, padded, edge, sums, pltpu.SemaphoreType.DMA((8,)),
+            pltpu.SemaphoreType.DMA((10,)),
         ),
         "first", 54,
         tokens, w_in, w_xproj, w_dt, a_log, w_out, out_grad, dt_bias,
-        fetched=range(7),
+        fetched=range(7), sent=range(10),
     )
     keep, came, chip_sums = row_scan(own, other, None, rates, False)
     col_sent = call(
@@ -517,13 +565,14 @@
         (out, out),
         (
             pltpu.VMEM((C, 2 * C), BF16), narrow, low_rank, square, cells, cells,
-            edge, edge, kept, kept, wide, wide, wide,
-            vmem(CELLS, N, 128), vmem(CELLS, N, 128), narrow, pltpu.SemaphoreType.DMA((6,)),
+            edge, edge, kept, kept, wide, wide, wide, vmem(CELLS, N, 128),
+            vmem(CELLS, N, 128), parts, parts, narrow, half_width, half_width, vmem(CELLS, 80),
+            pltpu.SemaphoreType.DMA((6,)),
         ),
         "last", 42,
         keep, came, col_got, back_keep, back_came, x_pre, z_pre, dt_pre, gated, step, u, x, grad, b, c, rates,
         d_skip, w_in, w_xproj, w_dt, w_out,
-        fetched=range(17, 21), out_spec=IN_HBM,
+        fetched=range(17, 21), sent=range(2),
     )
 
 

time: 156 us -> 152 us (0.974)
  Pallas kernels: 29.2 us -> 25.8 us
    pallas_call x11, Pallas kernels: 29.2 us -> 25.8 us  [call(): pl.pallas_call(kernel, out_shape=out_shape, in_specs=[IN_HBM if k in fetc...]
where the time goes in v4:
time: 152 us; the launch traced here: 151 us
  blocking collectives  106 us (70%)
  Pallas kernels  25.8 us (17%)
  starting transfers between devices  11.9 us (8%)
  waiting for transfers between devices  5.09 us (3%)
  local copies, waits for them, and re-layouts  1.85 us (1%)
    all_to_all x6, blocking collectives, swap(): lax.all_to_all(sent, axis, 0, 0, tiled=True, axis_index_groups=groups)  106 us
    pallas_call x11, Pallas kernels, call(): pl.pallas_call(kernel, out_shape=out_shape, in_specs=[IN_HBM if k in fetc...  25.8 us
    ppermute x2, starting transfers between devices, row_scan(): got = lax.ppermute(other, 'col', partner)  6.35 us
    ppermute x2, starting transfers between devices, row_scan(): return (keep, lax.ppermute(send, 'col', partner), (*sums[:2], chip_sums))  5.59 us
  transfers between devices with their start and end apart: 4, of which 4 were waited for; matrix products, arithmetic and copies ran while one was open for 0% of the time, Pallas kernels for 0%

profile of v4, /device:TPU:1, one launch (start us, length us, event | category | flops | bytes accessed | tf_op | source)
XLA Modules:
  0.0 151.4 jit_solution(10270544888093184425)
XLA Ops:
  0.6 8.8 %first.1 = (f32[192,768]{1,0:T(8,128)}, f32[192,768]{1,0:T(8,128)}, f32[192,768]{1,0:T(8,128)}, f32[192,768]{1,0:T(8,128)}, f32[12,16,768]{2,1,0:T(8,128)}, /*in...) custom-call(bf16[12,12,768]{2,1,0:T(8,128)(2,1)} %tokens_hbm.1, ...), custom_call_target="tpu_custom_call" | custom-call | tf_op jit(solution)/shard_map/first/pallas_call | solution.py:464
  9.4 3.3 %collective-permute-start = (f32[8,80,128]{2,1,0:T(8,128)}, f32[8,80,128]{2,1,0:T(8,128)S(1)}, u32[]{:S(2)}, u32[]{:S(2)}) collective-permute-start(f32[8,80,128]{2,1,0:T(8,128)} %get-tuple-element.23), channel_id=1, source_target_pairs={{0,1},{1,0},{2,3},{3,2},{4,5},{5,4},{6,7},{7,6},{8,9},{9,8},{10,11... | collective-permute-start | bytes 983048 | tf_op jit(solution)/shard_map/ppermute | solution.py:500
  12.7 1.5 collective-permute-done.refs_1_.refs_3_.refs_2_.refs_4_
  14.2 1.0 copy-done
  15.2 0.8 copy-done.5
  16.0 0.1 combine.2
  16.1 0.0 copy-start.15
  16.1 19.2 %all_to_all.30.got_ref.sums_ref = f32[8,80,128]{2,1,0:T(8,128)S(1)} all-to-all(f32[8,80,128]{2,1,0:T(8,128)S(1)} %combine.2), channel_id=1, replica_groups={{0,2,4,6,8,10,12,14},{1,3,5,7,9,11,13,15},{16,18,20,22,24,26,28,30},{17..., dimensions={0} | all-to-all | bytes 655360 | tf_op jit(solution)/shard_map/all_to_all | solution.py:494
  35.3 0.1 prefix_col.2
  35.3 0.0 copy-start.2
  35.4 0.0 copy-start.4
  35.4 13.0 %all_to_all.31.refs_0_ = f32[8,72,128]{2,1,0:T(8,128)S(1)} all-to-all(f32[8,72,128]{2,1,0:T(8,128)S(1)} %prefix_col.2), channel_id=1, replica_groups={{0,2,4,6,8,10,12,14},{1,3,5,7,9,11,13,15},{16,18,20,22,24,26,28,30},{17..., dimensions={0} | all-to-all | bytes 589824 | tf_op jit(solution)/shard_map/all_to_all | solution.py:494
  48.4 0.1 split.2
  48.5 3.1 %collective-permute-start.1 = (f32[8,72,128]{2,1,0:T(8,128)S(1)}, f32[8,72,128]{2,1,0:T(8,128)S(1)}, u32[]{:S(2)}, u32[]{:S(2)}) collective-permute-start(f32[8,72,128]{2,1,0:T(8,128)S(1)} %get-tuple-element.26), channel_id=1, source_target_pairs={{0,1},{1,0},{2,3},{3,2},{4,5},{5,4},{6,7},{7,6},{8,9},{9,8},{10,11... | collective-permute-start | bytes 884744 | tf_op jit(solution)/shard_map/ppermute | solution.py:520
  51.6 1.2 collective-permute-done.1.came_ref
  52.8 0.0 copy-done.15
  52.8 0.0 copy-done.8
  52.8 0.0 copy-done.2
  52.8 0.0 copy-done.4
  52.8 2.0 %forward.1 = f32[16,152,128]{2,1,0:T(8,128)S(1)} custom-call(f32[8,72,128]{2,1,0:T(8,128)S(1)} %get-tuple-element.25.keep_ref, f32[8,72,128]{2,1,0:T(8,128)S(1)} %collective-permute-done.1.came_ref, f32[16,768]{1,0:T(8,128)S(1)} %copy-done.5, f32[12,16,768]{2,1,0:T(8,128)S(1)} %copy-done.4, f32[12,16,768]{2,1,0:T(8,128)S(1)} %copy-done.8, ...), custom_call_target="tpu_custom_call" | custom-call | tf_op jit(solution)/shard_map/forward/pallas_call | solution.py:464
  54.8 0.0 copy-start.6
  54.8 24.8 %all_to_all.32.got_ref.sums_ref = f32[16,152,128]{2,1,0:T(8,128)S(1)} all-to-all(f32[16,152,128]{2,1,0:T(8,128)S(1)} %forward.1), channel_id=1, replica_groups=mesh['row'=16,'col'=16] {'row'}, dimensions={0} | all-to-all | bytes 2490368 | tf_op jit(solution)/shard_map/all_to_all | solution.py:494
  79.6 0.0 copy-done.6
  79.6 0.2 prefix_row.1
  79.8 0.0 copy-start.3
  79.8 0.0 copy-start.9
  79.8 20.0 %all_to_all.33.col_got_ref = f32[16,144,128]{2,1,0:T(8,128)S(1)} all-to-all(f32[16,144,128]{2,1,0:T(8,128)S(1)} %prefix_row.1), channel_id=1, replica_groups=mesh['row'=16,'col'=16] {'row'}, dimensions={0} | all-to-all | bytes 2359296 | tf_op jit(solution)/shard_map/all_to_all | solution.py:494
  99.8 0.0 copy-done.3
  99.8 0.0 copy-done.9
  99.8 1.7 %backward.1 = (f32[8,72,128]{2,1,0:T(8,128)S(1)}, f32[8,72,128]{2,1,0:T(8,128)S(1)}) custom-call(f32[16,144,128]{2,1,0:T(8,128)S(1)} %all_to_all.33.col_got_ref, f32[16,768]{1,0:T(8,128)S(1)} %copy-done.6, f32[12,16,768]{2,1,0:T(8,128)S(1)} %copy-done.4, f32[12,16,768]{2,1,0:T(8,128)S(1)} %copy-done.9, f32[192,16,128]{2,1,0:T(8,128)S(1)} %copy-done.3), custom_call_target="tpu_custom_call" | custom-call | tf_op jit(solution)/shard_map/backward/pallas_call | solution.py:464
  101.5 3.1 %collective-permute-start.2 = (f32[8,72,128]{2,1,0:T(8,128)S(1)}, f32[8,72,128]{2,1,0:T(8,128)S(1)}, u32[]{:S(2)}, u32[]{:S(2)}) collective-permute-start(f32[8,72,128]{2,1,0:T(8,128)S(1)} %get-tuple-element.34), channel_id=1, source_target_pairs={{0,1},{1,0},{2,3},{3,2},{4,5},{5,4},{6,7},{7,6},{8,9},{9,8},{10,11... | collective-permute-start | bytes 884744 | tf_op jit(solution)/shard_map/ppermute | solution.py:500
  104.6 1.2 collective-permute-done.2.refs_1_.refs_2_
  105.8 0.0 copy-done.1
  105.8 0.1 combine.3
  105.9 0.0 copy-start.13
  105.9 15.1 %all_to_all.34.got_ref = f32[8,72,128]{2,1,0:T(8,128)S(1)} all-to-all(f32[8,72,128]{2,1,0:T(8,128)S(1)} %combine.3), channel_id=1, replica_groups={{0,2,4,6,8,10,12,14},{1,3,5,7,9,11,13,15},{16,18,20,22,24,26,28,30},{17..., dimensions={0} | all-to-all | bytes 589824 | tf_op jit(solution)/shard_map/all_to_all | solution.py:494
  121.0 0.1 prefix_col.3
  121.1 0.0 copy-start.7
  121.1 0.0 copy-start.10
  121.1 0.0 copy-start.16
  121.2 0.0 copy-start.17
  121.2 0.0 copy-start.18
  121.2 13.7 %all_to_all.35.refs_0_ = f32[8,72,128]{2,1,0:T(8,128)S(1)} all-to-all(f32[8,72,128]{2,1,0:T(8,128)S(1)} %prefix_col.3), channel_id=1, replica_groups={{0,2,4,6,8,10,12,14},{1,3,5,7,9,11,13,15},{16,18,20,22,24,26,28,30},{17..., dimensions={0} | all-to-all | bytes 589824 | tf_op jit(solution)/shard_map/all_to_all | solution.py:494
  134.9 0.1 split.3
  135.0 2.5 %collective-permute-start.3 = (f32[8,72,128]{2,1,0:T(8,128)S(1)}, f32[8,72,128]{2,1,0:T(8,128)S(1)}, u32[]{:S(2)}, u32[]{:S(2)}) collective-permute-start(f32[8,72,128]{2,1,0:T(8,128)S(1)} %get-tuple-element.36), channel_id=1, source_target_pairs={{0,1},{1,0},{2,3},{3,2},{4,5},{5,4},{6,7},{7,6},{8,9},{9,8},{10,11... | collective-permute-start | bytes 884744 | tf_op jit(solution)/shard_map/ppermute | solution.py:520
  137.5 1.2 collective-permute-done.3.back_came_ref
  138.7 0.0 copy-done.14
  138.8 12.6 %last.1 = (bf16[12,12,768]{2,1,0:T(8,128)(2,1)}, bf16[12,12,768]{2,1,0:T(8,128)(2,1)}) custom-call(f32[8,72,128]{2,1,0:T(8,128)S(1)} %get-tuple-element.25.keep_ref, f32[8,72,128]{2,1,0:T(8,128)S(1)} %collective-permute-done.1.came_ref, f32[16,144,128]{2,1,0:T(8,128)S(1)} %all_to_all.33.col_got_ref, f32[8,72,128]{2,1,0:T(8,128)S(1)} %get-tuple-element.35.back_keep_ref, ...), custom_call_target="tpu_custom_call" | custom-call | tf_op jit(solution)/shard_map/last/pallas_call | solution.py:464
  (15 shorter events, 0.0 us)
Async XLA Ops:
  9.4 4.8 %collective-permute-start = (f32[8,80,128]{2,1,0:T(8,128)}, f32[8,80,128]{2,1,0:T(8,128)S(1)}, u32[]{:S(2)}, u32[]{:S(2)}) collective-permute-start(f32[8,80,128]{2,1,0:T(8,128)} %get-tuple-element.23), channel_id=1, source_target_pairs={{0,1},{1,0},{2,3},{3,2},{4,5},{5,4},{6,7},{7,6},{8,9},{9,8},{10,11... | collective-permute-start | bytes 983048 | tf_op jit(solution)/shard_map/ppermute | solution.py:500
  14.2 1.0 copy-start
  15.2 0.8 copy-start.5
  16.1 36.7 %copy-start.15 = (f32[12,16,768]{2,1,0:T(8,128)S(1)}, f32[12,16,768]{2,1,0:T(8,128)}, u32[]{:S(2)}) copy-start(f32[12,16,768]{2,1,0:T(8,128)} %get-tuple-element.30.term_ref) | copy-start | bytes 1769476
  35.3 17.5 %copy-start.8 = (f32[12,16,768]{2,1,0:T(8,128)S(1)}, f32[12,16,768]{2,1,0:T(8,128)}, u32[]{:S(2)}) copy-start(f32[12,16,768]{2,1,0:T(8,128)} %get-tuple-element.28.u_ref) | copy-start | bytes 1769476
  35.3 17.5 %copy-start.2 = (f32[192,16,128]{2,1,0:T(8,128)S(1)}, f32[192,16,128]{2,1,0:T(8,128)}, u32[]{:S(2)}) copy-start(f32[192,16,128]{2,1,0:T(8,128)} %get-tuple-element.29.b_ref) | copy-start | bytes 4718596
  35.4 17.4 %copy-start.4 = (f32[12,16,768]{2,1,0:T(8,128)S(1)}, f32[12,16,768]{2,1,0:T(8,128)}, u32[]{:S(2)}) copy-start(f32[12,16,768]{2,1,0:T(8,128)} %get-tuple-element.27.step_ref) | copy-start | bytes 1769476
  48.5 4.3 %collective-permute-start.1 = (f32[8,72,128]{2,1,0:T(8,128)S(1)}, f32[8,72,128]{2,1,0:T(8,128)S(1)}, u32[]{:S(2)}, u32[]{:S(2)}) collective-permute-start(f32[8,72,128]{2,1,0:T(8,128)S(1)} %get-tuple-element.26), channel_id=1, source_target_pairs={{0,1},{1,0},{2,3},{3,2},{4,5},{5,4},{6,7},{7,6},{8,9},{9,8},{10,11... | collective-permute-start | bytes 884744 | tf_op jit(solution)/shard_map/ppermute | solution.py:520
  54.8 24.8 %copy-start.6 = (f32[16,768]{1,0:T(8,128)S(1)}, f32[16,768]{1,0:T(8,128)}, u32[]{:S(2)}) copy-start(f32[16,768]{1,0:T(8,128)} %get-tuple-element.24.refs_4_.rates_ref.refs_5_.rates_s) | copy-start | bytes 147460
  79.8 20.0 %copy-start.3 = (f32[192,16,128]{2,1,0:T(8,128)S(1)}, f32[192,16,128]{2,1,0:T(8,128)}, u32[]{:S(2)}) copy-start(f32[192,16,128]{2,1,0:T(8,128)} %get-tuple-element.32.c_ref) | copy-start | bytes 4718596
  79.8 20.0 %copy-start.9 = (f32[12,16,768]{2,1,0:T(8,128)S(1)}, f32[12,16,768]{2,1,0:T(8,128)}, u32[]{:S(2)}) copy-start(f32[12,16,768]{2,1,0:T(8,128)} %get-tuple-element.31.grad_ref) | copy-start | bytes 1769476
  99.8 6.0 %copy-start.1 = (f32[8,80,128]{2,1,0:T(8,128)S(1)}, f32[8,80,128]{2,1,0:T(8,128)}, u32[]{:S(2)}) copy-start(f32[8,80,128]{2,1,0:T(8,128)} %get-tuple-element.22.refs_0_.refs_2_.refs_1_.refs_3_) | copy-start | bytes 983044
  101.5 4.3 %collective-permute-start.2 = (f32[8,72,128]{2,1,0:T(8,128)S(1)}, f32[8,72,128]{2,1,0:T(8,128)S(1)}, u32[]{:S(2)}, u32[]{:S(2)}) collective-permute-start(f32[8,72,128]{2,1,0:T(8,128)S(1)} %get-tuple-element.34), channel_id=1, source_target_pairs={{0,1},{1,0},{2,3},{3,2},{4,5},{5,4},{6,7},{7,6},{8,9},{9,8},{10,11... | collective-permute-start | bytes 884744 | tf_op jit(solution)/shard_map/ppermute | solution.py:500
  105.8 33.0 %copy-start.14 = (f32[192,768]{1,0:T(8,128)S(1)}, f32[192,768]{1,0:T(8,128)}, u32[]{:S(2)}) copy-start(f32[192,768]{1,0:T(8,128)} %get-tuple-element.41.x_ref) | copy-start | bytes 1769476
  105.9 32.9 %copy-start.13 = (f32[192,768]{1,0:T(8,128)S(1)}, f32[192,768]{1,0:T(8,128)}, u32[]{:S(2)}) copy-start(f32[192,768]{1,0:T(8,128)} %get-tuple-element.40.gated_ref) | copy-start | bytes 1769476
  121.0 17.7 %copy-start.11 = (f32[192,768]{1,0:T(8,128)S(1)}, f32[192,768]{1,0:T(8,128)}, u32[]{:S(2)}) copy-start(f32[192,768]{1,0:T(8,128)} %get-tuple-element.38.z_pre_ref) | copy-start | bytes 1769476
  121.0 17.7 %copy-start.12 = (f32[192,768]{1,0:T(8,128)S(1)}, f32[192,768]{1,0:T(8,128)}, u32[]{:S(2)}) copy-start(f32[192,768]{1,0:T(8,128)} %get-tuple-element.39.dt_pre_ref) | copy-start | bytes 1769476
  121.1 17.6 %copy-start.7 = (bf16[768,768]{1,0:T(8,128)(2,1)S(1)}, bf16[768,768]{1,0:T(8,128)(2,1)}, u32[]{:S(2)}) copy-start(bf16[768,768]{1,0:T(8,128)(2,1)} %w_out_hbm.3) | copy-start | bytes 3538948
  121.1 17.6 %copy-start.10 = (f32[192,768]{1,0:T(8,128)S(1)}, f32[192,768]{1,0:T(8,128)}, u32[]{:S(2)}) copy-start(f32[192,768]{1,0:T(8,128)} %get-tuple-element.37.x_pre_ref) | copy-start | bytes 1769476
  121.1 17.6 %copy-start.16 = (bf16[768,80]{0,1:T(8,128)(2,1)S(1)}, bf16[768,80]{0,1:T(8,128)(2,1)}, u32[]{:S(2)}) copy-start(bf16[768,80]{0,1:T(8,128)(2,1)} %param.11) | copy-start | bytes 368644
  121.2 17.6 %copy-start.17 = (bf16[48,768]{1,0:T(8,128)(2,1)S(1)}, bf16[48,768]{1,0:T(8,128)(2,1)}, u32[]{:S(2)}) copy-start(bf16[48,768]{1,0:T(8,128)(2,1)} %w_dt_hbm.3) | copy-start | bytes 221188
  121.2 17.6 %copy-start.18 = (f32[768]{0:T(1024)S(1)}, f32[768]{0:T(1024)}, u32[]{:S(2)}) copy-start(f32[768]{0:T(1024)} %d_skip_ref.1) | copy-start | bytes 9220
  135.0 3.7 %collective-permute-start.3 = (f32[8,72,128]{2,1,0:T(8,128)S(1)}, f32[8,72,128]{2,1,0:T(8,128)S(1)}, u32[]{:S(2)}, u32[]{:S(2)}) collective-permute-start(f32[8,72,128]{2,1,0:T(8,128)S(1)} %get-tuple-element.36), channel_id=1, source_target_pairs={{0,1},{1,0},{2,3},{3,2},{4,5},{5,4},{6,7},{7,6},{8,9},{9,8},{10,11... | collective-permute-start | bytes 884744 | tf_op jit(solution)/shard_map/ppermute | solution.py:520

commit v5 on v4

--- a/solution.py
+++ b/solution.py
@@ -74,10 +74,10 @@
 def first_kernel(
     tokens_hbm, w_in_hbm, w_xproj_hbm, w_dt_hbm, a_log_hbm, w_out_hbm, out_grad_hbm, dt_bias_ref,
     x_pre_hbm, z_pre_hbm, dt_pre_hbm, gated_hbm, step_hbm, u_hbm, x_hbm, grad_hbm, b_hbm, c_hbm,
-    term_ref, rates_ref, own_ref, other_ref,
+    term_hbm, rates_hbm, own_hbm, other_hbm,
     x_pre_ref, z_pre_ref, dt_pre_ref, gated_ref, step_ref, u_ref, x_ref, grad_ref, b_ref, c_ref,
     tokens_ref, w_x_ref, w_z_ref, w_xproj_ref, w_dt_ref, a_log_ref, w_out_ref, out_grad_ref,
-    tok_s, og_s, end_s, sum_s, sems, out_sems,
+    tok_s, og_s, end_s, sum_s, term_ref, rates_ref, own_ref, other_ref, sems, out_sems,
 ):
     leaving = []
 
@@ -137,6 +137,7 @@
     leave(u_ref, u_hbm)
     copies[4].wait()
     rates_ref[...] = -jnp.exp(a_log_ref[...]) * LOG2E
+    leave(rates_ref, rates_hbm)
     copies[5].wait()
     z_pre = jnp.dot(tok, w_z_ref[...], preferred_element_type=F32)
     z_pre_ref[...] = z_pre
@@ -169,12 +170,14 @@
         return carry
 
     lax.fori_loop(0, T, one_row, 0)
+    leave(term_ref, term_hbm)
     for i in range(T):
         sum_s[i : i + 1, :] = jnp.sum(step_ref[i, 0:T, :], axis=0, keepdims=True)
     core = lax.axis_index("col") % 2
-    for ref, half in ((own_ref, core), (other_ref, 1 - core)):
+    for ref, out, half in ((other_ref, other_hbm, 1 - core), (own_ref, own_hbm, core)):
         pack_half(one_half(ref), 0, end_s, half)
         pack_sums(one_half(ref), 72, sum_s, half)
+        leave(ref, out)
     for copy in leaving:
         copy.wait()
 
@@ -220,6 +223,11 @@
                 )
                 keep_ref[group, rows, :] = jnp.where(own_first, state, through)
                 send_ref[group, rows, :] = jnp.where(own_first, through, state)
+
+
+def stage_kernel(own_ref, rates_ref, own_out, rates_out):
+    own_out[...] = own_ref[...]
+    rates_out[...] = rates_ref[...]
 
 
 def prefix_kernel(axis, spans, sum_base, got_ref, sums_ref, rates_ref, out_ref):
@@ -494,10 +502,9 @@
     return lax.all_to_all(sent, axis, 0, 0, tiled=True, axis_index_groups=groups)
 
 
-def row_scan(own, other, sums, rates, reverse):
+def row_scan(own, got, sums, rates, reverse):
     partner = [(place, place ^ 1) for place in range(16)]
     same_core = [[2 * chip + core for chip in range(8)] for core in range(2)]
-    got = lax.ppermute(other, "col", partner)
     if sums is None:
         sums = (own, got)
 
@@ -526,8 +533,10 @@
     kept, sums, parts = vmem(T * T, N, C), vmem(PAD, C), vmem(C // 128, 8 * CELLS, 128)
     padded, cells = pltpu.VMEM((T, PAD, C), BF16), pltpu.VMEM((T, T, C), BF16)
     square, narrow = pltpu.VMEM((C, C), BF16), pltpu.VMEM((80, C), BF16)
+    halves = vmem(8, 80, 128)
     low_rank, half_width = pltpu.VMEM((48, C), BF16), pltpu.VMEM((CELLS, C), BF16)
     w_xproj = w_xproj.T
+    partner = [(place, place ^ 1) for place in range(16)]
     x_pre, z_pre, dt_pre, gated, step, u, x, grad, b, c, term, rates, own, other = call(
         first_kernel,
         (
@@ -537,14 +546,18 @@
         (
             dense, dense, dense, dense, wide, wide, dense, wide, vmem(CELLS, N, 128),
             vmem(CELLS, N, 128), cells, square, square, narrow, low_rank, vmem(N, C), square, cells,
-            padded, padded, edge, sums, pltpu.SemaphoreType.DMA((8,)),
-            pltpu.SemaphoreType.DMA((10,)),
+            padded, padded, edge, sums, edge, vmem(N, C), halves, halves,
+            pltpu.SemaphoreType.DMA((8,)), pltpu.SemaphoreType.DMA((14,)),
         ),
         "first", 54,
         tokens, w_in, w_xproj, w_dt, a_log, w_out, out_grad, dt_bias,
-        fetched=range(7), sent=range(10),
-    )
-    keep, came, chip_sums = row_scan(own, other, None, rates, False)
+        fetched=range(7), sent=range(14),
+    )
+    got = lax.ppermute(other, "col", partner)
+    own, rates = call(
+        stage_kernel, (f32(8, 80, 128), f32(N, C)), (), "stage", 4, own, rates
+    )
+    keep, came, chip_sums = row_scan(own, got, None, rates, False)
     col_sent = call(
         forward_kernel, f32(16, 152, 128), (edge, edge, sums), "forward", 6,
         keep, came, rates, step, u, b, term,
@@ -558,7 +571,8 @@
         backward_kernel, (back_half, back_half), (edge, edge), "backward", 6,
         col_got, rates, step, grad, c,
     )
-    back_keep, back_came, chip_sums = row_scan(back_own, back_other, chip_sums, rates, True)
+    back_got = lax.ppermute(back_other, "col", partner)
+    back_keep, back_came, chip_sums = row_scan(back_own, back_got, chip_sums, rates, True)
     out = jax.ShapeDtypeStruct((T, T, C), BF16)
     return call(
         last_kernel,

time: 152 us -> 151 us (level)
  blocking collectives: 106 us -> 109 us
  starting transfers between devices: 11.9 us -> 9.71 us
    all_to_all x6, blocking collectives: 106 us -> 109 us  [swap(): lax.all_to_all(sent, axis, 0, 0, tiled=True, axis_index_groups=groups)]
    ppermute x2, starting transfers between devices: 5.59 us -> 3.37 us  [row_scan(): return (keep, lax.ppermute(send, 'col', partner), (*sums[:2], chip_sums))]
    pallas_call x11 -> x12, Pallas kernels: 25.8 us -> 25.7 us  [call(): pl.pallas_call(kernel, out_shape=out_shape, in_specs=[IN_HBM if k in fetc...]
  transfers between devices with their start and end apart: 4 -> 4, of which waited for: 4 -> 3; matrix products, arithmetic and copies ran while one was open for 0% -> 0% of each run, Pallas kernels for 0% -> 0%
where the time goes in v5:
time: 151 us
  blocking collectives  109 us (72%)
  Pallas kernels  25.7 us (17%)
  starting transfers between devices  9.71 us (6%)
  waiting for transfers between devices  3.63 us (2%)
  local copies, waits for them, and re-layouts  1.84 us (1%)
    all_to_all x6, blocking collectives, swap(): lax.all_to_all(sent, axis, 0, 0, tiled=True, axis_index_groups=groups)  109 us
    pallas_call x12, Pallas kernels, call(): pl.pallas_call(kernel, out_shape=out_shape, in_specs=[IN_HBM if k in fetc...  25.7 us
    ppermute x2, starting transfers between devices, row_scan(): return (keep, lax.ppermute(send, 'col', partner), (*sums[:2], chip_sums))  3.37 us
    ppermute x1, starting transfers between devices, body(): got = lax.ppermute(other, 'col', partner)  3.29 us
    ppermute x1, starting transfers between devices, body(): back_got = lax.ppermute(back_other, 'col', partner)  3.06 us
  transfers between devices with their start and end apart: 4, of which 3 were waited for; matrix products, arithmetic and copies ran while one was open for 0% of the time, Pallas kernels for 0%

profile of v5, /device:TPU:1, one launch (start us, length us, event | category | flops | bytes accessed | tf_op | source)
XLA Modules:
  0.0 150.7 jit_solution(7246994526501450715)
XLA Ops:
  0.6 8.7 %first.1 = (f32[192,768]{1,0:T(8,128)}, f32[192,768]{1,0:T(8,128)}, f32[192,768]{1,0:T(8,128)}, f32[192,768]{1,0:T(8,128)}, f32[12,16,768]{2,1,0:T(8,128)}, /*in...) custom-call(bf16[12,12,768]{2,1,0:T(8,128)(2,1)} %tokens_hbm.1, ...), custom_call_target="tpu_custom_call" | custom-call | tf_op jit(solution)/shard_map/first/pallas_call | solution.py:472
  9.3 3.3 %collective-permute-start = (f32[8,80,128]{2,1,0:T(8,128)}, f32[8,80,128]{2,1,0:T(8,128)S(1)}, u32[]{:S(2)}, u32[]{:S(2)}) collective-permute-start(f32[8,80,128]{2,1,0:T(8,128)} %get-tuple-element.27), channel_id=1, source_target_pairs={{0,1},{1,0},{2,3},{3,2},{4,5},{5,4},{6,7},{7,6},{8,9},{9,8},{10,11... | collective-permute-start | bytes 983048 | tf_op jit(solution)/shard_map/ppermute | solution.py:556
  12.6 1.0 copy-done.13
  13.6 0.8 copy-done.15
  14.4 0.0 collective-permute-done.refs_1_.refs_3_.refs_2_.refs_4_
  14.4 0.1 combine.2
  14.5 0.0 copy-start.11
  14.5 20.2 %all_to_all.30.got_ref.sums_ref = f32[8,80,128]{2,1,0:T(8,128)S(1)} all-to-all(f32[8,80,128]{2,1,0:T(8,128)S(1)} %combine.2), channel_id=1, replica_groups={{0,2,4,6,8,10,12,14},{1,3,5,7,9,11,13,15},{16,18,20,22,24,26,28,30},{17..., dimensions={0} | all-to-all | bytes 655360 | tf_op jit(solution)/shard_map/all_to_all | solution.py:502
  34.7 0.1 prefix_col.2
  34.8 0.0 copy-start
  34.8 0.0 copy-start.2
  34.8 15.3 %all_to_all.31.refs_0_ = f32[8,72,128]{2,1,0:T(8,128)S(1)} all-to-all(f32[8,72,128]{2,1,0:T(8,128)S(1)} %prefix_col.2), channel_id=1, replica_groups={{0,2,4,6,8,10,12,14},{1,3,5,7,9,11,13,15},{16,18,20,22,24,26,28,30},{17..., dimensions={0} | all-to-all | bytes 589824 | tf_op jit(solution)/shard_map/all_to_all | solution.py:502
  50.1 0.1 split.2
  50.2 0.8 collective-permute-start.1
  51.0 1.2 collective-permute-done.1.came_ref
  52.3 0.0 copy-done.11
  52.3 0.0 copy-done.4
  52.3 0.0 copy-done
  52.3 0.0 copy-done.2
  52.3 2.0 %forward.1 = f32[16,152,128]{2,1,0:T(8,128)S(1)} custom-call(f32[8,72,128]{2,1,0:T(8,128)S(1)} %get-tuple-element.29.keep_ref, f32[8,72,128]{2,1,0:T(8,128)S(1)} %collective-permute-done.1.came_ref, f32[16,768]{1,0:T(8,128)S(1)} %get-tuple-element.28.refs_4_.rates_ref.refs_5_.rates_s, f32[12,16,768]{2,1,0:T(8,128)S(1)} %copy-done.2, ...), custom_call_target="tpu_custom_call" | custom-call | tf_op jit(solution)/shard_map/forward/pallas_call | solution.py:472
  54.2 24.7 %all_to_all.32.got_ref.sums_ref = f32[16,152,128]{2,1,0:T(8,128)S(1)} all-to-all(f32[16,152,128]{2,1,0:T(8,128)S(1)} %forward.1), channel_id=1, replica_groups=mesh['row'=16,'col'=16] {'row'}, dimensions={0} | all-to-all | bytes 2490368 | tf_op jit(solution)/shard_map/all_to_all | solution.py:502
  78.9 0.2 prefix_row.1
  79.1 0.0 copy-start.1
  79.1 0.0 copy-start.5
  79.1 20.0 %all_to_all.33.col_got_ref = f32[16,144,128]{2,1,0:T(8,128)S(1)} all-to-all(f32[16,144,128]{2,1,0:T(8,128)S(1)} %prefix_row.1), channel_id=1, replica_groups=mesh['row'=16,'col'=16] {'row'}, dimensions={0} | all-to-all | bytes 2359296 | tf_op jit(solution)/shard_map/all_to_all | solution.py:502
  99.1 0.0 copy-done.1
  99.1 0.0 copy-done.5
  99.1 1.7 %backward.1 = (f32[8,72,128]{2,1,0:T(8,128)S(1)}, f32[8,72,128]{2,1,0:T(8,128)S(1)}) custom-call(f32[16,144,128]{2,1,0:T(8,128)S(1)} %all_to_all.33.col_got_ref, f32[16,768]{1,0:T(8,128)S(1)} %get-tuple-element.28.refs_4_.rates_ref.refs_5_.rates_s, f32[12,16,768]{2,1,0:T(8,128)S(1)} %copy-done.2, f32[12,16,768]{2,1,0:T(8,128)S(1)} %copy-done.5, ...), custom_call_target="tpu_custom_call" | custom-call | tf_op jit(solution)/shard_map/backward/pallas_call | solution.py:472
  100.8 3.1 %collective-permute-start.2 = (f32[8,72,128]{2,1,0:T(8,128)S(1)}, f32[8,72,128]{2,1,0:T(8,128)S(1)}, u32[]{:S(2)}, u32[]{:S(2)}) collective-permute-start(f32[8,72,128]{2,1,0:T(8,128)S(1)} %get-tuple-element.38), channel_id=1, source_target_pairs={{0,1},{1,0},{2,3},{3,2},{4,5},{5,4},{6,7},{7,6},{8,9},{9,8},{10,11... | collective-permute-start | bytes 884744 | tf_op jit(solution)/shard_map/ppermute | solution.py:574
  103.9 1.2 collective-permute-done.2.refs_1_.refs_2_
  105.1 0.1 combine.3
  105.2 15.1 %all_to_all.34.got_ref = f32[8,72,128]{2,1,0:T(8,128)S(1)} all-to-all(f32[8,72,128]{2,1,0:T(8,128)S(1)} %combine.3), channel_id=1, replica_groups={{0,2,4,6,8,10,12,14},{1,3,5,7,9,11,13,15},{16,18,20,22,24,26,28,30},{17..., dimensions={0} | all-to-all | bytes 589824 | tf_op jit(solution)/shard_map/all_to_all | solution.py:502
  120.3 0.1 prefix_col.3
  120.4 0.0 copy-start.3
  120.4 0.0 copy-start.12
  120.4 0.0 copy-start.14
  120.5 0.0 copy-start.16
  120.5 13.7 %all_to_all.35.refs_0_ = f32[8,72,128]{2,1,0:T(8,128)S(1)} all-to-all(f32[8,72,128]{2,1,0:T(8,128)S(1)} %prefix_col.3), channel_id=1, replica_groups={{0,2,4,6,8,10,12,14},{1,3,5,7,9,11,13,15},{16,18,20,22,24,26,28,30},{17..., dimensions={0} | all-to-all | bytes 589824 | tf_op jit(solution)/shard_map/all_to_all | solution.py:502
  134.2 0.1 split.3
  134.3 2.5 %collective-permute-start.3 = (f32[8,72,128]{2,1,0:T(8,128)S(1)}, f32[8,72,128]{2,1,0:T(8,128)S(1)}, u32[]{:S(2)}, u32[]{:S(2)}) collective-permute-start(f32[8,72,128]{2,1,0:T(8,128)S(1)} %get-tuple-element.40), channel_id=1, source_target_pairs={{0,1},{1,0},{2,3},{3,2},{4,5},{5,4},{6,7},{7,6},{8,9},{9,8},{10,11... | collective-permute-start | bytes 884744 | tf_op jit(solution)/shard_map/ppermute | solution.py:527
  136.8 1.2 collective-permute-done.3.back_came_ref
  138.0 0.0 copy-done.10
  138.0 0.0 copy-done.3
  138.1 0.0 copy-done.6
  138.1 0.0 copy-done.12
  138.1 0.0 copy-done.14
  138.1 0.0 copy-done.16
  138.1 12.6 %last.1 = (bf16[12,12,768]{2,1,0:T(8,128)(2,1)}, bf16[12,12,768]{2,1,0:T(8,128)(2,1)}) custom-call(f32[8,72,128]{2,1,0:T(8,128)S(1)} %get-tuple-element.29.keep_ref, f32[8,72,128]{2,1,0:T(8,128)S(1)} %collective-permute-done.1.came_ref, f32[16,144,128]{2,1,0:T(8,128)S(1)} %all_to_all.33.col_got_ref, f32[8,72,128]{2,1,0:T(8,128)S(1)} %get-tuple-element.39.back_keep_ref, ...), custom_call_target="tpu_custom_call" | custom-call | tf_op jit(solution)/shard_map/last/pallas_call | solution.py:472
  (12 shorter events, 0.0 us)
Async XLA Ops:
  9.3 5.1 %collective-permute-start = (f32[8,80,128]{2,1,0:T(8,128)}, f32[8,80,128]{2,1,0:T(8,128)S(1)}, u32[]{:S(2)}, u32[]{:S(2)}) collective-permute-start(f32[8,80,128]{2,1,0:T(8,128)} %get-tuple-element.27), channel_id=1, source_target_pairs={{0,1},{1,0},{2,3},{3,2},{4,5},{5,4},{6,7},{7,6},{8,9},{9,8},{10,11... | collective-permute-start | bytes 983048 | tf_op jit(solution)/shard_map/ppermute | solution.py:556
  12.6 1.0 copy-start.13
  13.6 0.8 copy-start.15
  14.5 37.7 %copy-start.11 = (f32[12,16,768]{2,1,0:T(8,128)S(1)}, f32[12,16,768]{2,1,0:T(8,128)}, u32[]{:S(2)}) copy-start(f32[12,16,768]{2,1,0:T(8,128)} %get-tuple-element.34.term_ref) | copy-start | bytes 1769476
  34.7 17.5 %copy-start.4 = (f32[12,16,768]{2,1,0:T(8,128)S(1)}, f32[12,16,768]{2,1,0:T(8,128)}, u32[]{:S(2)}) copy-start(f32[12,16,768]{2,1,0:T(8,128)} %get-tuple-element.32.u_ref) | copy-start | bytes 1769476
  34.8 17.5 %copy-start = (f32[192,16,128]{2,1,0:T(8,128)S(1)}, f32[192,16,128]{2,1,0:T(8,128)}, u32[]{:S(2)}) copy-start(f32[192,16,128]{2,1,0:T(8,128)} %get-tuple-element.33.b_ref) | copy-start | bytes 4718596
  34.8 17.4 %copy-start.2 = (f32[12,16,768]{2,1,0:T(8,128)S(1)}, f32[12,16,768]{2,1,0:T(8,128)}, u32[]{:S(2)}) copy-start(f32[12,16,768]{2,1,0:T(8,128)} %get-tuple-element.31.step_ref) | copy-start | bytes 1769476
  50.2 2.0 %collective-permute-start.1 = (f32[8,72,128]{2,1,0:T(8,128)S(1)}, f32[8,72,128]{2,1,0:T(8,128)S(1)}, u32[]{:S(2)}, u32[]{:S(2)}) collective-permute-start(f32[8,72,128]{2,1,0:T(8,128)S(1)} %get-tuple-element.30), channel_id=1, source_target_pairs={{0,1},{1,0},{2,3},{3,2},{4,5},{5,4},{6,7},{7,6},{8,9},{9,8},{10,11... | collective-permute-start | bytes 884744 | tf_op jit(solution)/shard_map/ppermute | solution.py:527
  79.1 20.0 %copy-start.1 = (f32[192,16,128]{2,1,0:T(8,128)S(1)}, f32[192,16,128]{2,1,0:T(8,128)}, u32[]{:S(2)}) copy-start(f32[192,16,128]{2,1,0:T(8,128)} %get-tuple-element.36.c_ref) | copy-start | bytes 4718596
  79.1 20.0 %copy-start.5 = (f32[12,16,768]{2,1,0:T(8,128)S(1)}, f32[12,16,768]{2,1,0:T(8,128)}, u32[]{:S(2)}) copy-start(f32[12,16,768]{2,1,0:T(8,128)} %get-tuple-element.35.grad_ref) | copy-start | bytes 1769476
  100.8 4.3 %collective-permute-start.2 = (f32[8,72,128]{2,1,0:T(8,128)S(1)}, f32[8,72,128]{2,1,0:T(8,128)S(1)}, u32[]{:S(2)}, u32[]{:S(2)}) collective-permute-start(f32[8,72,128]{2,1,0:T(8,128)S(1)} %get-tuple-element.38), channel_id=1, source_target_pairs={{0,1},{1,0},{2,3},{3,2},{4,5},{5,4},{6,7},{7,6},{8,9},{9,8},{10,11... | collective-permute-start | bytes 884744 | tf_op jit(solution)/shard_map/ppermute | solution.py:574
  105.1 32.9 %copy-start.10 = (f32[192,768]{1,0:T(8,128)S(1)}, f32[192,768]{1,0:T(8,128)}, u32[]{:S(2)}) copy-start(f32[192,768]{1,0:T(8,128)} %get-tuple-element.45.x_ref) | copy-start | bytes 1769476
  105.2 32.9 %copy-start.9 = (f32[192,768]{1,0:T(8,128)S(1)}, f32[192,768]{1,0:T(8,128)}, u32[]{:S(2)}) copy-start(f32[192,768]{1,0:T(8,128)} %get-tuple-element.44.gated_ref) | copy-start | bytes 1769476
  120.3 17.7 %copy-start.7 = (f32[192,768]{1,0:T(8,128)S(1)}, f32[192,768]{1,0:T(8,128)}, u32[]{:S(2)}) copy-start(f32[192,768]{1,0:T(8,128)} %get-tuple-element.42.z_pre_ref) | copy-start | bytes 1769476
  120.3 17.7 %copy-start.8 = (f32[192,768]{1,0:T(8,128)S(1)}, f32[192,768]{1,0:T(8,128)}, u32[]{:S(2)}) copy-start(f32[192,768]{1,0:T(8,128)} %get-tuple-element.43.dt_pre_ref) | copy-start | bytes 1769476
  120.4 17.6 %copy-start.3 = (bf16[768,768]{1,0:T(8,128)(2,1)S(1)}, bf16[768,768]{1,0:T(8,128)(2,1)}, u32[]{:S(2)}) copy-start(bf16[768,768]{1,0:T(8,128)(2,1)} %w_out_hbm.3) | copy-start | bytes 3538948
  120.4 17.6 %copy-start.6 = (f32[192,768]{1,0:T(8,128)S(1)}, f32[192,768]{1,0:T(8,128)}, u32[]{:S(2)}) copy-start(f32[192,768]{1,0:T(8,128)} %get-tuple-element.41.x_pre_ref) | copy-start | bytes 1769476
  120.4 17.6 %copy-start.12 = (bf16[768,80]{0,1:T(8,128)(2,1)S(1)}, bf16[768,80]{0,1:T(8,128)(2,1)}, u32[]{:S(2)}) copy-start(bf16[768,80]{0,1:T(8,128)(2,1)} %param.11) | copy-start | bytes 368644
  120.4 17.6 %copy-start.14 = (bf16[48,768]{1,0:T(8,128)(2,1)S(1)}, bf16[48,768]{1,0:T(8,128)(2,1)}, u32[]{:S(2)}) copy-start(bf16[48,768]{1,0:T(8,128)(2,1)} %w_dt_hbm.3) | copy-start | bytes 221188
  120.5 17.6 %copy-start.16 = (f32[768]{0:T(1024)S(1)}, f32[768]{0:T(1024)}, u32[]{:S(2)}) copy-start(f32[768]{0:T(1024)} %d_skip_ref.1) | copy-start | bytes 9220
  134.3 3.8 %collective-permute-start.3 = (f32[8,72,128]{2,1,0:T(8,128)S(1)}, f32[8,72,128]{2,1,0:T(8,128)S(1)}, u32[]{:S(2)}, u32[]{:S(2)}) collective-permute-start(f32[8,72,128]{2,1,0:T(8,128)S(1)} %get-tuple-element.40), channel_id=1, source_target_pairs={{0,1},{1,0},{2,3},{3,2},{4,5},{5,4},{6,7},{7,6},{8,9},{9,8},{10,11... | collective-permute-start | bytes 884744 | tf_op jit(solution)/shard_map/ppermute | solution.py:527

commit v6 on v5

--- a/solution.py
+++ b/solution.py
@@ -72,12 +72,11 @@
 
 
 def first_kernel(
-    tokens_hbm, w_in_hbm, w_xproj_hbm, w_dt_hbm, a_log_hbm, w_out_hbm, out_grad_hbm, dt_bias_ref,
-    x_pre_hbm, z_pre_hbm, dt_pre_hbm, gated_hbm, step_hbm, u_hbm, x_hbm, grad_hbm, b_hbm, c_hbm,
-    term_hbm, rates_hbm, own_hbm, other_hbm,
-    x_pre_ref, z_pre_ref, dt_pre_ref, gated_ref, step_ref, u_ref, x_ref, grad_ref, b_ref, c_ref,
-    tokens_ref, w_x_ref, w_z_ref, w_xproj_ref, w_dt_ref, a_log_ref, w_out_ref, out_grad_ref,
-    tok_s, og_s, end_s, sum_s, term_ref, rates_ref, own_ref, other_ref, sems, out_sems,
+    tokens_hbm, w_in_hbm, w_xproj_hbm, w_dt_hbm, a_log_hbm, dt_bias_ref,
+    x_pre_hbm, dt_pre_hbm, step_hbm, u_hbm, x_hbm, b_hbm, c_hbm, rates_hbm, own_hbm, other_hbm,
+    x_pre_ref, dt_pre_ref, step_ref, u_ref, x_ref, b_ref, c_ref,
+    tokens_ref, w_x_ref, w_xproj_ref, w_dt_ref, a_log_ref,
+    tok_s, end_s, sum_s, rates_ref, own_ref, other_ref, sems, out_sems,
 ):
     leaving = []
 
@@ -93,22 +92,15 @@
             (w_xproj_hbm, w_xproj_ref),
             (w_dt_hbm, w_dt_ref),
             (a_log_hbm, a_log_ref),
-            (w_in_hbm.at[:, C : 2 * C], w_z_ref),
-            (out_grad_hbm, out_grad_ref),
-            (w_out_hbm, w_out_ref),
         ),
         sems,
-        5,
     )
     tok_s[...] = jnp.zeros_like(tok_s)
-    og_s[...] = jnp.zeros_like(og_s)
     copies[0].wait()
     for i in range(T):
         tok_s[i, 0:T, :] = tokens_ref[i]
     tok = tok_s[...].reshape(CELLS, C)
     copies[1].wait()
-    for copy in copies[5:]:
-        copy.start()
     x_pre = jnp.dot(tok, w_x_ref[...], preferred_element_type=F32)
     x_pre_ref[...] = x_pre
     x_act = (x_pre * jax.nn.sigmoid(x_pre)).astype(BF16)
@@ -138,39 +130,20 @@
     copies[4].wait()
     rates_ref[...] = -jnp.exp(a_log_ref[...]) * LOG2E
     leave(rates_ref, rates_hbm)
-    copies[5].wait()
-    z_pre = jnp.dot(tok, w_z_ref[...], preferred_element_type=F32)
-    z_pre_ref[...] = z_pre
-    leave(z_pre_ref, z_pre_hbm)
-    copies[6].wait()
-    for i in range(T):
-        og_s[i, 0:T, :] = out_grad_ref[i]
-    copies[7].wait()
-    gated = nt(og_s[...].reshape(CELLS, C), w_out_ref[...])
-    gated_ref[...] = gated
-    grad_ref[...] = (gated * (z_pre * jax.nn.sigmoid(z_pre))).reshape(T, PAD, C)
-    leave(gated_ref, gated_hbm)
-    leave(grad_ref, grad_hbm)
-    term_ref[...] = jnp.zeros_like(term_ref)
 
     def one_row(back, carry):
         i = T - 1 - back
         row = [jnp.zeros((N, 128), F32) for _ in LANES]
         for j in range(T):
             b = b_ref[PAD * i + j]
-            c = c_ref[PAD * i + j]
             for k, lanes in enumerate(LANES):
                 decay = jnp.exp2(rates_ref[:, lanes] * step_ref[i, j : j + 1, lanes])
                 row[k] = decay * row[k] + b * u_ref[i, j : j + 1, lanes]
-                term_ref[j, :, lanes] = decay * (
-                    c * grad_ref[i, j : j + 1, lanes] + term_ref[j, :, lanes]
-                )
         for k, lanes in enumerate(LANES):
             end_s[i, :, lanes] = row[k]
         return carry
 
     lax.fori_loop(0, T, one_row, 0)
-    leave(term_ref, term_hbm)
     for i in range(T):
         sum_s[i : i + 1, :] = jnp.sum(step_ref[i, 0:T, :], axis=0, keepdims=True)
     core = lax.axis_index("col") % 2
@@ -180,6 +153,39 @@
         leave(ref, out)
     for copy in leaving:
         copy.wait()
+
+
+def gate_kernel(
+    after_hbm, tokens_ref, out_grad_ref, w_in_ref, w_out_ref, step_ref, c_ref, rates_ref,
+    z_pre_ref, gated_ref, grad_ref, term_ref, rates_out,
+    tok_s, og_s,
+):
+    tok_s[...] = jnp.zeros_like(tok_s)
+    og_s[...] = jnp.zeros_like(og_s)
+    for i in range(T):
+        tok_s[i, 0:T, :] = tokens_ref[i]
+        og_s[i, 0:T, :] = out_grad_ref[i]
+    tok = tok_s[...].reshape(CELLS, C)
+    z_pre = jnp.dot(tok, w_in_ref[:, C : 2 * C], preferred_element_type=F32)
+    z_pre_ref[...] = z_pre
+    gated = nt(og_s[...].reshape(CELLS, C), w_out_ref[...])
+    gated_ref[...] = gated
+    grad_ref[...] = (gated * (z_pre * jax.nn.sigmoid(z_pre))).reshape(T, PAD, C)
+    term_ref[...] = jnp.zeros_like(term_ref)
+    rates_out[...] = rates_ref[...]
+
+    def one_row(back, carry):
+        i = T - 1 - back
+        for j in range(T):
+            c = c_ref[PAD * i + j]
+            for lanes in LANES:
+                decay = jnp.exp2(rates_ref[:, lanes] * step_ref[i, j : j + 1, lanes])
+                term_ref[j, :, lanes] = decay * (
+                    c * grad_ref[i, j : j + 1, lanes] + term_ref[j, :, lanes]
+                )
+        return carry
+
+    lax.fori_loop(0, T, one_row, 0)
 
 
 def chip_decay(core, rates_ref, part, group, t, k):
@@ -502,7 +508,7 @@
     return lax.all_to_all(sent, axis, 0, 0, tiled=True, axis_index_groups=groups)
 
 
-def row_scan(own, got, sums, rates, reverse):
+def row_scan(own, got, sums, rates, reverse, gate=None):
     partner = [(place, place ^ 1) for place in range(16)]
     same_core = [[2 * chip + core for chip in range(8)] for core in range(2)]
     if sums is None:
@@ -518,6 +524,8 @@
         combine, f32(8, own.shape[1], 128), (), "combine", 6, own, got, *sums[:2], rates
     )
     chips = swap(chip, "col", same_core)
+    if gate is not None:
+        rates = gate(chip)
     chip_sums = chips if len(sums) == 2 else sums[2]
     state = swap(
         prefix("col", ((0, reverse),), 72, 72, chips, chip_sums, rates), "col", same_core
@@ -537,27 +545,36 @@
     low_rank, half_width = pltpu.VMEM((48, C), BF16), pltpu.VMEM((CELLS, C), BF16)
     w_xproj = w_xproj.T
     partner = [(place, place ^ 1) for place in range(16)]
-    x_pre, z_pre, dt_pre, gated, step, u, x, grad, b, c, term, rates, own, other = call(
+    x_pre, dt_pre, step, u, x, b, c, rates, own, other = call(
         first_kernel,
+        (flat, flat, grid, grid, flat, spread, spread, f32(N, C), f32(8, 80, 128), f32(8, 80, 128)),
         (
-            flat, flat, flat, flat, grid, grid, flat, grid, spread, spread, f32(T, N, C),
-            f32(N, C), f32(8, 80, 128), f32(8, 80, 128),
-        ),
-        (
-            dense, dense, dense, dense, wide, wide, dense, wide, vmem(CELLS, N, 128),
-            vmem(CELLS, N, 128), cells, square, square, narrow, low_rank, vmem(N, C), square, cells,
-            padded, padded, edge, sums, edge, vmem(N, C), halves, halves,
-            pltpu.SemaphoreType.DMA((8,)), pltpu.SemaphoreType.DMA((14,)),
+            dense, dense, wide, wide, dense, vmem(CELLS, N, 128), vmem(CELLS, N, 128),
+            cells, square, narrow, low_rank, vmem(N, C),
+            padded, edge, sums, vmem(N, C), halves, halves,
+            pltpu.SemaphoreType.DMA((5,)), pltpu.SemaphoreType.DMA((10,)),
         ),
         "first", 54,
-        tokens, w_in, w_xproj, w_dt, a_log, w_out, out_grad, dt_bias,
-        fetched=range(7), sent=range(14),
+        tokens, w_in, w_xproj, w_dt, a_log, dt_bias,
+        fetched=range(5), sent=range(10),
     )
     got = lax.ppermute(other, "col", partner)
     own, rates = call(
         stage_kernel, (f32(8, 80, 128), f32(N, C)), (), "stage", 4, own, rates
     )
-    keep, came, chip_sums = row_scan(own, got, None, rates, False)
+    beside = []
+
+    def gate(chip):
+        out = call(
+            gate_kernel, (flat, flat, grid, f32(T, N, C), f32(N, C)), (padded, padded), "gate", 54,
+            chip, tokens, out_grad, w_in, w_out, step, c, rates,
+            fetched=(0,),
+        )
+        beside.extend(out[:4])
+        return out[4]
+
+    keep, came, chip_sums = row_scan(own, got, None, rates, False, gate)
+    z_pre, gated, grad, term = beside
     col_sent = call(
         forward_kernel, f32(16, 152, 128), (edge, edge, sums), "forward", 6,
         keep, came, rates, step, u, b, term,

time: 151 us -> 152 us (level)
  blocking collectives: 109 us -> 88.8 us
  waiting for transfers between devices: 3.63 us -> 11.2 us
  starting transfers between devices: 9.71 us -> 16.2 us
  Pallas kernels: 25.7 us -> 31 us
  local copies, waits for them, and re-layouts: 1.84 us -> 3.71 us
    all_to_all x6 -> x5, blocking collectives: 109 us -> 88.8 us  [swap(): lax.all_to_all(sent, axis, 0, 0, tiled=True, axis_index_groups=groups)]
    all_to_all x0 -> x1, waiting for transfers between devices: none -> 7.55 us  [swap(): lax.all_to_all(sent, axis, 0, 0, tiled=True, axis_index_groups=groups)]
    all_to_all x0 -> x1, starting transfers between devices: none -> 6.47 us  [swap(): lax.all_to_all(sent, axis, 0, 0, tiled=True, axis_index_groups=groups)]
    pallas_call x12 -> x13, Pallas kernels: 25.7 us -> 31 us  [call(): pl.pallas_call(kernel, out_shape=out_shape, in_specs=[IN_HBM if k in fetc...]
    unnamed x34 -> x42, local copies, waits for them, and re-layouts: 1.84 us -> 3.71 us
  transfers between devices with their start and end apart: 4 -> 5, of which waited for: 3 -> 4; matrix products, arithmetic and copies ran while one was open for 0% -> 0% of each run, Pallas kernels for 0% -> 4%
where the time goes in v6:
time: 152 us
  blocking collectives  88.8 us (58%)
  Pallas kernels  31 us (20%)
  starting transfers between devices  16.2 us (11%)
  waiting for transfers between devices  11.2 us (7%)
  local copies, waits for them, and re-layouts  3.71 us (2%)
    all_to_all x5, blocking collectives, swap(): lax.all_to_all(sent, axis, 0, 0, tiled=True, axis_index_groups=groups)  88.8 us
    pallas_call x13, Pallas kernels, call(): pl.pallas_call(kernel, out_shape=out_shape, in_specs=[IN_HBM if k in fetc...  31 us
    all_to_all x1, waiting for transfers between devices, swap(): lax.all_to_all(sent, axis, 0, 0, tiled=True, axis_index_groups=groups)  7.55 us
    all_to_all x1, starting transfers between devices, swap(): lax.all_to_all(sent, axis, 0, 0, tiled=True, axis_index_groups=groups)  6.47 us
    unnamed x42, local copies, waits for them, and re-layouts  3.71 us
    ppermute x2, starting transfers between devices, row_scan(): return (keep, lax.ppermute(send, 'col', partner), (*sums[:2], chip_sums))  3.36 us
    ppermute x1, starting transfers between devices, body(): got = lax.ppermute(other, 'col', partner)  3.29 us
    ppermute x1, starting transfers between devices, body(): back_got = lax.ppermute(back_other, 'col', partner)  3.06 us
  transfers between devices with their start and end apart: 5, of which 4 were waited for; matrix products, arithmetic and copies ran while one was open for 0% of the time, Pallas kernels for 4%

profile of v6, /device:TPU:1, one launch (start us, length us, event | category | flops | bytes accessed | tf_op | source)
XLA Modules:
  0.0 151.7 jit_solution(14848868076083318030)
XLA Ops:
  0.6 6.8 %first.1 = (f32[192,768]{1,0:T(8,128)}, f32[192,768]{1,0:T(8,128)}, f32[12,16,768]{2,1,0:T(8,128)}, f32[12,16,768]{2,1,0:T(8,128)}, f32[192,768]{1,0:T(8,128)}, ...) custom-call(bf16[12,12,768]{2,1,0:T(8,128)(2,1)} %tokens_ref.1, ...), custom_call_target="tpu_custom_call" | custom-call | tf_op jit(solution)/shard_map/first/pallas_call | solution.py:478
  7.4 3.3 %collective-permute-start = (f32[8,80,128]{2,1,0:T(8,128)}, f32[8,80,128]{2,1,0:T(8,128)S(1)}, u32[]{:S(2)}, u32[]{:S(2)}) collective-permute-start(f32[8,80,128]{2,1,0:T(8,128)} %get-tuple-element.28), channel_id=1, source_target_pairs={{0,1},{1,0},{2,3},{3,2},{4,5},{5,4},{6,7},{7,6},{8,9},{9,8},{10,11... | collective-permute-start | bytes 983048 | tf_op jit(solution)/shard_map/ppermute | solution.py:561
  10.7 1.0 copy-done.15
  11.7 0.8 copy-done.19
  12.5 0.0 copy-start.4
  12.5 0.0 collective-permute-done.refs_1_.refs_3_.refs_2_.refs_4_
  12.5 0.8 combine.2.after_hbm
  13.4 6.5 %all-to-all-start = ((f32[8,80,128]{2,1,0:T(8,128)}), f32[8,80,128]{2,1,0:T(8,128)S(1)}, u32[]{:S(2)}, u32[]{:S(2)}) async-start(f32[8,80,128]{2,1,0:T(8,128)} %combine.2.after_hbm), calls=%async_computation | async-start | bytes 655360 | tf_op jit(solution)/shard_map/all_to_all | solution.py:508
  19.9 0.0 copy-done.4
  19.9 6.2 %gate.1 = (f32[192,768]{1,0:T(8,128)}, f32[192,768]{1,0:T(8,128)}, f32[12,16,768]{2,1,0:T(8,128)}, f32[12,16,768]{2,1,0:T(8,128)}, f32[16,768]{1,0:T(8,128)}) custom-call(f32[8,80,128]{2,1,0:T(8,128)} %combine.2.after_hbm, bf16[12,12,768]{2,1,0:T(8,128)(2,1)} %tokens_ref.1, bf16[12,12,768]{2,1,0:T(8,128)(2,1)} %out_grad_ref.1, bf16[768,1536]{1,0:T(8,128)(2,1)} %w_in_hbm.3, ...), custom_call_target="tpu_custom_call" | custom-call | tf_op jit(solution)/shard_map/gate/pallas_call | solution.py:478
  26.1 7.6 %all-to-all-done.got_ref.sums_ref = f32[8,80,128]{2,1,0:T(8,128)S(1)} async-done(((f32[8,80,128]{2,1,0:T(8,128)}), f32[8,80,128]{2,1,0:T(8,128)S(1)}, u32[]{:S(2)}, u32[]{:S(2)}) %all-to-all-start) | async-done | bytes 327712 | tf_op jit(solution)/shard_map/all_to_all | solution.py:508
  33.6 0.8 copy-done.17
  34.4 0.1 prefix_col.2
  34.5 0.0 copy-start.1
  34.5 0.0 copy-start.2
  34.5 0.0 copy-start.5
  34.6 15.3 %all_to_all.30.refs_0_ = f32[8,72,128]{2,1,0:T(8,128)S(1)} all-to-all(f32[8,72,128]{2,1,0:T(8,128)S(1)} %prefix_col.2), channel_id=1, replica_groups={{0,2,4,6,8,10,12,14},{1,3,5,7,9,11,13,15},{16,18,20,22,24,26,28,30},{17..., dimensions={0} | all-to-all | bytes 589824 | tf_op jit(solution)/shard_map/all_to_all | solution.py:508
  49.9 0.0 copy-done.18
  49.9 0.1 split.2
  50.0 0.8 collective-permute-start.1
  50.8 1.2 collective-permute-done.1.came_ref
  52.0 0.0 copy-done.6
  52.0 0.0 copy-done.5
  52.0 0.0 copy-start.13
  52.0 1.1 copy-done.13
  53.1 2.0 %forward.1 = f32[16,152,128]{2,1,0:T(8,128)S(1)} custom-call(f32[8,72,128]{2,1,0:T(8,128)S(1)} %get-tuple-element.33.keep_ref, f32[8,72,128]{2,1,0:T(8,128)S(1)} %collective-permute-done.1.came_ref, f32[16,768]{1,0:T(8,128)S(1)} %copy-done.5, f32[12,16,768]{2,1,0:T(8,128)S(1)} %copy-done.1, f32[12,16,768]{2,1,0:T(8,128)S(1)} %copy-done.6, ...), custom_call_target="tpu_custom_call" | custom-call | tf_op jit(solution)/shard_map/forward/pallas_call | solution.py:478
  55.1 24.7 %all_to_all.31.got_ref.sums_ref = f32[16,152,128]{2,1,0:T(8,128)S(1)} all-to-all(f32[16,152,128]{2,1,0:T(8,128)S(1)} %forward.1), channel_id=1, replica_groups=mesh['row'=16,'col'=16] {'row'}, dimensions={0} | all-to-all | bytes 2490368 | tf_op jit(solution)/shard_map/all_to_all | solution.py:508
  79.7 0.2 prefix_row.1
  79.9 0.0 copy-start
  79.9 0.0 copy-start.7
  79.9 20.0 %all_to_all.32.col_got_ref = f32[16,144,128]{2,1,0:T(8,128)S(1)} all-to-all(f32[16,144,128]{2,1,0:T(8,128)S(1)} %prefix_row.1), channel_id=1, replica_groups=mesh['row'=16,'col'=16] {'row'}, dimensions={0} | all-to-all | bytes 2359296 | tf_op jit(solution)/shard_map/all_to_all | solution.py:508
  99.9 0.0 copy-done.7
  99.9 1.7 %backward.1 = (f32[8,72,128]{2,1,0:T(8,128)S(1)}, f32[8,72,128]{2,1,0:T(8,128)S(1)}) custom-call(f32[16,144,128]{2,1,0:T(8,128)S(1)} %all_to_all.32.col_got_ref, f32[16,768]{1,0:T(8,128)S(1)} %copy-done.5, f32[12,16,768]{2,1,0:T(8,128)S(1)} %copy-done.1, f32[12,16,768]{2,1,0:T(8,128)S(1)} %copy-done.7, f32[192,16,128]{2,1,0:T(8,128)S(1)} %copy-done), custom_call_target="tpu_custom_call" | custom-call | tf_op jit(solution)/shard_map/backward/pallas_call | solution.py:478
  101.7 3.1 %collective-permute-start.2 = (f32[8,72,128]{2,1,0:T(8,128)S(1)}, f32[8,72,128]{2,1,0:T(8,128)S(1)}, u32[]{:S(2)}, u32[]{:S(2)}) collective-permute-start(f32[8,72,128]{2,1,0:T(8,128)S(1)} %get-tuple-element.40), channel_id=1, source_target_pairs={{0,1},{1,0},{2,3},{3,2},{4,5},{5,4},{6,7},{7,6},{8,9},{9,8},{10,11... | collective-permute-start | bytes 884744 | tf_op jit(solution)/shard_map/ppermute | solution.py:591
  104.7 1.2 collective-permute-done.2.refs_1_.refs_2_
  106.0 0.1 combine.3
  106.0 15.1 %all_to_all.33.got_ref = f32[8,72,128]{2,1,0:T(8,128)S(1)} all-to-all(f32[8,72,128]{2,1,0:T(8,128)S(1)} %combine.3), channel_id=1, replica_groups={{0,2,4,6,8,10,12,14},{1,3,5,7,9,11,13,15},{16,18,20,22,24,26,28,30},{17..., dimensions={0} | all-to-all | bytes 589824 | tf_op jit(solution)/shard_map/all_to_all | solution.py:508
  121.2 0.1 prefix_col.3
  121.3 0.0 copy-start.3
  121.3 0.0 copy-start.14
  121.3 0.0 copy-start.16
  121.3 0.0 copy-start.20
  121.3 13.7 %all_to_all.34.refs_0_ = f32[8,72,128]{2,1,0:T(8,128)S(1)} all-to-all(f32[8,72,128]{2,1,0:T(8,128)S(1)} %prefix_col.3), channel_id=1, replica_groups={{0,2,4,6,8,10,12,14},{1,3,5,7,9,11,13,15},{16,18,20,22,24,26,28,30},{17..., dimensions={0} | all-to-all | bytes 589824 | tf_op jit(solution)/shard_map/all_to_all | solution.py:508
  135.0 0.1 split.3
  135.1 2.5 %collective-permute-start.3 = (f32[8,72,128]{2,1,0:T(8,128)S(1)}, f32[8,72,128]{2,1,0:T(8,128)S(1)}, u32[]{:S(2)}, u32[]{:S(2)}) collective-permute-start(f32[8,72,128]{2,1,0:T(8,128)S(1)} %get-tuple-element.42), channel_id=1, source_target_pairs={{0,1},{1,0},{2,3},{3,2},{4,5},{5,4},{6,7},{7,6},{8,9},{9,8},{10,11... | collective-permute-start | bytes 884744 | tf_op jit(solution)/shard_map/ppermute | solution.py:535
  137.7 1.2 collective-permute-done.3.back_came_ref
  138.9 0.0 copy-done.9
  139.0 12.8 %last.1 = (bf16[12,12,768]{2,1,0:T(8,128)(2,1)}, bf16[12,12,768]{2,1,0:T(8,128)(2,1)}) custom-call(f32[8,72,128]{2,1,0:T(8,128)S(1)} %get-tuple-element.33.keep_ref, f32[8,72,128]{2,1,0:T(8,128)S(1)} %collective-permute-done.1.came_ref, f32[16,144,128]{2,1,0:T(8,128)S(1)} %all_to_all.32.col_got_ref, f32[8,72,128]{2,1,0:T(8,128)S(1)} %get-tuple-element.41.back_keep_ref, ...), custom_call_target="tpu_custom_call" | custom-call | tf_op jit(solution)/shard_map/last/pallas_call | solution.py:478
  (22 shorter events, 0.1 us)
Async XLA Ops:
  7.4 5.1 %collective-permute-start = (f32[8,80,128]{2,1,0:T(8,128)}, f32[8,80,128]{2,1,0:T(8,128)S(1)}, u32[]{:S(2)}, u32[]{:S(2)}) collective-permute-start(f32[8,80,128]{2,1,0:T(8,128)} %get-tuple-element.28), channel_id=1, source_target_pairs={{0,1},{1,0},{2,3},{3,2},{4,5},{5,4},{6,7},{7,6},{8,9},{9,8},{10,11... | collective-permute-start | bytes 983048 | tf_op jit(solution)/shard_map/ppermute | solution.py:561
  10.7 1.0 copy-start.15
  11.7 0.8 copy-start.19
  12.5 7.3 %copy-start.4 = (f32[16,768]{1,0:T(8,128)}, f32[16,768]{1,0:T(8,128)S(1)}, u32[]{:S(2)}) copy-start(f32[16,768]{1,0:T(8,128)S(1)} %get-tuple-element.29.refs_4_.rates_ref.rates_s.refs_5_) | copy-start | bytes 147460
  13.4 20.2 %all-to-all-start = ((f32[8,80,128]{2,1,0:T(8,128)}), f32[8,80,128]{2,1,0:T(8,128)S(1)}, u32[]{:S(2)}, u32[]{:S(2)}) async-start(f32[8,80,128]{2,1,0:T(8,128)} %combine.2.after_hbm), calls=%async_computation | async-start | bytes 655360 | tf_op jit(solution)/shard_map/all_to_all | solution.py:508
  33.6 0.8 copy-start.17
  34.4 15.4 %copy-start.18 = (f32[16,768]{1,0:T(8,128)S(1)}, f32[16,768]{1,0:T(8,128)}, u32[]{:S(2)}) copy-start(f32[16,768]{1,0:T(8,128)} %get-tuple-element.32.rates_ref.refs_5_) | copy-start | bytes 147460
  34.4 17.6 %copy-start.6 = (f32[12,16,768]{2,1,0:T(8,128)S(1)}, f32[12,16,768]{2,1,0:T(8,128)}, u32[]{:S(2)}) copy-start(f32[12,16,768]{2,1,0:T(8,128)} %get-tuple-element.35.u_ref) | copy-start | bytes 1769476
  34.5 17.5 %copy-start.1 = (f32[12,16,768]{2,1,0:T(8,128)S(1)}, f32[12,16,768]{2,1,0:T(8,128)}, u32[]{:S(2)}) copy-start(f32[12,16,768]{2,1,0:T(8,128)} %get-tuple-element.30.step_ref) | copy-start | bytes 1769476
  34.5 17.5 %copy-start.2 = (f32[192,16,128]{2,1,0:T(8,128)S(1)}, f32[192,16,128]{2,1,0:T(8,128)}, u32[]{:S(2)}) copy-start(f32[192,16,128]{2,1,0:T(8,128)} %get-tuple-element.36.b_ref) | copy-start | bytes 4718596
  34.5 17.5 %copy-start.5 = (f32[16,768]{1,0:T(8,128)S(1)}, f32[16,768]{1,0:T(8,128)}, u32[]{:S(2)}) copy-start(f32[16,768]{1,0:T(8,128)} %copy-done.4) | copy-start | bytes 147460
  50.0 2.0 %collective-permute-start.1 = (f32[8,72,128]{2,1,0:T(8,128)S(1)}, f32[8,72,128]{2,1,0:T(8,128)S(1)}, u32[]{:S(2)}, u32[]{:S(2)}) collective-permute-start(f32[8,72,128]{2,1,0:T(8,128)S(1)} %get-tuple-element.34), channel_id=1, source_target_pairs={{0,1},{1,0},{2,3},{3,2},{4,5},{5,4},{6,7},{7,6},{8,9},{9,8},{10,11... | collective-permute-start | bytes 884744 | tf_op jit(solution)/shard_map/ppermute | solution.py:535
  52.0 1.1 copy-start.13
  79.9 20.0 %copy-start = (f32[192,16,128]{2,1,0:T(8,128)S(1)}, f32[192,16,128]{2,1,0:T(8,128)}, u32[]{:S(2)}) copy-start(f32[192,16,128]{2,1,0:T(8,128)} %get-tuple-element.31.c_ref) | copy-start | bytes 4718596
  79.9 20.0 %copy-start.7 = (f32[12,16,768]{2,1,0:T(8,128)S(1)}, f32[12,16,768]{2,1,0:T(8,128)}, u32[]{:S(2)}) copy-start(f32[12,16,768]{2,1,0:T(8,128)} %get-tuple-element.38.grad_ref) | copy-start | bytes 1769476
  101.7 4.3 %collective-permute-start.2 = (f32[8,72,128]{2,1,0:T(8,128)S(1)}, f32[8,72,128]{2,1,0:T(8,128)S(1)}, u32[]{:S(2)}, u32[]{:S(2)}) collective-permute-start(f32[8,72,128]{2,1,0:T(8,128)S(1)} %get-tuple-element.40), channel_id=1, source_target_pairs={{0,1},{1,0},{2,3},{3,2},{4,5},{5,4},{6,7},{7,6},{8,9},{9,8},{10,11... | collective-permute-start | bytes 884744 | tf_op jit(solution)/shard_map/ppermute | solution.py:591
  105.9 32.9 %copy-start.12 = (f32[192,768]{1,0:T(8,128)S(1)}, f32[192,768]{1,0:T(8,128)}, u32[]{:S(2)}) copy-start(f32[192,768]{1,0:T(8,128)} %get-tuple-element.46.gated_ref) | copy-start | bytes 1769476
  106.0 32.9 %copy-start.11 = (f32[192,768]{1,0:T(8,128)S(1)}, f32[192,768]{1,0:T(8,128)}, u32[]{:S(2)}) copy-start(f32[192,768]{1,0:T(8,128)} %get-tuple-element.44.z_pre_ref) | copy-start | bytes 1769476
  121.2 17.7 %copy-start.9 = (f32[192,768]{1,0:T(8,128)S(1)}, f32[192,768]{1,0:T(8,128)}, u32[]{:S(2)}) copy-start(f32[192,768]{1,0:T(8,128)} %get-tuple-element.45.dt_pre_ref) | copy-start | bytes 1769476
  121.2 17.7 %copy-start.10 = (f32[192,768]{1,0:T(8,128)S(1)}, f32[192,768]{1,0:T(8,128)}, u32[]{:S(2)}) copy-start(f32[192,768]{1,0:T(8,128)} %get-tuple-element.47.x_ref) | copy-start | bytes 1769476
  121.3 17.6 %copy-start.3 = (bf16[768,768]{1,0:T(8,128)(2,1)S(1)}, bf16[768,768]{1,0:T(8,128)(2,1)}, u32[]{:S(2)}) copy-start(bf16[768,768]{1,0:T(8,128)(2,1)} %w_out_hbm.1) | copy-start | bytes 3538948
  121.3 17.6 %copy-start.8 = (f32[192,768]{1,0:T(8,128)S(1)}, f32[192,768]{1,0:T(8,128)}, u32[]{:S(2)}) copy-start(f32[192,768]{1,0:T(8,128)} %get-tuple-element.43.x_pre_ref) | copy-start | bytes 1769476
  121.3 17.6 %copy-start.14 = (bf16[768,80]{0,1:T(8,128)(2,1)S(1)}, bf16[768,80]{0,1:T(8,128)(2,1)}, u32[]{:S(2)}) copy-start(bf16[768,80]{0,1:T(8,128)(2,1)} %param.11) | copy-start | bytes 368644
  121.3 17.6 %copy-start.16 = (bf16[48,768]{1,0:T(8,128)(2,1)S(1)}, bf16[48,768]{1,0:T(8,128)(2,1)}, u32[]{:S(2)}) copy-start(bf16[48,768]{1,0:T(8,128)(2,1)} %w_dt_hbm.3) | copy-start | bytes 221188
  121.3 17.6 %copy-start.20 = (f32[768]{0:T(1024)S(1)}, f32[768]{0:T(1024)}, u32[]{:S(2)}) copy-start(f32[768]{0:T(1024)} %d_skip_ref.1) | copy-start | bytes 9220
  135.1 3.8 %collective-permute-start.3 = (f32[8,72,128]{2,1,0:T(8,128)S(1)}, f32[8,72,128]{2,1,0:T(8,128)S(1)}, u32[]{:S(2)}, u32[]{:S(2)}) collective-permute-start(f32[8,72,128]{2,1,0:T(8,128)S(1)} %get-tuple-element.42), channel_id=1, source_target_pairs={{0,1},{1,0},{2,3},{3,2},{4,5},{5,4},{6,7},{7,6},{8,9},{9,8},{10,11... | collective-permute-start | bytes 884744 | tf_op jit(solution)/shard_map/ppermute | solution.py:535
